TPU v7x, 512 devices: a whole 4x4x16 slice. The times are simulated.
512 devices in a mesh: leaf: 64 (over x, z), front: 8 (over y, core).
Axes of the slice: x: 4, y: 4, z: 16, core: 2. Of those that a mesh axis runs over, the one named last changes fastest.
Arguments:
- interior_disp: float32 [64, 98304], P(None, 'leaf'), may hold values from -6 to 6
- separator_disp: float32 [64, 3072], P(None, 'leaf'), may hold values from -6 to 6
- modulus: float32 [64, 524288], P(None, ('leaf', 'front')), may hold values from 0.05 to 0.5
- connectivity: int32 [8, 524288], P(None, ('leaf', 'front')), may hold values from 0 to 543
- stiffness: float32 [24, 24], replicated, may hold values from -1.25 to 1.25
- load: float32 [64, 98304], P(None, ('leaf', 'front')), may hold values from -6 to 6
- leaf_pivot_inv: bfloat16 [98304, 1536], P(('leaf', 'front')), may hold values from -0.15625 to 0.15625
- leaf_coupling: bfloat16 [98304, 96], P(('leaf', 'front')), may hold values from -0.109375 to 0.109375
- pivot_inv: bfloat16 [3072, 6048], P('leaf'), may hold values from -2 to 2
- coupling: bfloat16 [3072, 5952], P('leaf'), may hold values from -2 to 2
Outputs:
- leaf_correction: float32 [64, 98304], P(None, ('leaf', 'front'))
- separator_correction: float32 [64, 18432], P('front', 'leaf')
Inputs may be any that keep to these rules, and one draw needn't show every extreme that they name: `connectivity`: local node numbers below 512 are nodes inside the element's leaf subtree; number 512 + n is node n of the separator between the element's leaf and its sibling.
All inputs are finite; a program needn't handle non-finite values.
Results may differ from a plain program's by a relative error of at most 0.019.
Values may be sent and summed in bfloat16 or wider, within the bound.
No kernel may reach another device: no remote copies, remote signals or barrier semaphores. Data moves between devices by JAX's collectives and lax.ppermute only.
A program may use at most 128 MiB of HBM per device.

v0:
```python
import jax
import jax.numpy as jnp
from jax import lax
from jax.sharding import PartitionSpec as P

ROW_CONTRACT = (((1,), (1,)), ((), ()))


def from_partner(value, axis, apart):
    mask = 2**apart
    pairs = [(source, source ^ mask) for source in range(lax.axis_size(axis))]
    return lax.ppermute(value, axis, pairs)


def group_sum(level_part, height):
    for bit_number in range(height):
        level_part = level_part + from_partner(
            level_part.astype(jnp.bfloat16), "leaf", bit_number
        ).astype(level_part.dtype)
    return level_part


def group_collect(front_low, height, leaf_index):
    for bit_number in range(height):
        partner = from_partner(front_low, "leaf", bit_number)
        upper_half = (leaf_index >> bit_number) % 2 == 1
        front_low = jnp.where(
            upper_half,
            jnp.concatenate([partner, front_low], 1),
            jnp.concatenate([front_low, partner], 1),
        )
    return front_low


def body(
    interior_disp,
    separator_disp,
    modulus,
    connectivity,
    stiffness,
    load,
    leaf_pivot_inv,
    leaf_coupling,
    pivot_inv,
    coupling,
):
    leaves = lax.axis_size("leaf")
    levels = leaves.bit_length() - 1
    leaf_index = lax.axis_index("leaf")
    front_index = lax.axis_index("front")
    samples, inner_size = interior_disp.shape
    row_count = separator_disp.shape[1]
    piece_size = load.shape[1]
    partner = from_partner(separator_disp, "leaf", 0)
    upper_leaf = leaf_index % 2 == 1
    shared = jnp.where(
        upper_leaf,
        jnp.concatenate([partner, separator_disp], 1),
        jnp.concatenate([separator_disp, partner], 1),
    )
    node_table = jnp.concatenate([interior_disp, shared], 1)
    element_count = connectivity.shape[1]
    dof_slots = (
        3 * connectivity[:, None, :] + jnp.arange(3, dtype=jnp.int32)[None, :, None]
    ).reshape(24, element_count)
    corners = jnp.take(node_table, dof_slots, axis=1)
    forces = (
        jnp.einsum("ij,sje->sie", stiffness, corners, precision=lax.Precision.HIGHEST)
        * modulus[:, None, :]
    )
    assembled = jnp.zeros(node_table.shape, jnp.float32).at[:, dof_slots].add(forces)
    placed = lax.dynamic_update_slice_in_dim(
        jnp.zeros((samples, inner_size), jnp.float32), load, front_index * piece_size, 1
    )
    residual = lax.psum((placed - assembled[:, :inner_size]).astype(jnp.bfloat16), "front").astype(
        jnp.float32
    )
    low_residual = residual.astype(jnp.bfloat16)
    own_residual = lax.dynamic_slice_in_dim(residual, front_index * piece_size, piece_size, 1)
    own_low = lax.dynamic_slice_in_dim(low_residual, front_index * piece_size, piece_size, 1)
    pivoted = own_residual + lax.dot_general(
        low_residual, leaf_pivot_inv, ROW_CONTRACT, preferred_element_type=jnp.float32
    )
    level_terms = -assembled[:, inner_size:] - jnp.dot(
        own_low, leaf_coupling, preferred_element_type=jnp.float32
    )
    level_part = lax.psum_scatter(level_terms, "front", scatter_dimension=0, tiled=True)
    pivot_parts = []
    own_piece = level_part
    for height in range(1, levels + 1):
        front_size = row_count << height
        if height > 1:
            band_start = row_count * (2**height - 4)
            level_part = -jnp.dot(
                own_piece.astype(jnp.bfloat16),
                coupling[:, band_start : band_start + front_size],
                preferred_element_type=jnp.float32,
            )
        full_front = group_sum(level_part, height)
        own_piece = lax.dynamic_slice_in_dim(
            full_front, leaf_index % 2**height * row_count, row_count, 1
        )
        band_start = row_count * (2**height - 2)
        pivot_band = pivot_inv[:, band_start : band_start + front_size]
        pivot_parts.append(
            own_piece
            + lax.dot_general(
                full_front.astype(jnp.bfloat16),
                pivot_band,
                ROW_CONTRACT,
                preferred_element_type=jnp.float32,
            )
        )
    corrections = [None] * levels
    current = pivot_parts[levels - 1]
    front_low = current.astype(jnp.bfloat16)
    for height in range(levels, 0, -1):
        corrections[height - 1] = current
        front_low = group_collect(current.astype(jnp.bfloat16), height, leaf_index)
        if height > 1:
            front_size = row_count << height
            band_start = row_count * (2**height - 4)
            coupling_band = coupling[:, band_start : band_start + front_size]
            current = pivot_parts[height - 2] - lax.dot_general(
                front_low, coupling_band, ROW_CONTRACT, preferred_element_type=jnp.float32
            )
    all_samples = lax.all_gather(front_low, "front", axis=0, tiled=True)
    leaf_correction = pivoted - lax.dot_general(
        all_samples, leaf_coupling, ROW_CONTRACT, preferred_element_type=jnp.float32
    )
    return (leaf_correction, jnp.concatenate(corrections, 1))


def solution(mesh):
    in_specs = (
        P(None, "leaf"),
        P(None, "leaf"),
        P(None, ("leaf", "front")),
        P(None, ("leaf", "front")),
        P(),
        P(None, ("leaf", "front")),
        P(("leaf", "front"), None),
        P(("leaf", "front"), None),
        P("leaf", None),
        P("leaf", None),
    )
    out_specs = (P(None, ("leaf", "front")), P("front", "leaf"))
    return jax.shard_map(body, mesh=mesh, in_specs=in_specs, out_specs=out_specs, check_vma=False)
```

profile of v0, /device:TPU:1, one launch (start us, length us, event | category | flops | bytes accessed | tf_op | source)
XLA Modules:
  0.0 733.3 jit_solution(9571399224009585680)
XLA Ops:
  7.2 4.5 collective-permute-start
  16.7 81.9 %gather_fusion = f32[24576,64]{1,0:T(8,128)} fusion(f32[64,1632]{0,1:T(8,128)S(1)} %pad_maximum_fusion, s32[24576]{0:T(1024)S(1)} %broadcast_clamp_fusion), kind=kCustom, calls=%fused_computation | custom fusion | bytes 12681216 | tf_op jit(solution)/shard_map/jit(_take)/gather | solution.py:66
  98.6 10.5 %copy.23 = f32[24,1024,64]{1,0,2:T(8,128)} copy(f32[24,1024,64]{2,1,0:T(8,128)} %bitcast.22) | data formatting | bytes 12582912 | tf_op jit(solution)/shard_map/jit(_take)/gather | solution.py:66
  109.1 10.2 %multiply_bitcast_fusion = f32[24,1024,64]{1,0,2:T(8,128)} fusion(f32[64,1024]{1,0:T(8,128)S(1)} %copy-done.3, f32[24,1024,64]{1,0,2:T(8,128)} %copy.23, pred[24,1024]{1,0:T(8,128)(4,1)S(1)} %compare_and_fusion, f32[24,24]{1,0:T(8,128)S(1)} %copy-done.5), kind=kOutput, calls=%fused_computation.5 | convolution fusion | flops 456130560 | bytes 12871936 | tf_op jit(solution)/shard_map/ij,sje->sie/dot_general | solution.py:68
  119.3 9.6 %copy.27 = f32[24,1024,64]{2,1,0:T(8,128)} copy(f32[24,1024,64]{1,0,2:T(8,128)} %multiply_bitcast_fusion) | data formatting | bytes 12582912 | tf_op jit(solution)/shard_map/mul | solution.py:68
  128.9 131.1 %scatter_custom_fusion = f32[64,1632]{0,1:T(8,128)S(1)} fusion(s32[24576]{0:T(1024)S(1)} %bitcast.25, f32[24576,64]{1,0:T(8,128)} %bitcast.23, f32[]{:T(128)} %constant.140.clone.1), kind=kCustom, calls=%fused_computation.27 | custom fusion | flops 1572864 | bytes 418304 | tf_op jit(solution)/shard_map/scatter-add | solution.py:71
  263.1 76.0 %all-reduce.3.cloned.1.call-done = bf16[64,1536]{1,0:T(8,128)(2,1)} async-done(((bf16[64,1536]{1,0:T(8,128)(2,1)}), bf16[64,1536]{1,0:T(8,128)(2,1)}) %all-reduce.3.cloned.1.call-update) | async-done | bytes 196624 | tf_op jit(solution)/shard_map/psum | solution.py:75
  340.2 23.4 %all-reduce = f32[64,96]{1,0:T(8,128)S(1)} all-reduce(f32[64,96]{1,0:T(8,128)S(1)} %convolution_subtract_fusion.1), channel_id=2, replica_groups=mesh['leaf'=64,'front'=8] {'front'}, use_global_device_ids=true, to_apply=%region_2.3.clone | all-reduce | flops 6144 | bytes 49152
  373.2 3.4 collective-permute-start.3
  383.8 3.4 collective-permute-start.5
  389.1 6.6 collective-permute-start.6
  398.5 2.6 collective-permute-start.7
  402.9 3.5 collective-permute-start.8
  408.3 6.6 collective-permute-start.9
  416.6 11.8 %collective-permute-start.10 = (bf16[8,768]{1,0:T(8,128)(2,1)S(1)}, bf16[8,768]{1,0:T(8,128)(2,1)S(1)}, u32[]{:S(2)}, u32[]{:S(2)}) collective-permute-start(bf16[8,768]{1,0:T(8,128)(2,1)S(1)} %fusion.58), channel_id=1, source_target_pairs={{0,64},{8,72},{16,80},{24,88},{32,96},{40,104},{48,112},{56,120},{... | collective-permute-start | bytes 36872 | tf_op jit(solution)/shard_map/ppermute | solution.py:12
  431.0 2.6 collective-permute-start.11
  435.5 3.5 collective-permute-start.12
  441.3 6.7 collective-permute-start.13
  449.8 12.8 %collective-permute-start.14 = (bf16[8,1536]{1,0:T(8,128)(2,1)S(1)}, bf16[8,1536]{1,0:T(8,128)(2,1)S(1)}, u32[]{:S(2)}, u32[]{:S(2)}) collective-permute-start(bf16[8,1536]{1,0:T(8,128)(2,1)S(1)} %fusion.40), channel_id=1, source_target_pairs={{0,64},{8,72},{16,80},{24,88},{32,96},{40,104},{48,112},{56,120},{... | collective-permute-start | bytes 73736 | tf_op jit(solution)/shard_map/ppermute | solution.py:12
  463.9 3.0 collective-permute-start.15
  472.0 2.6 collective-permute-done.16
  474.5 3.1 collective-permute-start.17
  477.6 3.5 collective-permute-done.17
  481.1 6.2 collective-permute-start.18
  487.3 3.4 collective-permute-done.18
  490.8 12.1 %collective-permute-start.19 = (bf16[8,3072]{1,0:T(8,128)(2,1)S(1)}, bf16[8,3072]{1,0:T(8,128)(2,1)S(1)}, u32[]{:S(2)}, u32[]{:S(2)}) collective-permute-start(bf16[8,3072]{1,0:T(8,128)(2,1)S(1)} %fusion.26), channel_id=1, source_target_pairs={{0,64},{8,72},{16,80},{24,88},{32,96},{40,104},{48,112},{56,120},{... | collective-permute-start | bytes 147464 | tf_op jit(solution)/shard_map/ppermute | solution.py:12
  504.8 3.1 collective-permute-start.20
  509.6 4.9 collective-permute-start.21
  521.6 2.8 collective-permute-start.23
  527.0 7.0 collective-permute-start.24
  535.3 11.9 %collective-permute-start.25 = (bf16[8,384]{1,0:T(8,128)(2,1)S(1)}, bf16[8,384]{1,0:T(8,128)(2,1)S(1)}, u32[]{:S(2)}, u32[]{:S(2)}) collective-permute-start(bf16[8,384]{1,0:T(8,128)(2,1)S(1)} %maximum_select_fusion.10), channel_id=1, source_target_pairs={{0,64},{8,72},{16,80},{24,88},{32,96},{40,104},{48,112},{56,120},{... | collective-permute-start | bytes 18440 | tf_op jit(solution)/shard_map/ppermute | solution.py:12
  548.5 3.5 collective-permute-start.26
  553.1 4.9 collective-permute-start.27
  565.0 3.7 collective-permute-start.29
  570.3 6.9 collective-permute-start.30
  578.9 12.0 %collective-permute-start.31 = (bf16[8,384]{1,0:T(8,128)(2,1)S(1)}, bf16[8,384]{1,0:T(8,128)(2,1)S(1)}, u32[]{:S(2)}, u32[]{:S(2)}) collective-permute-start(bf16[8,384]{1,0:T(8,128)(2,1)S(1)} %maximum_select_fusion.11), channel_id=1, source_target_pairs={{0,64},{8,72},{16,80},{24,88},{32,96},{40,104},{48,112},{56,120},{... | collective-permute-start | bytes 18440 | tf_op jit(solution)/shard_map/ppermute | solution.py:12
  592.0 3.4 collective-permute-start.32
  597.9 2.6 collective-permute-start.33
  602.3 3.6 collective-permute-start.34
  607.6 6.7 collective-permute-start.35
  615.9 11.9 %collective-permute-start.36 = (bf16[8,384]{1,0:T(8,128)(2,1)S(1)}, bf16[8,384]{1,0:T(8,128)(2,1)S(1)}, u32[]{:S(2)}, u32[]{:S(2)}) collective-permute-start(bf16[8,384]{1,0:T(8,128)(2,1)S(1)} %maximum_select_fusion.12), channel_id=1, source_target_pairs={{0,64},{8,72},{16,80},{24,88},{32,96},{40,104},{48,112},{56,120},{... | collective-permute-start | bytes 18440 | tf_op jit(solution)/shard_map/ppermute | solution.py:12
  630.3 2.8 collective-permute-start.37
  634.7 3.8 collective-permute-start.38
  640.0 6.9 collective-permute-start.39
  649.5 2.8 collective-permute-start.40
  653.9 3.9 collective-permute-start.41
  660.1 2.9 collective-permute-start.42
  664.5 61.1 %all_gather.3 = bf16[64,96]{1,0:T(8,128)(2,1)S(1)} all-gather(bf16[8,96]{1,0:T(8,128)(2,1)S(1)} %maximum_select_fusion.26), channel_id=1, replica_groups=mesh['leaf'=64,'front'=8] {'front'}, dimensions={0}, use_global_device_ids=true | all-gather | bytes 13824 | tf_op jit(solution)/shard_map/all_gather | solution.py:127
  (139 shorter events, 99.9 us)
Async XLA Ops:
  7.2 655.8 %copy-start = (bf16[192,1536]{1,0:T(8,128)(2,1)S(1)}, bf16[192,1536]{1,0:T(8,128)(2,1)}, u32[]{:S(2)}) copy-start(bf16[192,1536]{1,0:T(8,128)(2,1)} %param.16) | copy-start | bytes 1769476
  7.2 331.9 %all-reduce.3.cloned.1.call-start = ((), (), s32[]{:S(2)}) async-start(), calls=%async_computation | async-start | bytes 393216 | tf_op jit(solution)/shard_map/psum | solution.py:75
  7.2 8.6 %collective-permute-start = (f32[64,48]{0,1:T(8,128)}, f32[64,48]{0,1:T(8,128)S(1)}, u32[]{:S(2)}, u32[]{:S(2)}) collective-permute-start(f32[64,48]{0,1:T(8,128)} %param.11), channel_id=1, source_target_pairs={{0,8},{8,0},{16,24},{24,16},{32,40},{40,32},{48,56},{56,48},{64,72... | collective-permute-start | bytes 36872 | tf_op jit(solution)/shard_map/ppermute | solution.py:12
  119.3 219.8 %copy-start.4 = (bf16[192,96]{1,0:T(8,128)(2,1)S(1)}, bf16[192,96]{1,0:T(8,128)(2,1)}, u32[]{:S(2)}) copy-start(bf16[192,96]{1,0:T(8,128)(2,1)} %param.17) | copy-start | bytes 110596
  260.4 300.0 %copy-start.1 = (bf16[48,6048]{1,0:T(8,128)(2,1)S(1)}, bf16[48,6048]{1,0:T(8,128)(2,1)}, u32[]{:S(2)}) copy-start(bf16[48,6048]{1,0:T(8,128)(2,1)} %param.18) | copy-start | bytes 1741828
  339.1 323.8 %copy-start.2 = (bf16[64,1536]{1,0:T(8,128)(2,1)S(1)}, bf16[64,1536]{1,0:T(8,128)(2,1)}, u32[]{:S(2)}) copy-start(bf16[64,1536]{1,0:T(8,128)(2,1)} %all-reduce.3.cloned.1.call-done) | copy-start | bytes 589828
  363.6 4.3 collective-permute-start.1
  368.9 4.3 collective-permute-start.2
  373.2 5.2 collective-permute-start.3
  379.5 4.4 collective-permute-start.4
  383.8 5.3 collective-permute-start.5
  389.1 8.3 %collective-permute-start.6 = (bf16[8,384]{1,0:T(8,128)(2,1)S(1)}, bf16[8,384]{1,0:T(8,128)(2,1)S(1)}, u32[]{:S(2)}, u32[]{:S(2)}) collective-permute-start(bf16[8,384]{1,0:T(8,128)(2,1)S(1)} %fusion.77), channel_id=1, source_target_pairs={{0,32},{8,40},{16,48},{24,56},{32,0},{40,8},{48,16},{56,24},{64,96... | collective-permute-start | bytes 18440 | tf_op jit(solution)/shard_map/ppermute | solution.py:12
  398.5 4.4 collective-permute-start.7
  402.9 5.3 collective-permute-start.8
  408.3 8.3 %collective-permute-start.9 = (bf16[8,768]{1,0:T(8,128)(2,1)S(1)}, bf16[8,768]{1,0:T(8,128)(2,1)S(1)}, u32[]{:S(2)}, u32[]{:S(2)}) collective-permute-start(bf16[8,768]{1,0:T(8,128)(2,1)S(1)} %fusion.98), channel_id=1, source_target_pairs={{0,32},{8,40},{16,48},{24,56},{32,0},{40,8},{48,16},{56,24},{64,96... | collective-permute-start | bytes 36872 | tf_op jit(solution)/shard_map/ppermute | solution.py:12
  416.6 13.2 %collective-permute-start.10 = (bf16[8,768]{1,0:T(8,128)(2,1)S(1)}, bf16[8,768]{1,0:T(8,128)(2,1)S(1)}, u32[]{:S(2)}, u32[]{:S(2)}) collective-permute-start(bf16[8,768]{1,0:T(8,128)(2,1)S(1)} %fusion.58), channel_id=1, source_target_pairs={{0,64},{8,72},{16,80},{24,88},{32,96},{40,104},{48,112},{56,120},{... | collective-permute-start | bytes 36872 | tf_op jit(solution)/shard_map/ppermute | solution.py:12
  431.0 4.6 collective-permute-start.11
  435.5 5.8 collective-permute-start.12
  441.3 8.5 %collective-permute-start.13 = (bf16[8,1536]{1,0:T(8,128)(2,1)S(1)}, bf16[8,1536]{1,0:T(8,128)(2,1)S(1)}, u32[]{:S(2)}, u32[]{:S(2)}) collective-permute-start(bf16[8,1536]{1,0:T(8,128)(2,1)S(1)} %get-tuple-element.6), channel_id=1, source_target_pairs={{0,32},{8,40},{16,48},{24,56},{32,0},{40,8},{48,16},{56,24},{64,96... | collective-permute-start | bytes 73736 | tf_op jit(solution)/shard_map/ppermute | solution.py:12
  449.8 14.1 %collective-permute-start.14 = (bf16[8,1536]{1,0:T(8,128)(2,1)S(1)}, bf16[8,1536]{1,0:T(8,128)(2,1)S(1)}, u32[]{:S(2)}, u32[]{:S(2)}) collective-permute-start(bf16[8,1536]{1,0:T(8,128)(2,1)S(1)} %fusion.40), channel_id=1, source_target_pairs={{0,64},{8,72},{16,80},{24,88},{32,96},{40,104},{48,112},{56,120},{... | collective-permute-start | bytes 73736 | tf_op jit(solution)/shard_map/ppermute | solution.py:12
  463.9 4.6 collective-permute-start.15
  469.7 4.8 collective-permute-start.16
  474.5 6.6 collective-permute-start.17
  481.1 9.6 %collective-permute-start.18 = (bf16[8,3072]{1,0:T(8,128)(2,1)S(1)}, bf16[8,3072]{1,0:T(8,128)(2,1)S(1)}, u32[]{:S(2)}, u32[]{:S(2)}) collective-permute-start(bf16[8,3072]{1,0:T(8,128)(2,1)S(1)} %fusion.99), channel_id=1, source_target_pairs={{0,32},{8,40},{16,48},{24,56},{32,0},{40,8},{48,16},{56,24},{64,96... | collective-permute-start | bytes 147464 | tf_op jit(solution)/shard_map/ppermute | solution.py:12
  490.8 13.9 %collective-permute-start.19 = (bf16[8,3072]{1,0:T(8,128)(2,1)S(1)}, bf16[8,3072]{1,0:T(8,128)(2,1)S(1)}, u32[]{:S(2)}, u32[]{:S(2)}) collective-permute-start(bf16[8,3072]{1,0:T(8,128)(2,1)S(1)} %fusion.26), channel_id=1, source_target_pairs={{0,64},{8,72},{16,80},{24,88},{32,96},{40,104},{48,112},{56,120},{... | collective-permute-start | bytes 147464 | tf_op jit(solution)/shard_map/ppermute | solution.py:12
  504.8 4.8 collective-permute-start.20
  509.6 6.3 collective-permute-start.21
  517.2 4.3 collective-permute-start.22
  521.6 5.3 collective-permute-start.23
  527.0 8.2 %collective-permute-start.24 = (bf16[8,192]{1,0:T(8,128)(2,1)S(1)}, bf16[8,192]{1,0:T(8,128)(2,1)S(1)}, u32[]{:S(2)}, u32[]{:S(2)}) collective-permute-start(bf16[8,192]{1,0:T(8,128)(2,1)S(1)} %maximum_select_fusion.15), channel_id=1, source_target_pairs={{0,32},{8,40},{16,48},{24,56},{32,0},{40,8},{48,16},{56,24},{64,96... | collective-permute-start | bytes 9224 | tf_op jit(solution)/shard_map/ppermute | solution.py:12
  535.3 13.1 %collective-permute-start.25 = (bf16[8,384]{1,0:T(8,128)(2,1)S(1)}, bf16[8,384]{1,0:T(8,128)(2,1)S(1)}, u32[]{:S(2)}, u32[]{:S(2)}) collective-permute-start(bf16[8,384]{1,0:T(8,128)(2,1)S(1)} %maximum_select_fusion.10), channel_id=1, source_target_pairs={{0,64},{8,72},{16,80},{24,88},{32,96},{40,104},{48,112},{56,120},{... | collective-permute-start | bytes 18440 | tf_op jit(solution)/shard_map/ppermute | solution.py:12
  548.5 4.6 collective-permute-start.26
  553.1 6.1 collective-permute-start.27
  560.6 4.3 collective-permute-start.28
  565.0 5.2 collective-permute-start.29
  570.3 8.5 %collective-permute-start.30 = (bf16[8,192]{1,0:T(8,128)(2,1)S(1)}, bf16[8,192]{1,0:T(8,128)(2,1)S(1)}, u32[]{:S(2)}, u32[]{:S(2)}) collective-permute-start(bf16[8,192]{1,0:T(8,128)(2,1)S(1)} %maximum_select_fusion.16), channel_id=1, source_target_pairs={{0,32},{8,40},{16,48},{24,56},{32,0},{40,8},{48,16},{56,24},{64,96... | collective-permute-start | bytes 9224 | tf_op jit(solution)/shard_map/ppermute | solution.py:12
  578.9 13.1 %collective-permute-start.31 = (bf16[8,384]{1,0:T(8,128)(2,1)S(1)}, bf16[8,384]{1,0:T(8,128)(2,1)S(1)}, u32[]{:S(2)}, u32[]{:S(2)}) collective-permute-start(bf16[8,384]{1,0:T(8,128)(2,1)S(1)} %maximum_select_fusion.11), channel_id=1, source_target_pairs={{0,64},{8,72},{16,80},{24,88},{32,96},{40,104},{48,112},{56,120},{... | collective-permute-start | bytes 18440 | tf_op jit(solution)/shard_map/ppermute | solution.py:12
  592.0 4.5 collective-permute-start.32
  597.9 4.3 collective-permute-start.33
  602.3 5.2 collective-permute-start.34
  607.6 8.2 %collective-permute-start.35 = (bf16[8,192]{1,0:T(8,128)(2,1)S(1)}, bf16[8,192]{1,0:T(8,128)(2,1)S(1)}, u32[]{:S(2)}, u32[]{:S(2)}) collective-permute-start(bf16[8,192]{1,0:T(8,128)(2,1)S(1)} %maximum_select_fusion.17), channel_id=1, source_target_pairs={{0,32},{8,40},{16,48},{24,56},{32,0},{40,8},{48,16},{56,24},{64,96... | collective-permute-start | bytes 9224 | tf_op jit(solution)/shard_map/ppermute | solution.py:12
  615.9 13.1 %collective-permute-start.36 = (bf16[8,384]{1,0:T(8,128)(2,1)S(1)}, bf16[8,384]{1,0:T(8,128)(2,1)S(1)}, u32[]{:S(2)}, u32[]{:S(2)}) collective-permute-start(bf16[8,384]{1,0:T(8,128)(2,1)S(1)} %maximum_select_fusion.12), channel_id=1, source_target_pairs={{0,64},{8,72},{16,80},{24,88},{32,96},{40,104},{48,112},{56,120},{... | collective-permute-start | bytes 18440 | tf_op jit(solution)/shard_map/ppermute | solution.py:12
  630.3 4.3 collective-permute-start.37
  634.7 5.2 collective-permute-start.38
  640.0 8.2 %collective-permute-start.39 = (bf16[8,192]{1,0:T(8,128)(2,1)S(1)}, bf16[8,192]{1,0:T(8,128)(2,1)S(1)}, u32[]{:S(2)}, u32[]{:S(2)}) collective-permute-start(bf16[8,192]{1,0:T(8,128)(2,1)S(1)} %maximum_select_fusion.18), channel_id=1, source_target_pairs={{0,32},{8,40},{16,48},{24,56},{32,0},{40,8},{48,16},{56,24},{64,96... | collective-permute-start | bytes 9224 | tf_op jit(solution)/shard_map/ppermute | solution.py:12
  649.5 4.3 collective-permute-start.40
  653.9 5.2 collective-permute-start.41
  660.1 4.4 collective-permute-start.42
  (2 other events, 21.1 us)
Sparse Core Ops, SparseCore 0:
  261.2 77.8 all-reduce.2
where the time goes:
time: 736 us; the launch traced here: 733 us
  starting transfers between devices  218 us (30%)
  waiting for transfers between devices  147 us (20%)
  other arithmetic  135 us (18%)
  local copies, waits for them, and re-layouts  107 us (15%)
  blocking collectives  84.5 us (11%)
  matrix products  25.2 us (3%)
  between operations  15.5 us (2%)
    ppermute x43, starting transfers between devices, from_partner(): return lax.ppermute(value, axis, pairs)  218 us
    scatter-add x1, other arithmetic, body(): jnp.zeros(node_table.shape, jnp.float32).at[:, dof_slots].add(forces)  131 us
    gather x2, local copies, waits for them, and re-layouts, body(): corners = jnp.take(node_table, dof_slots, axis=1)  92.4 us
    psum x1, waiting for transfers between devices, body(): lax.psum((placed - assembled[:, :inner_size]).astype(jnp.bfloat16), 'front')  76 us
    ppermute x43, waiting for transfers between devices, from_partner(): return lax.ppermute(value, axis, pairs)  71.3 us
    all_gather x1, blocking collectives, body(): all_samples = lax.all_gather(front_low, 'front', axis=0, tiled=True)  61.1 us
    unnamed x1, blocking collectives  23.4 us
  transfers between devices with their start and end apart: 44, of which 43 were waited for; matrix products, arithmetic and copies ran while one was open for 1% of the time, Pallas kernels for 0%

commit v1 on v0

v1 whole, which is shorter than its diff:
```python
import jax
import jax.numpy as jnp
from jax import lax
from jax.experimental import pallas as pl
from jax.experimental.pallas import tpu as pltpu
from jax.sharding import PartitionSpec as P

BF = jnp.bfloat16
F32 = jnp.float32
ROW_CONTRACT = (((1,), (1,)), ((), ()))
TILE = 256


def rows_dot(left, right):
    return lax.dot_general(left, right, ROW_CONTRACT, preferred_element_type=F32)


def plain_dot(left, right):
    return jnp.dot(left, right, preferred_element_type=F32)


def iota(shape, dim):
    return lax.broadcasted_iota(jnp.int32, shape, dim)


def spread(components, nodes):
    size = components * nodes
    column = iota((size, size), 1)
    comp = sum((column >= nodes * k).astype(jnp.int32) for k in range(1, components))
    return jnp.where(iota((size, size), 0) == components * (column - comp * nodes) + comp, 1.0, 0.0).astype(BF)


def element_kernel(disp_ref, shared_ref, modulus_ref, conn_ref, stiff_ref, pieces_ref, sep_ref,
                   table_ref, onehot_ref, kron_ref, gather_ref, force_ref, acc_ref):
    samples, inner = disp_ref.shape
    shared = shared_ref.shape[1]
    elements = conn_ref.shape[1]
    nodes = inner // 3
    sep_nodes = shared // 3
    all_nodes = nodes + sep_nodes
    blocks = samples // 8
    sort = spread(3, 128)
    for chunk in range(nodes // 128):
        part = plain_dot(disp_ref[:, chunk * 384:(chunk + 1) * 384].astype(BF), sort)
        for block in range(blocks):
            for comp in range(3):
                row = block * 24 + comp * 8
                table_ref[row:row + 8, chunk * 128:(chunk + 1) * 128] = part[
                    block * 8:block * 8 + 8, comp * 128:(comp + 1) * 128]
    column = iota((shared, 384), 1)
    comp_of = (column >= 128).astype(jnp.int32) + (column >= 256).astype(jnp.int32)
    local = column - 128 * comp_of
    sep_sort = jnp.where((iota((shared, 384), 0) == 3 * local + comp_of) & (local < sep_nodes), 1.0, 0.0).astype(BF)
    part = plain_dot(shared_ref[...].astype(BF), sep_sort)
    for block in range(blocks):
        for comp in range(3):
            row = block * 24 + comp * 8
            table_ref[row:row + 8, nodes:nodes + 128] = part[
                block * 8:block * 8 + 8, comp * 128:(comp + 1) * 128]
    table = table_ref[:, :all_nodes].astype(BF)
    up = jnp.where((iota((192, 24), 0) >> 3) == iota((192, 24), 1), 1.0, 0.0).astype(BF)
    wide = rows_dot(plain_dot(up, stiff_ref[...].astype(BF)).astype(BF), up)
    same = (iota((192, 192), 0) & 7) == (iota((192, 192), 1) & 7)
    kron_ref[...] = jnp.where(same, wide, 0.0).astype(BF)
    acc_ref[...] = jnp.zeros_like(acc_ref)

    def tile_step(tile, carry):
        start = pl.multiple_of(tile * TILE, TILE)
        node_row = iota((all_nodes, TILE), 0)
        for corner in range(8):
            which = conn_ref[corner:corner + 1, pl.ds(start, TILE)]
            onehot_ref[:, corner * TILE:(corner + 1) * TILE] = jnp.where(
                node_row == which, 1.0, 0.0).astype(BF)
        for corner in range(8):
            gather_ref[:, corner * TILE:(corner + 1) * TILE] = plain_dot(
                table, onehot_ref[:, corner * TILE:(corner + 1) * TILE])
        for block in range(blocks):
            corners = jnp.concatenate(
                [gather_ref[block * 24:block * 24 + 24, corner * TILE:(corner + 1) * TILE] for corner in range(8)],
                0).astype(BF)
            forces = plain_dot(kron_ref[...], corners)
            scale = modulus_ref[block * 8:block * 8 + 8, pl.ds(start, TILE)]
            forces = forces.reshape(24, 8, TILE) * scale[None]
            forces = forces.reshape(192, TILE)
            for corner in range(8):
                force_ref[block * 24:block * 24 + 24, corner * TILE:(corner + 1) * TILE] = forces[
                    corner * 24:corner * 24 + 24]
        acc_ref[...] += rows_dot(force_ref[...].astype(BF), onehot_ref[...])
        return carry

    lax.fori_loop(0, elements // TILE, tile_step, 0)

    def by_component(first, width):
        rows = []
        for comp in range(3):
            rows.append(jnp.concatenate(
                [acc_ref[block * 24 + comp * 8:block * 24 + comp * 8 + 8, first:first + width]
                 for block in range(blocks)], 0))
        return jnp.concatenate(rows, 1)

    for chunk in range(nodes // 128):
        low = by_component(chunk * 128, 128).astype(BF)
        back = rows_dot(low, sort).astype(BF)
        pieces_ref[2 * chunk] = back[:, :192]
        pieces_ref[2 * chunk + 1] = back[:, 192:]
    rows = []
    for comp in range(3):
        rows.append(jnp.concatenate(
            [acc_ref[block * 24 + comp * 8:block * 24 + comp * 8 + 8, nodes:all_nodes] for block in range(blocks)], 0))
    total = jnp.zeros((samples, shared), F32)
    for comp in range(3):
        place = jnp.where(iota((sep_nodes, shared), 1) == 3 * iota((sep_nodes, shared), 0) + comp, 1.0, 0.0).astype(BF)
        high = rows[comp].astype(BF)
        rest = (rows[comp] - high.astype(F32)).astype(BF)
        total = total + plain_dot(high, place) + plain_dot(rest, place)
    sep_ref[...] = total


def assemble(disp, shared, modulus, connectivity, stiffness, pieces):
    samples, inner = disp.shape
    all_nodes = (inner + shared.shape[1]) // 3
    padded = inner // 3 + 128
    return pl.pallas_call(
        element_kernel,
        out_shape=(
            jax.ShapeDtypeStruct((pieces, samples, inner // pieces), BF),
            jax.ShapeDtypeStruct((samples, shared.shape[1]), F32),
        ),
        scratch_shapes=[
            pltpu.VMEM((3 * samples, padded), F32),
            pltpu.VMEM((all_nodes, 8 * TILE), BF),
            pltpu.VMEM((192, 192), BF),
            pltpu.VMEM((3 * samples, 8 * TILE), F32),
            pltpu.VMEM((3 * samples, 8 * TILE), F32),
            pltpu.VMEM((3 * samples, all_nodes), F32),
        ],
        compiler_params=pltpu.CompilerParams(vmem_limit_bytes=40 << 20),
        name="elements",
    )(disp, shared, modulus, connectivity, stiffness)


def exchange(value, axis, groups=None):
    return lax.all_to_all(value, axis, 0, 0, axis_index_groups=groups, tiled=True)


def group_lists(leaves, height):
    size = 1 << height
    return [[base + i for i in range(size)] for base in range(0, leaves, size)]


def body(
    interior_disp,
    separator_disp,
    modulus,
    connectivity,
    stiffness,
    load,
    leaf_pivot_inv,
    leaf_coupling,
    pivot_inv,
    coupling,
):
    leaves = lax.axis_size("leaf")
    fronts = lax.axis_size("front")
    levels = leaves.bit_length() - 1
    leaf_index = lax.axis_index("leaf")
    samples, inner_size = interior_disp.shape
    rows = separator_disp.shape[1]
    own_samples = samples // fronts
    pairs = [(source, source ^ 1) for source in range(leaves)]
    partner = lax.ppermute(separator_disp, "leaf", pairs)
    upper_leaf = leaf_index % 2 == 1
    shared = jnp.where(
        upper_leaf,
        jnp.concatenate([partner, separator_disp], 1),
        jnp.concatenate([separator_disp, partner], 1),
    )
    pieces, sep_terms = assemble(interior_disp, shared, modulus, connectivity, stiffness, fronts)
    received = exchange(pieces, "front")
    own_residual = load - jnp.sum(received.astype(F32), 0)
    own_low = own_residual.astype(BF)
    terms = -sep_terms - plain_dot(own_low, leaf_coupling)
    parts = exchange(terms.reshape(fronts, own_samples, 2 * rows), "front")
    term = jnp.sum(parts, 0)
    everyone = exchange(jnp.broadcast_to(own_low[None], (fronts,) + own_low.shape), "front")
    low_residual = jnp.transpose(everyone, (1, 0, 2)).reshape(samples, inner_size)
    pivoted = own_residual + rows_dot(low_residual, leaf_pivot_inv)

    level_part = term
    fulls = []
    own_pieces = []
    for height in range(1, levels + 1):
        size = 1 << height
        front_size = rows << height
        if height > 1:
            band = rows * (2**height - 4)
            level_part = -plain_dot(own_pieces[-1].astype(BF), coupling[:, band:band + front_size])
        outgoing = jnp.transpose(level_part.astype(BF).reshape(own_samples, size, rows), (1, 0, 2))
        incoming = exchange(outgoing, "leaf", group_lists(leaves, height))
        own_pieces.append(jnp.sum(incoming.astype(F32), 0))

    def collect(low, height):
        size = 1 << height
        sent = jnp.broadcast_to(low[None], (size,) + low.shape)
        return exchange(sent, "leaf", group_lists(leaves, height))

    low_pieces = jnp.concatenate([piece.astype(BF) for piece in own_pieces], 1)
    gathered = collect(low_pieces, levels)
    pivot_parts = []
    for height in range(1, levels + 1):
        size = 1 << height
        front_size = rows << height
        band = rows * (2**height - 2)
        base = leaf_index // size * size
        mine = lax.dynamic_slice_in_dim(gathered, base, size, 0)[:, :, (height - 1) * rows:height * rows]
        full = jnp.transpose(mine, (1, 0, 2)).reshape(own_samples, front_size)
        pivot_parts.append(own_pieces[height - 1] + rows_dot(full, pivot_inv[:, band:band + front_size]))
    corrections = [None] * levels
    current = pivot_parts[levels - 1]
    for height in range(levels, 0, -1):
        corrections[height - 1] = current
        front_size = rows << height
        incoming = collect(current.astype(BF), height)
        front_low = jnp.transpose(incoming, (1, 0, 2)).reshape(own_samples, front_size)
        if height > 1:
            band = rows * (2**height - 4)
            current = pivot_parts[height - 2] - rows_dot(front_low, coupling[:, band:band + front_size])
    all_samples = exchange(jnp.broadcast_to(front_low[None], (fronts,) + front_low.shape), "front")
    leaf_correction = pivoted - rows_dot(all_samples.reshape(samples, 2 * rows), leaf_coupling)
    return (leaf_correction, jnp.concatenate(corrections, 1))


def solution(mesh):
    in_specs = (
        P(None, "leaf"),
        P(None, "leaf"),
        P(None, ("leaf", "front")),
        P(None, ("leaf", "front")),
        P(),
        P(None, ("leaf", "front")),
        P(("leaf", "front"), None),
        P(("leaf", "front"), None),
        P("leaf", None),
        P("leaf", None),
    )
    out_specs = (P(None, ("leaf", "front")), P("front", "leaf"))
    return jax.shard_map(body, mesh=mesh, in_specs=in_specs, out_specs=out_specs, check_vma=False)
```

time: 736 us -> 277 us (0.38)
  starting transfers between devices: 218 us -> 57.1 us
  other arithmetic: 135 us -> 0.36 us
  local copies, waits for them, and re-layouts: 107 us -> 16.7 us
  waiting for transfers between devices: 147 us -> 80.9 us
  matrix products: 25.2 us -> 4.46 us
  blocking collectives: 84.5 us -> 105 us
  between operations: 15.5 us -> 1.11 us
  Pallas kernels: 0 us -> 10.2 us
    ppermute x43 -> x1, starting transfers between devices: 218 us -> 4.36 us  [body(): partner = lax.ppermute(separator_disp, 'leaf', pairs)]
    scatter-add x1 -> x0, other arithmetic: 131 us -> none  [body(): jnp.zeros(node_table.shape, jnp.float32).at[:, dof_slots].add(forces)]
    all_to_all x0 -> x8, blocking collectives: none -> 105 us  [exchange(): lax.all_to_all(value, axis, 0, 0, axis_index_groups=groups, tiled=True)]
    gather x2 -> x0, local copies, waits for them, and re-layouts: 92.4 us -> none  [body(): corners = jnp.take(node_table, dof_slots, axis=1)]
    all_to_all x0 -> x9, waiting for transfers between devices: none -> 79.6 us  [exchange(): lax.all_to_all(value, axis, 0, 0, axis_index_groups=groups, tiled=True)]
    psum x1 -> x0, waiting for transfers between devices: 76 us -> none  [body(): lax.psum((placed - assembled[:, :inner_size]).astype(jnp.bfloat16), 'front')]
    ppermute x43 -> x1, waiting for transfers between devices: 71.3 us -> 1.25 us  [body(): partner = lax.ppermute(separator_disp, 'leaf', pairs)]
    all_gather x1 -> x0, blocking collectives: 61.1 us -> none  [body(): all_samples = lax.all_gather(front_low, 'front', axis=0, tiled=True)]
  transfers between devices with their start and end apart: 44 -> 10, of which waited for: 43 -> 10; matrix products, arithmetic and copies ran while one was open for 1% -> 1% of each run, Pallas kernels for 0% -> 0%
where the time goes in v1:
time: 277 us; the launch traced here: 276 us
  blocking collectives  105 us (38%)
  waiting for transfers between devices  80.9 us (29%)
  starting transfers between devices  57.1 us (21%)
  local copies, waits for them, and re-layouts  16.7 us (6%)
  Pallas kernels  10.2 us (4%)
  matrix products  4.46 us (2%)
    all_to_all x8, blocking collectives, exchange(): lax.all_to_all(value, axis, 0, 0, axis_index_groups=groups, tiled=True)  105 us
    all_to_all x9, waiting for transfers between devices, exchange(): lax.all_to_all(value, axis, 0, 0, axis_index_groups=groups, tiled=True)  79.6 us
    all_to_all x9, starting transfers between devices, exchange(): lax.all_to_all(value, axis, 0, 0, axis_index_groups=groups, tiled=True)  52.8 us
    unnamed x43, local copies, waits for them, and re-layouts  10.6 us
    pallas_call x1, Pallas kernels, assemble(): pl.pallas_call(element_kernel, out_shape=(jax.ShapeDtypeStruct((pieces, s...  10.2 us
  transfers between devices with their start and end apart: 10, of which 10 were waited for; matrix products, arithmetic and copies ran while one was open for 1% of the time, Pallas kernels for 0%

profile of v1, /device:TPU:1, one launch (start us, length us, event | category | flops | bytes accessed | tf_op | source)
XLA Modules:
  0.0 275.8 jit_solution(9783525989098766382)
XLA Ops:
  0.6 0.9 copy.39
  1.5 4.4 %collective-permute-start = (f32[64,48]{1,0:T(8,128)S(1)}, f32[64,48]{1,0:T(8,128)S(1)}, u32[]{:S(2)}, u32[]{:S(2)}) collective-permute-start(f32[64,48]{1,0:T(8,128)S(1)} %copy.39), channel_id=1, source_target_pairs={{0,8},{8,0},{16,24},{24,16},{32,40},{40,32},{48,56},{56,48},{64,72... | collective-permute-start | bytes 36872 | tf_op jit(solution)/shard_map/ppermute | solution.py:171
  5.9 1.3 collective-permute-done
  7.3 1.0 copy-done.1
  8.3 0.9 copy-done.2
  9.2 10.2 %elements.1 = (bf16[8,64,192]{2,1,0:T(8,128)(2,1)S(1)}, f32[64,96]{1,0:T(8,128)S(1)}) custom-call(f32[64,1536]{1,0:T(8,128)S(1)} %copy-done.1, f32[64,96]{1,0:T(8,128)S(1)} %maximum_select_fusion.shared_ref, f32[64,1024]{1,0:T(8,128)S(1)} %copy-done.2, s32[8,1024]{1,0:T(8,128)S(1)} %copy-done.3, f32[24,24]{1,0:T(8,128)S(1)} %copy-done.4), custom_call_target="tpu_custom_call" | custom-call | tf_op jit(solution)/shard_map/elements/pallas_call | solution.py:123
  19.5 16.0 %all_to_all.85 = bf16[8,64,192]{2,1,0:T(8,128)(2,1)S(1)} all-to-all(bf16[8,64,192]{2,1,0:T(8,128)(2,1)S(1)} %get-tuple-element.4), channel_id=1, replica_groups=mesh['leaf'=64,'front'=8] {'front'}, dimensions={0} | all-to-all | bytes 393216 | tf_op jit(solution)/shard_map/all_to_all | solution.py:143
  35.5 0.8 copy-done.8
  36.3 0.8 copy-done.7
  37.2 8.1 %all_to_all.86 = f32[8,8,96]{2,1,0:T(8,128)S(1)} all-to-all(f32[8,8,96]{2,1,0:T(8,128)S(1)} %fusion.2), channel_id=1, replica_groups=mesh['leaf'=64,'front'=8] {'front'}, dimensions={0} | all-to-all | bytes 49152 | tf_op jit(solution)/shard_map/all_to_all | solution.py:143
  45.5 4.9 %all_to_all.87 = bf16[2,2,192]{2,1,0:T(2,128)(2,1)S(1)} all-to-all(bf16[2,2,192]{2,1,0:T(2,128)(2,1)S(1)} %reshape.92), channel_id=1, replica_groups={{0,8},{16,24},{32,40},{48,56},{64,72},{80,88},{96,104},{112,120},{128,1..., dimensions={0} | all-to-all | bytes 3072 | tf_op jit(solution)/shard_map/all_to_all | solution.py:143
  50.9 6.8 %all_to_all.88 = bf16[4,2,192]{2,1,0:T(2,128)(2,1)S(1)} all-to-all(bf16[4,2,192]{2,1,0:T(2,128)(2,1)S(1)} %reshape.94), channel_id=1, replica_groups={{0,8,16,24},{32,40,48,56},{64,72,80,88},{96,104,112,120},{128,136,144,1..., dimensions={0} | all-to-all | bytes 6144 | tf_op jit(solution)/shard_map/all_to_all | solution.py:143
  58.2 15.9 %all_to_all.89 = bf16[8,2,192]{2,1,0:T(2,128)(2,1)S(1)} all-to-all(bf16[8,2,192]{2,1,0:T(2,128)(2,1)S(1)} %reshape.96), channel_id=1, replica_groups={{0,8,16,24,32,40,48,56},{64,72,80,88,96,104,112,120},{128,136,144,152,1..., dimensions={0} | all-to-all | bytes 12288 | tf_op jit(solution)/shard_map/all_to_all | solution.py:143
  74.6 19.2 %all_to_all.90 = bf16[16,2,192]{2,1,0:T(2,128)(2,1)S(1)} all-to-all(bf16[16,2,192]{2,1,0:T(2,128)(2,1)S(1)} %reshape.98), channel_id=1, replica_groups={{0,8,16,24,32,40,48,56,64,72,80,88,96,104,112,120},{128,136,144,152,160..., dimensions={0} | all-to-all | bytes 24576 | tf_op jit(solution)/shard_map/all_to_all | solution.py:143
  94.5 15.7 %all_to_all.91 = bf16[32,2,192]{2,1,0:T(2,128)(2,1)S(1)} all-to-all(bf16[32,2,192]{2,1,0:T(2,128)(2,1)S(1)} %reshape.100), channel_id=1, replica_groups={{0,8,16,24,32,40,48,56,64,72,80,88,96,104,112,120,128,136,144,152,160,1..., dimensions={0} | all-to-all | bytes 49152 | tf_op jit(solution)/shard_map/all_to_all | solution.py:143
  110.3 0.3 fusion
  111.0 18.3 %all_to_all.92 = bf16[64,2,192]{2,1,0:T(2,128)(2,1)S(1)} all-to-all(bf16[64,2,192]{2,1,0:T(2,128)(2,1)S(1)} %reshape.102), channel_id=1, replica_groups={{0,8,16,24,32,40,48,56,64,72,80,88,96,104,112,120,128,136,144,152,160,1..., dimensions={0} | all-to-all | bytes 98304 | tf_op jit(solution)/shard_map/all_to_all | solution.py:143
  129.6 0.8 broadcast_in_dim.21
  130.4 4.8 %all-to-all-start.9 = ((bf16[64,8,288]{2,1,0:T(8,128)(2,1)}), bf16[64,8,288]{2,1,0:T(8,128)(2,1)S(1)}, u32[]{:S(2)}, u32[]{:S(2)}) async-start(bf16[64,8,288]{2,1,0:T(8,128)(2,1)} %broadcast_in_dim.21), calls=%async_computation.9 | async-start | bytes 786432 | tf_op jit(solution)/shard_map/all_to_all | solution.py:143
  135.2 18.1 %all-to-all-done.9 = bf16[64,8,288]{2,1,0:T(8,128)(2,1)S(1)} async-done(((bf16[64,8,288]{2,1,0:T(8,128)(2,1)}), bf16[64,8,288]{2,1,0:T(8,128)(2,1)S(1)}, u32[]{:S(2)}, u32[]{:S(2)}) %all-to-all-start.9) | async-done | bytes 294944 | tf_op jit(solution)/shard_map/all_to_all | solution.py:143
  155.1 0.8 reshape.104
  155.9 6.6 %all-to-all-start.10 = ((bf16[64,2,192]{2,1,0:T(2,128)(2,1)}), bf16[64,2,192]{2,1,0:T(2,128)(2,1)S(1)}, u32[]{:S(2)}, u32[]{:S(2)}) async-start(bf16[64,2,192]{2,1,0:T(2,128)(2,1)} %reshape.104), calls=%async_computation.10 | async-start | bytes 131072 | tf_op jit(solution)/shard_map/all_to_all | solution.py:143
  162.7 13.3 %all-to-all-done.10 = bf16[64,2,192]{2,1,0:T(2,128)(2,1)S(1)} async-done(((bf16[64,2,192]{2,1,0:T(2,128)(2,1)}), bf16[64,2,192]{2,1,0:T(2,128)(2,1)S(1)}, u32[]{:S(2)}, u32[]{:S(2)}) %all-to-all-start.10) | async-done | bytes 49184 | tf_op jit(solution)/shard_map/all_to_all | solution.py:143
  176.4 0.3 fusion.25
  176.7 0.7 reshape.106
  177.4 3.9 %all-to-all-start.11 = ((bf16[32,2,192]{2,1,0:T(2,128)(2,1)}), bf16[32,2,192]{2,1,0:T(2,128)(2,1)S(1)}, u32[]{:S(2)}, u32[]{:S(2)}) async-start(bf16[32,2,192]{2,1,0:T(2,128)(2,1)} %reshape.106), calls=%async_computation.11 | async-start | bytes 65536 | tf_op jit(solution)/shard_map/all_to_all | solution.py:143
  181.5 12.4 %all-to-all-done.11 = bf16[32,2,192]{2,1,0:T(2,128)(2,1)S(1)} async-done(((bf16[32,2,192]{2,1,0:T(2,128)(2,1)}), bf16[32,2,192]{2,1,0:T(2,128)(2,1)S(1)}, u32[]{:S(2)}, u32[]{:S(2)}) %all-to-all-start.11) | async-done | bytes 24608 | tf_op jit(solution)/shard_map/all_to_all | solution.py:143
  194.3 0.7 reshape.108
  195.0 3.5 %all-to-all-start.12 = ((bf16[16,2,192]{2,1,0:T(2,128)(2,1)}), bf16[16,2,192]{2,1,0:T(2,128)(2,1)S(1)}, u32[]{:S(2)}, u32[]{:S(2)}) async-start(bf16[16,2,192]{2,1,0:T(2,128)(2,1)} %reshape.108), calls=%async_computation.12 | async-start | bytes 32768 | tf_op jit(solution)/shard_map/all_to_all | solution.py:143
  198.7 11.0 %all-to-all-done.12 = bf16[16,2,192]{2,1,0:T(2,128)(2,1)S(1)} async-done(((bf16[16,2,192]{2,1,0:T(2,128)(2,1)}), bf16[16,2,192]{2,1,0:T(2,128)(2,1)S(1)}, u32[]{:S(2)}, u32[]{:S(2)}) %all-to-all-start.12) | async-done | bytes 12320 | tf_op jit(solution)/shard_map/all_to_all | solution.py:143
  210.2 0.7 reshape.110
  210.9 3.3 %all-to-all-start.13 = ((bf16[8,2,192]{2,1,0:T(2,128)(2,1)}), bf16[8,2,192]{2,1,0:T(2,128)(2,1)S(1)}, u32[]{:S(2)}, u32[]{:S(2)}) async-start(bf16[8,2,192]{2,1,0:T(2,128)(2,1)} %reshape.110), calls=%async_computation.13 | async-start | bytes 16384 | tf_op jit(solution)/shard_map/all_to_all | solution.py:143
  214.3 9.1 %all-to-all-done.13 = bf16[8,2,192]{2,1,0:T(2,128)(2,1)S(1)} async-done(((bf16[8,2,192]{2,1,0:T(2,128)(2,1)}), bf16[8,2,192]{2,1,0:T(2,128)(2,1)S(1)}, u32[]{:S(2)}, u32[]{:S(2)}) %all-to-all-start.13) | async-done | bytes 6176 | tf_op jit(solution)/shard_map/all_to_all | solution.py:143
  223.9 0.7 reshape.112
  224.5 3.2 %all-to-all-start.14 = ((bf16[4,2,192]{2,1,0:T(2,128)(2,1)}), bf16[4,2,192]{2,1,0:T(2,128)(2,1)S(1)}, u32[]{:S(2)}, u32[]{:S(2)}) async-start(bf16[4,2,192]{2,1,0:T(2,128)(2,1)} %reshape.112), calls=%async_computation.14 | async-start | bytes 8192 | tf_op jit(solution)/shard_map/all_to_all | solution.py:143
  227.9 4.3 %all-to-all-done.14 = bf16[4,2,192]{2,1,0:T(2,128)(2,1)S(1)} async-done(((bf16[4,2,192]{2,1,0:T(2,128)(2,1)}), bf16[4,2,192]{2,1,0:T(2,128)(2,1)S(1)}, u32[]{:S(2)}, u32[]{:S(2)}) %all-to-all-start.14) | async-done | bytes 3104 | tf_op jit(solution)/shard_map/all_to_all | solution.py:143
  232.2 0.7 broadcast_in_dim.20
  232.9 18.8 %all-to-all-start.1 = ((bf16[8,64,192]{2,1,0:T(8,128)(2,1)}), bf16[8,64,192]{2,1,0:T(8,128)(2,1)S(1)}, u32[]{:S(2)}, u32[]{:S(2)}) async-start(bf16[8,64,192]{2,1,0:T(8,128)(2,1)} %broadcast_in_dim.20), calls=%async_computation.1 | async-start | bytes 524288 | tf_op jit(solution)/shard_map/all_to_all | solution.py:143
  252.1 0.7 reshape.114
  252.7 5.5 %all-to-all-done.1 = bf16[8,64,192]{2,1,0:T(8,128)(2,1)S(1)} async-done(((bf16[8,64,192]{2,1,0:T(8,128)(2,1)}), bf16[8,64,192]{2,1,0:T(8,128)(2,1)S(1)}, u32[]{:S(2)}, u32[]{:S(2)}) %all-to-all-start.1) | async-done | bytes 196640 | tf_op jit(solution)/shard_map/all_to_all | solution.py:143
  258.2 3.2 %all-to-all-start.15 = ((bf16[2,2,192]{2,1,0:T(2,128)(2,1)}), bf16[2,2,192]{2,1,0:T(2,128)(2,1)S(1)}, u32[]{:S(2)}, u32[]{:S(2)}) async-start(bf16[2,2,192]{2,1,0:T(2,128)(2,1)} %reshape.114), calls=%async_computation.15 | async-start | bytes 4096 | tf_op jit(solution)/shard_map/all_to_all | solution.py:143
  261.9 2.2 all-to-all-done.15
  264.3 0.6 broadcast_in_dim.29
  264.9 5.4 %all-to-all-start.16 = ((bf16[8,8,96]{2,1,0:T(8,128)(2,1)}), bf16[8,8,96]{2,1,0:T(8,128)(2,1)S(1)}, u32[]{:S(2)}, u32[]{:S(2)}) async-start(bf16[8,8,96]{2,1,0:T(8,128)(2,1)} %broadcast_in_dim.29), calls=%async_computation.16 | async-start | bytes 32768 | tf_op jit(solution)/shard_map/all_to_all | solution.py:143
  270.3 0.3 convolution_add_fusion
  270.6 0.7 concatenate.15
  271.3 3.7 %all-to-all-done.16 = bf16[8,8,96]{2,1,0:T(8,128)(2,1)S(1)} async-done(((bf16[8,8,96]{2,1,0:T(8,128)(2,1)}), bf16[8,8,96]{2,1,0:T(8,128)(2,1)S(1)}, u32[]{:S(2)}, u32[]{:S(2)}) %all-to-all-start.16) | async-done | bytes 12320 | tf_op jit(solution)/shard_map/all_to_all | solution.py:143
  275.0 0.8 convolution_subtract_fusion
  (114 shorter events, 8.4 us)
Async XLA Ops:
  0.6 269.7 %copy-start = (bf16[192,1536]{1,0:T(8,128)(2,1)S(1)}, bf16[192,1536]{1,0:T(8,128)(2,1)}, u32[]{:S(2)}) copy-start(bf16[192,1536]{1,0:T(8,128)(2,1)} %param.16) | copy-start | bytes 1769476
  1.5 5.7 %collective-permute-start = (f32[64,48]{1,0:T(8,128)S(1)}, f32[64,48]{1,0:T(8,128)S(1)}, u32[]{:S(2)}, u32[]{:S(2)}) collective-permute-start(f32[64,48]{1,0:T(8,128)S(1)} %copy.39), channel_id=1, source_target_pairs={{0,8},{8,0},{16,24},{24,16},{32,40},{40,32},{48,56},{56,48},{64,72... | collective-permute-start | bytes 36872 | tf_op jit(solution)/shard_map/ppermute | solution.py:171
  5.9 1.4 copy-start.3
  5.9 1.4 copy-start.4
  7.3 1.0 copy-start.1
  8.3 0.9 copy-start.2
  19.5 31.1 %copy-start.5 = (bf16[48,5952]{1,0:T(8,128)(2,1)S(1)}, bf16[48,5952]{1,0:T(8,128)(2,1)}, u32[]{:S(2)}) copy-start(bf16[48,5952]{1,0:T(8,128)(2,1)} %param.19) | copy-start | bytes 1714180
  35.5 0.8 copy-start.8
  36.3 0.8 copy-start.7
  130.4 23.6 %copy-start.6 = (bf16[48,6048]{1,0:T(8,128)(2,1)S(1)}, bf16[48,6048]{1,0:T(8,128)(2,1)}, u32[]{:S(2)}) copy-start(bf16[48,6048]{1,0:T(8,128)(2,1)} %param.18) | copy-start | bytes 1741828
  130.4 23.0 %all-to-all-start.9 = ((bf16[64,8,288]{2,1,0:T(8,128)(2,1)}), bf16[64,8,288]{2,1,0:T(8,128)(2,1)S(1)}, u32[]{:S(2)}, u32[]{:S(2)}) async-start(bf16[64,8,288]{2,1,0:T(8,128)(2,1)} %broadcast_in_dim.21), calls=%async_computation.9 | async-start | bytes 786432 | tf_op jit(solution)/shard_map/all_to_all | solution.py:143
  155.9 20.2 %all-to-all-start.10 = ((bf16[64,2,192]{2,1,0:T(2,128)(2,1)}), bf16[64,2,192]{2,1,0:T(2,128)(2,1)S(1)}, u32[]{:S(2)}, u32[]{:S(2)}) async-start(bf16[64,2,192]{2,1,0:T(2,128)(2,1)} %reshape.104), calls=%async_computation.10 | async-start | bytes 131072 | tf_op jit(solution)/shard_map/all_to_all | solution.py:143
  177.4 16.4 %all-to-all-start.11 = ((bf16[32,2,192]{2,1,0:T(2,128)(2,1)}), bf16[32,2,192]{2,1,0:T(2,128)(2,1)S(1)}, u32[]{:S(2)}, u32[]{:S(2)}) async-start(bf16[32,2,192]{2,1,0:T(2,128)(2,1)} %reshape.106), calls=%async_computation.11 | async-start | bytes 65536 | tf_op jit(solution)/shard_map/all_to_all | solution.py:143
  195.0 14.7 %all-to-all-start.12 = ((bf16[16,2,192]{2,1,0:T(2,128)(2,1)}), bf16[16,2,192]{2,1,0:T(2,128)(2,1)S(1)}, u32[]{:S(2)}, u32[]{:S(2)}) async-start(bf16[16,2,192]{2,1,0:T(2,128)(2,1)} %reshape.108), calls=%async_computation.12 | async-start | bytes 32768 | tf_op jit(solution)/shard_map/all_to_all | solution.py:143
  210.9 12.6 %all-to-all-start.13 = ((bf16[8,2,192]{2,1,0:T(2,128)(2,1)}), bf16[8,2,192]{2,1,0:T(2,128)(2,1)S(1)}, u32[]{:S(2)}, u32[]{:S(2)}) async-start(bf16[8,2,192]{2,1,0:T(2,128)(2,1)} %reshape.110), calls=%async_computation.13 | async-start | bytes 16384 | tf_op jit(solution)/shard_map/all_to_all | solution.py:143
  224.5 7.7 %all-to-all-start.14 = ((bf16[4,2,192]{2,1,0:T(2,128)(2,1)}), bf16[4,2,192]{2,1,0:T(2,128)(2,1)S(1)}, u32[]{:S(2)}, u32[]{:S(2)}) async-start(bf16[4,2,192]{2,1,0:T(2,128)(2,1)} %reshape.112), calls=%async_computation.14 | async-start | bytes 8192 | tf_op jit(solution)/shard_map/all_to_all | solution.py:143
  232.9 25.3 %all-to-all-start.1 = ((bf16[8,64,192]{2,1,0:T(8,128)(2,1)}), bf16[8,64,192]{2,1,0:T(8,128)(2,1)S(1)}, u32[]{:S(2)}, u32[]{:S(2)}) async-start(bf16[8,64,192]{2,1,0:T(8,128)(2,1)} %broadcast_in_dim.20), calls=%async_computation.1 | async-start | bytes 524288 | tf_op jit(solution)/shard_map/all_to_all | solution.py:143
  258.2 5.8 %all-to-all-start.15 = ((bf16[2,2,192]{2,1,0:T(2,128)(2,1)}), bf16[2,2,192]{2,1,0:T(2,128)(2,1)S(1)}, u32[]{:S(2)}, u32[]{:S(2)}) async-start(bf16[2,2,192]{2,1,0:T(2,128)(2,1)} %reshape.114), calls=%async_computation.15 | async-start | bytes 4096 | tf_op jit(solution)/shard_map/all_to_all | solution.py:143
  264.9 10.1 %all-to-all-start.16 = ((bf16[8,8,96]{2,1,0:T(8,128)(2,1)}), bf16[8,8,96]{2,1,0:T(8,128)(2,1)S(1)}, u32[]{:S(2)}, u32[]{:S(2)}) async-start(bf16[8,8,96]{2,1,0:T(8,128)(2,1)} %broadcast_in_dim.29), calls=%async_computation.16 | async-start | bytes 32768 | tf_op jit(solution)/shard_map/all_to_all | solution.py:143

commit v2 on v1

--- a/solution.py
+++ b/solution.py
@@ -175,56 +175,113 @@
         jnp.concatenate([partner, separator_disp], 1),
         jnp.concatenate([separator_disp, partner], 1),
     )
+    near = 8
+    near_cols = -(-rows * (2**5 - 4) // 128) * 128
+    near_groups = [[base + i for i in range(near)] for base in range(0, leaves, near)]
+    ring_groups = group_lists(leaves, 4)
+    spot = leaf_index % near
+    near_bands = lax.all_gather(coupling[:, :near_cols], "leaf", axis_index_groups=near_groups)
+    start5 = rows * (2**5 - 4)
+    ring_band = lax.all_gather(
+        lax.optimization_barrier((coupling, near_bands))[0][:, start5:2 * start5 + 4 * rows], "leaf",
+        axis_index_groups=ring_groups,
+    ).reshape(16 * rows, 32 * rows)
+
+    def band(height, width):
+        start = rows * (2**height - 4)
+        return near_bands[:, :, start:start + width].reshape(near * rows, width)
+
+    def own_coupling(height):
+        start = rows * (2**height - 4)
+        return coupling[:, start:start + (rows << height)]
+
+    def own_pivot(height):
+        start = rows * (2**height - 2)
+        return pivot_inv[:, start:start + (rows << height)]
+
+    def joined(stack):
+        return jnp.transpose(stack, (1, 0, 2)).reshape(own_samples, -1)
+
+    def split(flat):
+        return jnp.transpose(flat.reshape(own_samples, -1, rows), (1, 0, 2))
+
+    def collect(low, height):
+        sent = jnp.broadcast_to(low[None], (1 << height,) + low.shape)
+        return exchange(sent, "leaf", group_lists(leaves, height))
+
     pieces, sep_terms = assemble(interior_disp, shared, modulus, connectivity, stiffness, fronts)
     received = exchange(pieces, "front")
     own_residual = load - jnp.sum(received.astype(F32), 0)
     own_low = own_residual.astype(BF)
     terms = -sep_terms - plain_dot(own_low, leaf_coupling)
-    parts = exchange(terms.reshape(fronts, own_samples, 2 * rows), "front")
-    term = jnp.sum(parts, 0)
-    everyone = exchange(jnp.broadcast_to(own_low[None], (fronts,) + own_low.shape), "front")
-    low_residual = jnp.transpose(everyone, (1, 0, 2)).reshape(samples, inner_size)
+    high = lax.reduce_precision(terms, 8, 7)
+    both = jnp.concatenate([high, terms - high], 1).astype(BF).reshape(fronts, own_samples, 4 * rows)
+    packed = jnp.concatenate([jnp.broadcast_to(own_low[None], (fronts,) + own_low.shape), both], 1)
+    everyone = exchange(packed, "front")
+    halves = jnp.sum(everyone[:, samples:].astype(F32), 0)
+    term = halves[:, :2 * rows] + halves[:, 2 * rows:]
+    low_residual = jnp.transpose(everyone[:, :samples], (1, 0, 2)).reshape(samples, inner_size)
     pivoted = own_residual + rows_dot(low_residual, leaf_pivot_inv)
 
-    level_part = term
-    fulls = []
-    own_pieces = []
-    for height in range(1, levels + 1):
+    near_terms = exchange(jnp.broadcast_to(term.astype(BF)[None], (near,) + term.shape), "leaf", near_groups)
+    paired = near_terms.reshape(near // 2, 2, own_samples, 2 * rows).astype(F32).sum(1)
+    q1 = jnp.transpose(paired, (1, 0, 2)).reshape(own_samples, near * rows)
+    half = near * rows // 2
+    band2 = band(2, half)
+    band3 = band(3, 2 * half)
+    band4 = band(4, 4 * half)
+    low1 = q1.astype(BF)
+    q2 = -jnp.concatenate(
+        [plain_dot(low1[:, :half], band2[:half]), plain_dot(low1[:, half:], band2[half:])], 1)
+    low2 = q2.astype(BF)
+    q3 = -plain_dot(low2, band3)
+    low3 = q3.astype(BF)
+    part4 = (-plain_dot(low3, band4)).astype(BF)
+    ring = 16
+    across = []
+    for source in range(leaves):
+        place = source % ring
+        other = place + (12 if place < 4 else -12 if place >= 12 else 4 if place < 8 else -4)
+        across.append((source, source - place + other))
+    q4 = part4.astype(F32) + lax.ppermute(part4, "leaf", across).astype(F32)
+    low4 = q4.astype(BF)
+
+    def piece(flat, index):
+        return lax.dynamic_slice_in_dim(flat, index * rows, rows, 1)
+
+    z_own = []
+    for height, (value, low) in enumerate(((q1, low1), (q2, low2), (q3, low3)), 1):
         size = 1 << height
-        front_size = rows << height
-        if height > 1:
-            band = rows * (2**height - 4)
-            level_part = -plain_dot(own_pieces[-1].astype(BF), coupling[:, band:band + front_size])
-        outgoing = jnp.transpose(level_part.astype(BF).reshape(own_samples, size, rows), (1, 0, 2))
-        incoming = exchange(outgoing, "leaf", group_lists(leaves, height))
-        own_pieces.append(jnp.sum(incoming.astype(F32), 0))
-
-    def collect(low, height):
-        size = 1 << height
-        sent = jnp.broadcast_to(low[None], (size,) + low.shape)
-        return exchange(sent, "leaf", group_lists(leaves, height))
-
-    low_pieces = jnp.concatenate([piece.astype(BF) for piece in own_pieces], 1)
-    gathered = collect(low_pieces, levels)
-    pivot_parts = []
-    for height in range(1, levels + 1):
-        size = 1 << height
-        front_size = rows << height
-        band = rows * (2**height - 2)
-        base = leaf_index // size * size
-        mine = lax.dynamic_slice_in_dim(gathered, base, size, 0)[:, :, (height - 1) * rows:height * rows]
-        full = jnp.transpose(mine, (1, 0, 2)).reshape(own_samples, front_size)
-        pivot_parts.append(own_pieces[height - 1] + rows_dot(full, pivot_inv[:, band:band + front_size]))
-    corrections = [None] * levels
-    current = pivot_parts[levels - 1]
-    for height in range(levels, 0, -1):
-        corrections[height - 1] = current
-        front_size = rows << height
-        incoming = collect(current.astype(BF), height)
-        front_low = jnp.transpose(incoming, (1, 0, 2)).reshape(own_samples, front_size)
-        if height > 1:
-            band = rows * (2**height - 4)
-            current = pivot_parts[height - 2] - rows_dot(front_low, coupling[:, band:band + front_size])
+        front = lax.dynamic_slice_in_dim(low, spot // size * (size * rows), size * rows, 1)
+        z_own.append(piece(value, spot) + rows_dot(front, own_pivot(height)))
+    ring_spot = leaf_index % ring
+    z4 = piece(q4, ring_spot) + rows_dot(low4, own_pivot(4))
+    part5 = -plain_dot(piece(low4, ring_spot), own_coupling(5))
+    q5 = jnp.sum(exchange(split(part5.astype(BF)), "leaf", group_lists(leaves, 5)).astype(F32), 0)
+    low5 = q5.astype(BF)
+    part6 = -plain_dot(low5, own_coupling(6))
+    sent = jnp.concatenate(
+        [split(part6.astype(BF)), jnp.broadcast_to(low5[None], (leaves,) + low5.shape)], 2)
+    back = exchange(sent, "leaf")
+    q6 = jnp.sum(back[:, :, :rows].astype(F32), 0)
+    full5 = joined(lax.dynamic_slice_in_dim(back, leaf_index // 32 * 32, 32, 0)[:, :, rows:])
+    z5 = q5 + rows_dot(full5, own_pivot(5))
+    x6 = q6 + rows_dot(joined(collect(q6.astype(BF), 6)), own_pivot(6))
+    x5 = z5 - rows_dot(joined(collect(x6.astype(BF), 6)), own_coupling(6))
+    last = collect(jnp.concatenate([x5, z4] + z_own, 1).astype(BF), 5)
+    same_ring = lax.dynamic_slice_in_dim(last, leaf_index % 32 // 16 * 16, 16, 0)
+    x4_full = joined(same_ring[:, :, rows:2 * rows]).astype(F32) - rows_dot(joined(last[:, :, :rows]), ring_band)
+    full4 = x4_full.astype(BF)
+    x4 = piece(x4_full, ring_spot)
+    nearby = lax.dynamic_slice_in_dim(last, leaf_index % 32 // near * near, near, 0)[:, :, rows:]
+    z1, z2, z3 = (joined(nearby[:, :, rows * k:rows * (k + 1)]).astype(F32) for k in (1, 2, 3))
+    x3 = z3 - rows_dot(full4, band4)
+    x2 = z2 - rows_dot(x3.astype(BF), band3)
+    low_x2 = x2.astype(BF)
+    x1 = z1 - jnp.concatenate(
+        [rows_dot(low_x2[:, :half], band2[:half]), rows_dot(low_x2[:, half:], band2[half:])], 1)
+    corrections = [piece(x1, spot), piece(x2, spot), piece(x3, spot), x4, x5, x6]
+    front_low = lax.dynamic_slice_in_dim(x1.astype(BF), spot // 2 * (2 * rows), 2 * rows, 1)
     all_samples = exchange(jnp.broadcast_to(front_low[None], (fronts,) + front_low.shape), "front")
     leaf_correction = pivoted - rows_dot(all_samples.reshape(samples, 2 * rows), leaf_coupling)
     return (leaf_correction, jnp.concatenate(corrections, 1))

time: 277 us -> 228 us (0.82)
  blocking collectives: 105 us -> 44.7 us
  between operations: 1.11 us -> 14.6 us
  starting transfers between devices: 57.1 us -> 50.6 us
  matrix products: 4.46 us -> 8.44 us
  waiting for transfers between devices: 80.9 us -> 77.2 us
    all_to_all x8 -> x3, blocking collectives: 105 us -> 44.7 us  [exchange(): lax.all_to_all(value, axis, 0, 0, axis_index_groups=groups, tiled=True)]
    all_to_all x9 -> x6, waiting for transfers between devices: 79.6 us -> 69.2 us  [exchange(): lax.all_to_all(value, axis, 0, 0, axis_index_groups=groups, tiled=True)]
    all_to_all x9 -> x6, starting transfers between devices: 52.8 us -> 43.8 us  [exchange(): lax.all_to_all(value, axis, 0, 0, axis_index_groups=groups, tiled=True)]
    ppermute x0 -> x1, waiting for transfers between devices: none -> 5.85 us  [body(): q4 = part4.astype(F32) + lax.ppermute(part4, 'leaf', across).astype(F32)]
    slice x0 -> x5, local copies, waits for them, and re-layouts: none -> 5.83 us  [the longest x2 2.49 us: band(): return near_bands[:, :, start:start + width].reshape(near * rows, width)]
    dot_general x13 -> x14, matrix products: 3.33 us -> 7.14 us  [rows_dot(): lax.dot_general(left, right, ROW_CONTRACT, preferred_element_type=F32)]
    unnamed x43 -> x23, local copies, waits for them, and re-layouts: 10.6 us -> 6.93 us
  transfers between devices with their start and end apart: 10 -> 10, of which waited for: 10 -> 9; matrix products, arithmetic and copies ran while one was open for 1% -> 7% of each run, Pallas kernels for 0% -> 4%
where the time goes in v2:
time: 228 us; the launch traced here: 227 us
  waiting for transfers between devices  77.2 us (34%)
  starting transfers between devices  50.6 us (22%)
  blocking collectives  44.7 us (20%)
  local copies, waits for them, and re-layouts  18.6 us (8%)
  between operations  14.6 us (6%)
  Pallas kernels  10.2 us (4%)
  matrix products  8.44 us (4%)
  other arithmetic  2.39 us (1%)
    all_to_all x6, waiting for transfers between devices, exchange(): lax.all_to_all(value, axis, 0, 0, axis_index_groups=groups, tiled=True)  69.2 us
    all_to_all x3, blocking collectives, exchange(): lax.all_to_all(value, axis, 0, 0, axis_index_groups=groups, tiled=True)  44.7 us
    all_to_all x6, starting transfers between devices, exchange(): lax.all_to_all(value, axis, 0, 0, axis_index_groups=groups, tiled=True)  43.8 us
    pallas_call x1, Pallas kernels, assemble(): pl.pallas_call(element_kernel, out_shape=(jax.ShapeDtypeStruct((pieces, s...  10.2 us
    dot_general x14, matrix products, rows_dot(): lax.dot_general(left, right, ROW_CONTRACT, preferred_element_type=F32)  7.14 us
    unnamed x23, local copies, waits for them, and re-layouts  6.93 us
    ppermute x1, waiting for transfers between devices, body(): q4 = part4.astype(F32) + lax.ppermute(part4, 'leaf', across).astype(F32)  5.85 us
  transfers between devices with their start and end apart: 10, of which 9 were waited for; matrix products, arithmetic and copies ran while one was open for 7% of the time, Pallas kernels for 4%

profile of v2, /device:TPU:1, one launch (start us, length us, event | category | flops | bytes accessed | tf_op | source)
XLA Modules:
  0.0 226.7 jit_solution(9573396985142907637)
XLA Ops:
  7.2 1.6 slice.108
  8.9 0.8 copy.46
  9.7 4.4 %collective-permute-start = (f32[64,48]{1,0:T(8,128)S(1)}, f32[64,48]{1,0:T(8,128)S(1)}, u32[]{:S(2)}, u32[]{:S(2)}) collective-permute-start(f32[64,48]{1,0:T(8,128)S(1)} %copy.46), channel_id=1, source_target_pairs={{0,8},{8,0},{16,24},{24,16},{32,40},{40,32},{48,56},{56,48},{64,72... | collective-permute-start | bytes 36872 | tf_op jit(solution)/shard_map/ppermute | solution.py:171
  14.1 1.3 collective-permute-done
  15.5 1.0 copy-done.1
  16.5 0.9 copy-done.2
  17.4 0.8 copy-done.3
  18.2 0.7 copy-done.4
  18.9 10.2 %elements.1 = (bf16[8,64,192]{2,1,0:T(8,128)(2,1)S(1)}, f32[64,96]{1,0:T(8,128)S(1)}) custom-call(f32[64,1536]{1,0:T(8,128)S(1)} %copy-done.1, f32[64,96]{1,0:T(8,128)S(1)} %maximum_select_fusion.shared_ref, f32[64,1024]{1,0:T(8,128)S(1)} %copy-done.2, s32[8,1024]{1,0:T(8,128)S(1)} %copy-done.3, f32[24,24]{1,0:T(8,128)S(1)} %copy-done.4), custom_call_target="tpu_custom_call" | custom-call | tf_op jit(solution)/shard_map/elements/pallas_call | solution.py:123
  29.1 16.3 %all_to_all.45 = bf16[8,64,192]{2,1,0:T(8,128)(2,1)S(1)} all-to-all(bf16[8,64,192]{2,1,0:T(8,128)(2,1)S(1)} %get-tuple-element.5), channel_id=1, replica_groups=mesh['leaf'=64,'front'=8] {'front'}, dimensions={0} | all-to-all | bytes 393216 | tf_op jit(solution)/shard_map/all_to_all | solution.py:143
  45.4 0.9 fusion.38
  46.6 10.5 %all_to_all.46 = bf16[8,72,192]{2,1,0:T(8,128)(2,1)S(1)} all-to-all(bf16[8,72,192]{2,1,0:T(8,128)(2,1)S(1)} %maximum_maximum_fusion), channel_id=1, replica_groups=mesh['leaf'=64,'front'=8] {'front'}, dimensions={0} | all-to-all | bytes 442368 | tf_op jit(solution)/shard_map/all_to_all | solution.py:143
  57.2 17.9 %all_to_all.47 = bf16[8,8,96]{2,1,0:T(8,128)(2,1)S(1)} all-to-all(bf16[8,8,96]{2,1,0:T(8,128)(2,1)S(1)} %broadcast_in_dim.15), channel_id=1, replica_groups={{0,8,16,24,32,40,48,56},{64,72,80,88,96,104,112,120},{128,136,144,152,1..., dimensions={0} | all-to-all | bytes 24576 | tf_op jit(solution)/shard_map/all_to_all | solution.py:143
  75.3 0.9 all-gather.5.cloned.1.call-done
  76.1 1.3 slice.143
  77.5 1.0 fusion.39
  78.4 1.2 slice.142
  79.6 0.8 slice.131
  81.1 2.4 %collective-permute-start.1 = (bf16[8,768]{1,0:T(8,128)(2,1)S(1)}, bf16[8,768]{1,0:T(8,128)(2,1)S(1)}, u32[]{:S(2)}, u32[]{:S(2)}) collective-permute-start(bf16[8,768]{1,0:T(8,128)(2,1)S(1)} %fusion.2), channel_id=1, source_target_pairs={{0,96},{8,104},{16,112},{24,120},{32,64},{40,72},{48,80},{56,88},{... | collective-permute-start | bytes 36872 | tf_op jit(solution)/shard_map/ppermute | solution.py:246
  83.7 5.8 %collective-permute-done.1 = bf16[8,768]{1,0:T(8,128)(2,1)S(1)} collective-permute-done((bf16[8,768]{1,0:T(8,128)(2,1)S(1)}, bf16[8,768]{1,0:T(8,128)(2,1)S(1)}, u32[]{:S(2)}, u32[]{:S(2)}) %collective-permute-start.1) | collective-permute-done | bytes 12320 | tf_op jit(solution)/shard_map/ppermute | solution.py:246
  89.5 0.6 convert_add_fusion
  90.5 0.7 reshape.129
  91.3 7.8 %all-to-all-start.3 = ((bf16[32,2,192]{2,1,0:T(2,128)(2,1)}), bf16[32,2,192]{2,1,0:T(2,128)(2,1)S(1)}, u32[]{:S(2)}, u32[]{:S(2)}) async-start(bf16[32,2,192]{2,1,0:T(2,128)(2,1)} %reshape.129), calls=%async_computation.3 | async-start | bytes 65536 | tf_op jit(solution)/shard_map/all_to_all | solution.py:143
  99.1 0.8 fusion.3
  99.9 12.0 %all-to-all-done.3 = bf16[32,2,192]{2,1,0:T(2,128)(2,1)S(1)} async-done(((bf16[32,2,192]{2,1,0:T(2,128)(2,1)}), bf16[32,2,192]{2,1,0:T(2,128)(2,1)S(1)}, u32[]{:S(2)}, u32[]{:S(2)}) %all-to-all-start.3) | async-done | bytes 24608 | tf_op jit(solution)/shard_map/all_to_all | solution.py:143
  112.6 0.7 copy.52
  113.3 4.7 %all-to-all-start.4 = ((bf16[64,8,96]{2,1,0:T(8,128)(2,1)}), bf16[64,8,96]{2,1,0:T(8,128)(2,1)S(1)}, u32[]{:S(2)}, u32[]{:S(2)}) async-start(bf16[64,8,96]{2,1,0:T(8,128)(2,1)} %copy.52), calls=%async_computation.4 | async-start | bytes 262144 | tf_op jit(solution)/shard_map/all_to_all | solution.py:143
  118.5 14.0 %all-to-all-done.4 = bf16[64,8,96]{2,1,0:T(8,128)(2,1)S(1)} async-done(((bf16[64,8,96]{2,1,0:T(8,128)(2,1)}), bf16[64,8,96]{2,1,0:T(8,128)(2,1)S(1)}, u32[]{:S(2)}, u32[]{:S(2)}) %all-to-all-start.4) | async-done | bytes 98336 | tf_op jit(solution)/shard_map/all_to_all | solution.py:143
  132.6 0.8 reshape.131
  133.4 6.2 %all-to-all-start.5 = ((bf16[64,2,192]{2,1,0:T(2,128)(2,1)}), bf16[64,2,192]{2,1,0:T(2,128)(2,1)S(1)}, u32[]{:S(2)}, u32[]{:S(2)}) async-start(bf16[64,2,192]{2,1,0:T(2,128)(2,1)} %reshape.131), calls=%async_computation.5 | async-start | bytes 131072 | tf_op jit(solution)/shard_map/all_to_all | solution.py:143
  139.6 0.9 fusion.23
  140.8 12.3 %all-to-all-done.5 = bf16[64,2,192]{2,1,0:T(2,128)(2,1)S(1)} async-done(((bf16[64,2,192]{2,1,0:T(2,128)(2,1)}), bf16[64,2,192]{2,1,0:T(2,128)(2,1)S(1)}, u32[]{:S(2)}, u32[]{:S(2)}) %all-to-all-start.5) | async-done | bytes 49184 | tf_op jit(solution)/shard_map/all_to_all | solution.py:143
  153.8 0.8 reshape.133
  154.6 4.9 %all-to-all-start.6 = ((bf16[64,2,192]{2,1,0:T(2,128)(2,1)}), bf16[64,2,192]{2,1,0:T(2,128)(2,1)S(1)}, u32[]{:S(2)}, u32[]{:S(2)}) async-start(bf16[64,2,192]{2,1,0:T(2,128)(2,1)} %reshape.133), calls=%async_computation.6 | async-start | bytes 131072 | tf_op jit(solution)/shard_map/all_to_all | solution.py:143
  159.7 13.3 %all-to-all-done.6 = bf16[64,2,192]{2,1,0:T(2,128)(2,1)S(1)} async-done(((bf16[64,2,192]{2,1,0:T(2,128)(2,1)}), bf16[64,2,192]{2,1,0:T(2,128)(2,1)S(1)}, u32[]{:S(2)}, u32[]{:S(2)}) %all-to-all-start.6) | async-done | bytes 49184 | tf_op jit(solution)/shard_map/all_to_all | solution.py:143
  173.4 0.3 fusion.41
  173.6 0.8 concatenate.46
  174.4 0.7 broadcast_in_dim.19
  175.1 3.8 %all-to-all-start.7 = ((bf16[32,8,240]{2,1,0:T(8,128)(2,1)}), bf16[32,8,240]{2,1,0:T(8,128)(2,1)S(1)}, u32[]{:S(2)}, u32[]{:S(2)}) async-start(bf16[32,8,240]{2,1,0:T(8,128)(2,1)} %broadcast_in_dim.19), calls=%async_computation.7 | async-start | bytes 262144 | tf_op jit(solution)/shard_map/all_to_all | solution.py:143
  179.3 0.3 convolution_add_fusion
  179.6 13.7 %all-to-all-done.7 = bf16[32,8,240]{2,1,0:T(8,128)(2,1)S(1)} async-done(((bf16[32,8,240]{2,1,0:T(8,128)(2,1)}), bf16[32,8,240]{2,1,0:T(8,128)(2,1)S(1)}, u32[]{:S(2)}, u32[]{:S(2)}) %all-to-all-start.7) | async-done | bytes 122912 | tf_op jit(solution)/shard_map/all_to_all | solution.py:143
  194.1 2.4 %convolution_subtract_fusion.2 = f32[8,768]{1,0:T(8,128)S(1)} fusion(f32[8,768]{1,0:T(8,128)S(1)} %reshape.125, bf16[8,1536]{1,0:T(8,128)(2,1)S(1)} %reshape.118, bf16[768,1536]{1,0:T(8,128)(2,1)} %all-gather.7.cloned.1.call-done), kind=kOutput, calls=%fused_computation.8 | convolution fusion | flops 18880512 | bytes 2433024 | tf_op jit(solution)/shard_map/dot_general | solution.py:15
  196.4 0.3 convolution_subtract_fusion.4
  197.5 0.6 broadcast_in_dim.20
  198.1 16.3 %all-to-all-start.8 = ((bf16[8,8,96]{2,1,0:T(8,128)(2,1)}), bf16[8,8,96]{2,1,0:T(8,128)(2,1)S(1)}, u32[]{:S(2)}, u32[]{:S(2)}) async-start(bf16[8,8,96]{2,1,0:T(8,128)(2,1)} %broadcast_in_dim.20), calls=%async_computation.8 | async-start | bytes 32768 | tf_op jit(solution)/shard_map/all_to_all | solution.py:143
  214.5 0.7 concatenate.48
  215.2 3.9 %all-to-all-done.8 = bf16[8,8,96]{2,1,0:T(8,128)(2,1)S(1)} async-done(((bf16[8,8,96]{2,1,0:T(8,128)(2,1)}), bf16[8,8,96]{2,1,0:T(8,128)(2,1)S(1)}, u32[]{:S(2)}, u32[]{:S(2)}) %all-to-all-start.8) | async-done | bytes 12320 | tf_op jit(solution)/shard_map/all_to_all | solution.py:143
  219.1 0.8 convolution_subtract_fusion
  (84 shorter events, 6.4 us)
Async XLA Ops:
  7.2 172.2 %copy-start = (bf16[192,1536]{1,0:T(8,128)(2,1)S(1)}, bf16[192,1536]{1,0:T(8,128)(2,1)}, u32[]{:S(2)}) copy-start(bf16[192,1536]{1,0:T(8,128)(2,1)} %param.16) | copy-start | bytes 1769476
  7.2 39.2 %copy-start.7 = (bf16[192,96]{1,0:T(8,128)(2,1)S(1)}, bf16[192,96]{1,0:T(8,128)(2,1)}, u32[]{:S(2)}) copy-start(bf16[192,96]{1,0:T(8,128)(2,1)} %param.17) | copy-start | bytes 110596
  7.2 68.9 %all-gather.5.cloned.1.call-start = ((), (), s32[]{:S(2)}) async-start(), calls=%async_computation.9 | async-start | bytes 1216512 | tf_op jit(solution)/shard_map/all_gather | solution.py:183
  8.9 185.2 %all-gather.7.cloned.1.call-start = ((), (), s32[]{:S(2)}) async-start(), calls=%async_computation.10 | async-start | bytes 2506752 | tf_op jit(solution)/shard_map/all_gather | solution.py:185
  9.7 5.7 %collective-permute-start = (f32[64,48]{1,0:T(8,128)S(1)}, f32[64,48]{1,0:T(8,128)S(1)}, u32[]{:S(2)}, u32[]{:S(2)}) collective-permute-start(f32[64,48]{1,0:T(8,128)S(1)} %copy.46), channel_id=1, source_target_pairs={{0,8},{8,0},{16,24},{24,16},{32,40},{40,32},{48,56},{56,48},{64,72... | collective-permute-start | bytes 36872 | tf_op jit(solution)/shard_map/ppermute | solution.py:171
  15.5 1.0 copy-start.1
  16.5 0.9 copy-start.2
  17.4 0.8 copy-start.3
  18.2 0.7 copy-start.4
  45.4 34.2 %copy-start.5 = (bf16[48,5952]{1,0:T(8,128)(2,1)S(1)}, bf16[48,5952]{1,0:T(8,128)(2,1)}, u32[]{:S(2)}) copy-start(bf16[48,5952]{1,0:T(8,128)(2,1)} %param.19) | copy-start | bytes 1714180
  75.2 23.9 %copy-start.6 = (bf16[48,6048]{1,0:T(8,128)(2,1)S(1)}, bf16[48,6048]{1,0:T(8,128)(2,1)}, u32[]{:S(2)}) copy-start(bf16[48,6048]{1,0:T(8,128)(2,1)} %param.18) | copy-start | bytes 1741828
  81.1 8.4 %collective-permute-start.1 = (bf16[8,768]{1,0:T(8,128)(2,1)S(1)}, bf16[8,768]{1,0:T(8,128)(2,1)S(1)}, u32[]{:S(2)}, u32[]{:S(2)}) collective-permute-start(bf16[8,768]{1,0:T(8,128)(2,1)S(1)} %fusion.2), channel_id=1, source_target_pairs={{0,96},{8,104},{16,112},{24,120},{32,64},{40,72},{48,80},{56,88},{... | collective-permute-start | bytes 36872 | tf_op jit(solution)/shard_map/ppermute | solution.py:246
  91.3 20.6 %all-to-all-start.3 = ((bf16[32,2,192]{2,1,0:T(2,128)(2,1)}), bf16[32,2,192]{2,1,0:T(2,128)(2,1)S(1)}, u32[]{:S(2)}, u32[]{:S(2)}) async-start(bf16[32,2,192]{2,1,0:T(2,128)(2,1)} %reshape.129), calls=%async_computation.3 | async-start | bytes 65536 | tf_op jit(solution)/shard_map/all_to_all | solution.py:143
  113.3 19.1 %all-to-all-start.4 = ((bf16[64,8,96]{2,1,0:T(8,128)(2,1)}), bf16[64,8,96]{2,1,0:T(8,128)(2,1)S(1)}, u32[]{:S(2)}, u32[]{:S(2)}) async-start(bf16[64,8,96]{2,1,0:T(8,128)(2,1)} %copy.52), calls=%async_computation.4 | async-start | bytes 262144 | tf_op jit(solution)/shard_map/all_to_all | solution.py:143
  133.4 19.8 %all-to-all-start.5 = ((bf16[64,2,192]{2,1,0:T(2,128)(2,1)}), bf16[64,2,192]{2,1,0:T(2,128)(2,1)S(1)}, u32[]{:S(2)}, u32[]{:S(2)}) async-start(bf16[64,2,192]{2,1,0:T(2,128)(2,1)} %reshape.131), calls=%async_computation.5 | async-start | bytes 131072 | tf_op jit(solution)/shard_map/all_to_all | solution.py:143
  154.6 18.4 %all-to-all-start.6 = ((bf16[64,2,192]{2,1,0:T(2,128)(2,1)}), bf16[64,2,192]{2,1,0:T(2,128)(2,1)S(1)}, u32[]{:S(2)}, u32[]{:S(2)}) async-start(bf16[64,2,192]{2,1,0:T(2,128)(2,1)} %reshape.133), calls=%async_computation.6 | async-start | bytes 131072 | tf_op jit(solution)/shard_map/all_to_all | solution.py:143
  175.1 18.3 %all-to-all-start.7 = ((bf16[32,8,240]{2,1,0:T(8,128)(2,1)}), bf16[32,8,240]{2,1,0:T(8,128)(2,1)S(1)}, u32[]{:S(2)}, u32[]{:S(2)}) async-start(bf16[32,8,240]{2,1,0:T(8,128)(2,1)} %broadcast_in_dim.19), calls=%async_computation.7 | async-start | bytes 262144 | tf_op jit(solution)/shard_map/all_to_all | solution.py:143
  198.1 20.9 %all-to-all-start.8 = ((bf16[8,8,96]{2,1,0:T(8,128)(2,1)}), bf16[8,8,96]{2,1,0:T(8,128)(2,1)S(1)}, u32[]{:S(2)}, u32[]{:S(2)}) async-start(bf16[8,8,96]{2,1,0:T(8,128)(2,1)} %broadcast_in_dim.20), calls=%async_computation.8 | async-start | bytes 32768 | tf_op jit(solution)/shard_map/all_to_all | solution.py:143
Sparse Core Ops, SparseCore 0:
  10.1 65.9 all-gather.4
  80.5 67.5 all-gather.6

commit v3 on v2

--- a/solution.py
+++ b/solution.py
@@ -8,7 +8,7 @@
 BF = jnp.bfloat16
 F32 = jnp.float32
 ROW_CONTRACT = (((1,), (1,)), ((), ()))
-TILE = 256
+TILE = 1024
 
 
 def rows_dot(left, right):
@@ -30,38 +30,78 @@
     return jnp.where(iota((size, size), 0) == components * (column - comp * nodes) + comp, 1.0, 0.0).astype(BF)
 
 
-def element_kernel(disp_ref, shared_ref, modulus_ref, conn_ref, stiff_ref, pieces_ref, sep_ref,
-                   table_ref, onehot_ref, kron_ref, gather_ref, force_ref, acc_ref):
+def fetch(source, target, semaphore):
+    copy = pltpu.make_async_copy(source, target, semaphore)
+    copy.start()
+    return copy
+
+
+def prepare_kernel(disp_hbm, stiff_hbm, table_ref, kron_ref, disp_ref, stiff_ref, disp_sem, stiff_sem):
+    disp_copy = fetch(disp_hbm, disp_ref, disp_sem)
+    stiff_copy = fetch(stiff_hbm, stiff_ref, stiff_sem)
     samples, inner = disp_ref.shape
-    shared = shared_ref.shape[1]
+    blocks = samples // 8
+    sort = spread(3, 128)
+    up = jnp.where((iota((192, 24), 0) >> 3) == iota((192, 24), 1), 1.0, 0.0).astype(BF)
+    same = (iota((192, 192), 0) & 7) == (iota((192, 192), 1) & 7)
+    stiff_copy.wait()
+    wide = rows_dot(plain_dot(up, stiff_ref[...].astype(BF)).astype(BF), up)
+    kron_ref[...] = jnp.where(same, wide, 0.0).astype(BF)
+    disp_copy.wait()
+    for chunk in range(inner // 384):
+        part = plain_dot(disp_ref[:, chunk * 384:(chunk + 1) * 384].astype(BF), sort)
+        rows = [
+            part[block * 8:block * 8 + 8, comp * 128:(comp + 1) * 128]
+            for block in range(blocks) for comp in range(3)
+        ]
+        table_ref[:, chunk * 128:(chunk + 1) * 128] = jnp.concatenate(rows, 0).astype(BF)
+
+
+def prepare(disp, stiffness):
+    samples, inner = disp.shape
+    return pl.pallas_call(
+        prepare_kernel,
+        in_specs=[pl.BlockSpec(memory_space=pl.ANY), pl.BlockSpec(memory_space=pl.ANY)],
+        out_shape=(
+            jax.ShapeDtypeStruct((3 * samples, inner // 3), BF),
+            jax.ShapeDtypeStruct((192, 192), BF),
+        ),
+        scratch_shapes=[
+            pltpu.VMEM(disp.shape, F32),
+            pltpu.VMEM(stiffness.shape, F32),
+            pltpu.SemaphoreType.DMA,
+            pltpu.SemaphoreType.DMA,
+        ],
+        compiler_params=pltpu.CompilerParams(vmem_limit_bytes=16 << 20),
+        name="prepare",
+    )(disp, stiffness)
+
+
+def element_kernel(shared_ref, modulus_hbm, conn_hbm, inner_table_ref, kron_ref, pieces_ref, sep_ref,
+                   modulus_ref, conn_ref, table_ref, onehot_ref, gather_ref, force_ref, acc_ref,
+                   modulus_sem, conn_sem):
+    conn_copy = fetch(conn_hbm, conn_ref, conn_sem)
+    modulus_copy = fetch(modulus_hbm, modulus_ref, modulus_sem)
+    samples, shared = shared_ref.shape
     elements = conn_ref.shape[1]
-    nodes = inner // 3
+    nodes = inner_table_ref.shape[1]
     sep_nodes = shared // 3
     all_nodes = nodes + sep_nodes
     blocks = samples // 8
     sort = spread(3, 128)
-    for chunk in range(nodes // 128):
-        part = plain_dot(disp_ref[:, chunk * 384:(chunk + 1) * 384].astype(BF), sort)
-        for block in range(blocks):
-            for comp in range(3):
-                row = block * 24 + comp * 8
-                table_ref[row:row + 8, chunk * 128:(chunk + 1) * 128] = part[
-                    block * 8:block * 8 + 8, comp * 128:(comp + 1) * 128]
+    table_ref[:, :nodes] = inner_table_ref[...]
     column = iota((shared, 384), 1)
     comp_of = (column >= 128).astype(jnp.int32) + (column >= 256).astype(jnp.int32)
     local = column - 128 * comp_of
     sep_sort = jnp.where((iota((shared, 384), 0) == 3 * local + comp_of) & (local < sep_nodes), 1.0, 0.0).astype(BF)
     part = plain_dot(shared_ref[...].astype(BF), sep_sort)
-    for block in range(blocks):
-        for comp in range(3):
-            row = block * 24 + comp * 8
-            table_ref[row:row + 8, nodes:nodes + 128] = part[
-                block * 8:block * 8 + 8, comp * 128:(comp + 1) * 128]
-    table = table_ref[:, :all_nodes].astype(BF)
-    up = jnp.where((iota((192, 24), 0) >> 3) == iota((192, 24), 1), 1.0, 0.0).astype(BF)
-    wide = rows_dot(plain_dot(up, stiff_ref[...].astype(BF)).astype(BF), up)
-    same = (iota((192, 192), 0) & 7) == (iota((192, 192), 1) & 7)
-    kron_ref[...] = jnp.where(same, wide, 0.0).astype(BF)
+    rows = [
+        part[block * 8:block * 8 + 8, comp * 128:(comp + 1) * 128] for block in range(blocks) for comp in range(3)
+    ]
+    table_ref[:, nodes:] = jnp.concatenate(rows, 0).astype(BF)
+    table = table_ref[:, :all_nodes]
+    conn_copy.wait()
+    modulus_copy.wait()
     acc_ref[...] = jnp.zeros_like(acc_ref)
 
     def tile_step(tile, carry):
@@ -116,27 +156,116 @@
     sep_ref[...] = total
 
 
-def assemble(disp, shared, modulus, connectivity, stiffness, pieces):
-    samples, inner = disp.shape
-    all_nodes = (inner + shared.shape[1]) // 3
-    padded = inner // 3 + 128
+def assemble(shared, modulus, connectivity, table, kron, pieces):
+    samples, width = shared.shape
+    nodes = table.shape[1]
+    all_nodes = nodes + width // 3
+    whole = pl.BlockSpec(memory_space=pltpu.VMEM)
+    far = pl.BlockSpec(memory_space=pl.ANY)
     return pl.pallas_call(
         element_kernel,
+        in_specs=[whole, far, far, whole, whole],
         out_shape=(
-            jax.ShapeDtypeStruct((pieces, samples, inner // pieces), BF),
-            jax.ShapeDtypeStruct((samples, shared.shape[1]), F32),
+            jax.ShapeDtypeStruct((pieces, samples, 3 * nodes // pieces), BF),
+            jax.ShapeDtypeStruct((samples, width), F32),
         ),
         scratch_shapes=[
-            pltpu.VMEM((3 * samples, padded), F32),
+            pltpu.VMEM(modulus.shape, F32),
+            pltpu.VMEM(connectivity.shape, jnp.int32),
+            pltpu.VMEM((3 * samples, nodes + 128), BF),
             pltpu.VMEM((all_nodes, 8 * TILE), BF),
-            pltpu.VMEM((192, 192), BF),
             pltpu.VMEM((3 * samples, 8 * TILE), F32),
             pltpu.VMEM((3 * samples, 8 * TILE), F32),
             pltpu.VMEM((3 * samples, all_nodes), F32),
+            pltpu.SemaphoreType.DMA,
+            pltpu.SemaphoreType.DMA,
         ],
-        compiler_params=pltpu.CompilerParams(vmem_limit_bytes=40 << 20),
+        compiler_params=pltpu.CompilerParams(vmem_limit_bytes=48 << 20),
         name="elements",
-    )(disp, shared, modulus, connectivity, stiffness)
+    )(shared, modulus, connectivity, table, kron)
+
+
+def near_kernel(terms_ref, band_hbm, q_ref, part_ref, band_ref, last_ref, band_sem, last_sem):
+    split = last_ref.shape[1]
+    begin = band_hbm.shape[1] - split
+    band_copy = fetch(band_hbm.at[:, :band_ref.shape[1]], band_ref, band_sem)
+    last_copy = fetch(band_hbm.at[:, begin:], last_ref, last_sem)
+    near, samples, width = terms_ref.shape
+    half = near * width // 4
+    terms = terms_ref[...].astype(F32)
+    q1 = jnp.concatenate([terms[2 * k] + terms[2 * k + 1] for k in range(near // 2)], 1)
+    q_ref[0] = q1
+    low = q1.astype(BF)
+    band_copy.wait()
+    q2 = -jnp.concatenate(
+        [plain_dot(low[:, :half], band_ref[:half, :half]), plain_dot(low[:, half:], band_ref[half:2 * half, :half])], 1)
+    q_ref[1] = q2
+    q3 = -plain_dot(q2.astype(BF), band_ref[:, half:3 * half])
+    q_ref[2] = q3
+    last_copy.wait()
+    offset = 3 * half - begin
+    part_ref[...] = (-plain_dot(q3.astype(BF), last_ref[:, offset:offset + 4 * half])).astype(BF)
+
+
+def near_levels(terms, bands):
+    near, samples, width = terms.shape
+    columns = near * width // 2
+    lead = -(-(3 * columns // 2) // 128) * 128
+    tail = bands.shape[1] - 3 * columns // 2 // 128 * 128
+    return pl.pallas_call(
+        near_kernel,
+        in_specs=[pl.BlockSpec(memory_space=pltpu.VMEM), pl.BlockSpec(memory_space=pl.ANY)],
+        scratch_shapes=[
+            pltpu.VMEM((columns, lead), BF),
+            pltpu.VMEM((columns, tail), BF),
+            pltpu.SemaphoreType.DMA,
+            pltpu.SemaphoreType.DMA,
+        ],
+        out_shape=(
+            jax.ShapeDtypeStruct((3, samples, columns), F32),
+            jax.ShapeDtypeStruct((samples, 2 * columns), BF),
+        ),
+        compiler_params=pltpu.CompilerParams(vmem_limit_bytes=16 << 20),
+        name="near_levels",
+    )(terms, bands)
+
+
+def far_kernel(front5_ref, z4_ref, z_ref, ring_hbm, band_ref, x4_ref, x_ref, ring_ref, upper_sem, lower_sem):
+    half = band_ref.shape[0] // 2
+    middle = ring_ref.shape[0] // 2
+    upper = fetch(ring_hbm.at[:middle], ring_ref.at[:middle], upper_sem)
+    lower = fetch(ring_hbm.at[middle:], ring_ref.at[middle:], lower_sem)
+    upper.wait()
+    first = rows_dot(front5_ref[...], ring_ref[:middle])
+    lower.wait()
+    x4 = z4_ref[...].astype(F32) - jnp.concatenate([first, rows_dot(front5_ref[...], ring_ref[middle:])], 1)
+    x4_ref[...] = x4
+    x3 = z_ref[2].astype(F32) - rows_dot(x4.astype(BF), band_ref[:, 3 * half:7 * half])
+    x_ref[2] = x3
+    x2 = z_ref[1].astype(F32) - rows_dot(x3.astype(BF), band_ref[:, half:3 * half])
+    x_ref[1] = x2
+    low = x2.astype(BF)
+    x_ref[0] = z_ref[0].astype(F32) - jnp.concatenate(
+        [rows_dot(low[:, :half], band_ref[:half, :half]), rows_dot(low[:, half:], band_ref[half:, :half])], 1)
+
+
+def far_levels(front5, z4, z_near, ring_band, bands):
+    whole = pl.BlockSpec(memory_space=pltpu.VMEM)
+    return pl.pallas_call(
+        far_kernel,
+        in_specs=[whole, whole, whole, pl.BlockSpec(memory_space=pl.ANY), whole],
+        scratch_shapes=[
+            pltpu.VMEM(ring_band.shape, BF),
+            pltpu.SemaphoreType.DMA,
+            pltpu.SemaphoreType.DMA,
+        ],
+        out_shape=(
+            jax.ShapeDtypeStruct(z4.shape, F32),
+            jax.ShapeDtypeStruct(z_near.shape, F32),
+        ),
+        compiler_params=pltpu.CompilerParams(vmem_limit_bytes=24 << 20),
+        name="far_levels",
+    )(front5, z4, z_near, ring_band, bands)
 
 
 def exchange(value, axis, groups=None):
@@ -181,15 +310,6 @@
     ring_groups = group_lists(leaves, 4)
     spot = leaf_index % near
     near_bands = lax.all_gather(coupling[:, :near_cols], "leaf", axis_index_groups=near_groups)
-    start5 = rows * (2**5 - 4)
-    ring_band = lax.all_gather(
-        lax.optimization_barrier((coupling, near_bands))[0][:, start5:2 * start5 + 4 * rows], "leaf",
-        axis_index_groups=ring_groups,
-    ).reshape(16 * rows, 32 * rows)
-
-    def band(height, width):
-        start = rows * (2**height - 4)
-        return near_bands[:, :, start:start + width].reshape(near * rows, width)
 
     def own_coupling(height):
         start = rows * (2**height - 4)
@@ -209,7 +329,8 @@
         sent = jnp.broadcast_to(low[None], (1 << height,) + low.shape)
         return exchange(sent, "leaf", group_lists(leaves, height))
 
-    pieces, sep_terms = assemble(interior_disp, shared, modulus, connectivity, stiffness, fronts)
+    table, kron = prepare(interior_disp, stiffness)
+    pieces, sep_terms = assemble(shared, modulus, connectivity, table, kron, fronts)
     received = exchange(pieces, "front")
     own_residual = load - jnp.sum(received.astype(F32), 0)
     own_low = own_residual.astype(BF)
@@ -224,19 +345,15 @@
     pivoted = own_residual + rows_dot(low_residual, leaf_pivot_inv)
 
     near_terms = exchange(jnp.broadcast_to(term.astype(BF)[None], (near,) + term.shape), "leaf", near_groups)
-    paired = near_terms.reshape(near // 2, 2, own_samples, 2 * rows).astype(F32).sum(1)
-    q1 = jnp.transpose(paired, (1, 0, 2)).reshape(own_samples, near * rows)
-    half = near * rows // 2
-    band2 = band(2, half)
-    band3 = band(3, 2 * half)
-    band4 = band(4, 4 * half)
-    low1 = q1.astype(BF)
-    q2 = -jnp.concatenate(
-        [plain_dot(low1[:, :half], band2[:half]), plain_dot(low1[:, half:], band2[half:])], 1)
-    low2 = q2.astype(BF)
-    q3 = -plain_dot(low2, band3)
-    low3 = q3.astype(BF)
-    part4 = (-plain_dot(low3, band4)).astype(BF)
+    bands = near_bands.reshape(near * rows, near_cols)
+    near_q, part4 = near_levels(near_terms, bands)
+    start5 = rows * (2**5 - 4)
+    ring_band = lax.all_gather(
+        lax.optimization_barrier((coupling, part4))[0][:, start5:2 * start5 + 4 * rows], "leaf",
+        axis_index_groups=ring_groups,
+    ).reshape(16 * rows, 32 * rows)
+    q1, q2, q3 = near_q[0], near_q[1], near_q[2]
+    low1, low2, low3 = q1.astype(BF), q2.astype(BF), q3.astype(BF)
     ring = 16
     across = []
     for source in range(leaves):
@@ -268,18 +385,18 @@
     z5 = q5 + rows_dot(full5, own_pivot(5))
     x6 = q6 + rows_dot(joined(collect(q6.astype(BF), 6)), own_pivot(6))
     x5 = z5 - rows_dot(joined(collect(x6.astype(BF), 6)), own_coupling(6))
-    last = collect(jnp.concatenate([x5, z4] + z_own, 1).astype(BF), 5)
+    packed5 = jnp.concatenate([x5, z4] + z_own, 1).astype(BF)
+    packed5, ring_band = lax.optimization_barrier((packed5, ring_band))
+    last = collect(packed5, 5)
     same_ring = lax.dynamic_slice_in_dim(last, leaf_index % 32 // 16 * 16, 16, 0)
-    x4_full = joined(same_ring[:, :, rows:2 * rows]).astype(F32) - rows_dot(joined(last[:, :, :rows]), ring_band)
-    full4 = x4_full.astype(BF)
+    nearby = lax.dynamic_slice_in_dim(last, leaf_index % 32 // near * near, near, 0)
+    z_near = jnp.transpose(
+        nearby[:, :, 2 * rows:].reshape(near, own_samples, 3, rows), (2, 1, 0, 3)
+    ).reshape(3, own_samples, near * rows)
+    x4_full, x_near = far_levels(
+        joined(last[:, :, :rows]), joined(same_ring[:, :, rows:2 * rows]), z_near, ring_band, bands)
     x4 = piece(x4_full, ring_spot)
-    nearby = lax.dynamic_slice_in_dim(last, leaf_index % 32 // near * near, near, 0)[:, :, rows:]
-    z1, z2, z3 = (joined(nearby[:, :, rows * k:rows * (k + 1)]).astype(F32) for k in (1, 2, 3))
-    x3 = z3 - rows_dot(full4, band4)
-    x2 = z2 - rows_dot(x3.astype(BF), band3)
-    low_x2 = x2.astype(BF)
-    x1 = z1 - jnp.concatenate(
-        [rows_dot(low_x2[:, :half], band2[:half]), rows_dot(low_x2[:, half:], band2[half:])], 1)
+    x1, x2, x3 = x_near[0], x_near[1], x_near[2]
     corrections = [piece(x1, spot), piece(x2, spot), piece(x3, spot), x4, x5, x6]
     front_low = lax.dynamic_slice_in_dim(x1.astype(BF), spot // 2 * (2 * rows), 2 * rows, 1)
     all_samples = exchange(jnp.broadcast_to(front_low[None], (fronts,) + front_low.shape), "front")

time: 228 us -> 225 us (0.987)
  matrix products: 8.44 us -> 3.27 us
  waiting for transfers between devices: 77.2 us -> 82.3 us
    all_gather x1, waiting for transfers between devices: 0.86 us -> 5.52 us  [body(): lax.all_gather(coupling[:, :near_cols], 'leaf', axis_index_groups=near_gr...]
    dot_general x14 -> x9, matrix products: 7.14 us -> 2.64 us  [rows_dot(): lax.dot_general(left, right, ROW_CONTRACT, preferred_element_type=F32)]
    slice x4, local copies, waits for them, and re-layouts: 4.22 us -> 0.87 us  [the longest x1 0.77 us: body(): lax.optimization_barrier((coupling, part4))[0]]
    unnamed x23 -> x31, local copies, waits for them, and re-layouts: 6.93 us -> 9.82 us
    pallas_call x1 -> x4, Pallas kernels: 10.2 us -> 12 us  [the longest x1 7.97 us: assemble(): pl.pallas_call(element_kernel, in_specs=[whole, far, far, whole, whole],...]
  transfers between devices with their start and end apart: 10 -> 10, of which waited for: 9 -> 8; matrix products, arithmetic and copies ran while one was open for 7% -> 4% of each run, Pallas kernels for 4% -> 4%
where the time goes in v3:
time: 225 us; the launch traced here: 224 us
  waiting for transfers between devices  82.3 us (37%)
  starting transfers between devices  50.2 us (22%)
  blocking collectives  43.6 us (19%)
  local copies, waits for them, and re-layouts  17.5 us (8%)
  between operations  14.6 us (6%)
  Pallas kernels  12 us (5%)
  matrix products  3.27 us (1%)
    all_to_all x6, waiting for transfers between devices, exchange(): lax.all_to_all(value, axis, 0, 0, axis_index_groups=groups, tiled=True)  70.3 us
    all_to_all x6, starting transfers between devices, exchange(): lax.all_to_all(value, axis, 0, 0, axis_index_groups=groups, tiled=True)  43.8 us
    all_to_all x3, blocking collectives, exchange(): lax.all_to_all(value, axis, 0, 0, axis_index_groups=groups, tiled=True)  43.6 us
    unnamed x31, local copies, waits for them, and re-layouts  9.82 us
    pallas_call x1, Pallas kernels, assemble(): pl.pallas_call(element_kernel, in_specs=[whole, far, far, whole, whole],...  7.97 us
    ppermute x1, waiting for transfers between devices, body(): q4 = part4.astype(F32) + lax.ppermute(part4, 'leaf', across).astype(F32)  6.41 us
    all_gather x1, waiting for transfers between devices, body(): lax.all_gather(coupling[:, :near_cols], 'leaf', axis_index_groups=near_gr...  5.52 us
  transfers between devices with their start and end apart: 10, of which 8 were waited for; matrix products, arithmetic and copies ran while one was open for 4% of the time, Pallas kernels for 4%

profile of v3, /device:TPU:1, one launch (start us, length us, event | category | flops | bytes accessed | tf_op | source)
XLA Modules:
  0.0 224.0 jit_solution(10450153345326547693)
XLA Ops:
  7.2 1.6 slice.80
  8.9 0.8 copy.34
  9.8 4.4 %collective-permute-start = (f32[64,48]{1,0:T(8,128)S(1)}, f32[64,48]{1,0:T(8,128)S(1)}, u32[]{:S(2)}, u32[]{:S(2)}) collective-permute-start(f32[64,48]{1,0:T(8,128)S(1)} %copy.34), channel_id=1, source_target_pairs={{0,8},{8,0},{16,24},{24,16},{32,40},{40,32},{48,56},{56,48},{64,72... | collective-permute-start | bytes 36872 | tf_op jit(solution)/shard_map/ppermute | solution.py:300
  14.2 1.0 copy-done.4
  15.1 0.7 copy-done.7
  15.8 1.0 prepare.1
  16.9 0.9 copy-done.5
  17.9 0.8 copy-done.6
  18.6 8.0 %elements.1 = (bf16[8,64,192]{2,1,0:T(8,128)(2,1)S(1)}, f32[64,96]{1,0:T(8,128)S(1)}) custom-call(f32[64,96]{1,0:T(8,128)S(1)} %maximum_select_fusion.shared_ref, f32[64,1024]{1,0:T(8,128)S(1)} %copy-done.5, s32[8,1024]{1,0:T(8,128)S(1)} %copy-done.6, bf16[192,512]{1,0:T(8,128)(2,1)S(1)} %get-tuple-element.13.inner_table_ref, ...), custom_call_target="tpu_custom_call" | custom-call | tf_op jit(solution)/shard_map/elements/pallas_call | solution.py:165
  26.6 14.9 %all_to_all.45 = bf16[8,64,192]{2,1,0:T(8,128)(2,1)S(1)} all-to-all(bf16[8,64,192]{2,1,0:T(8,128)(2,1)S(1)} %get-tuple-element.15), channel_id=1, replica_groups=mesh['leaf'=64,'front'=8] {'front'}, dimensions={0} | all-to-all | bytes 393216 | tf_op jit(solution)/shard_map/all_to_all | solution.py:272
  41.8 10.3 %all_to_all.46 = bf16[8,72,192]{2,1,0:T(8,128)(2,1)S(1)} all-to-all(bf16[8,72,192]{2,1,0:T(8,128)(2,1)S(1)} %maximum_maximum_fusion), channel_id=1, replica_groups=mesh['leaf'=64,'front'=8] {'front'}, dimensions={0} | all-to-all | bytes 442368 | tf_op jit(solution)/shard_map/all_to_all | solution.py:272
  52.2 18.4 %all_to_all.47.terms_ref = bf16[8,8,96]{2,1,0:T(8,128)(2,1)S(1)} all-to-all(bf16[8,8,96]{2,1,0:T(8,128)(2,1)S(1)} %broadcast_in_dim.15), channel_id=1, replica_groups={{0,8,16,24,32,40,48,56},{64,72,80,88,96,104,112,120},{128,136,144,152,1..., dimensions={0} | all-to-all | bytes 24576 | tf_op jit(solution)/shard_map/all_to_all | solution.py:272
  70.6 5.5 %all-gather.5.cloned.1.call-done.band_hbm.band_ref = bf16[384,1408]{1,0:T(8,128)(2,1)} async-done(((bf16[48,1408]{1,0:T(8,128)(2,1)}), bf16[384,1408]{1,0:T(8,128)(2,1)}) %all-gather.5.cloned.1.call-update) | async-done | bytes 1081360 | tf_op jit(solution)/shard_map/all_gather | solution.py:312
  76.1 1.2 copy-done.1
  77.4 1.0 near_levels.1
  78.4 0.8 slice.94
  79.3 1.9 collective-permute-start.1
  81.2 6.4 %collective-permute-done.1 = bf16[8,768]{1,0:T(8,128)(2,1)S(1)} collective-permute-done((bf16[8,768]{1,0:T(8,128)(2,1)S(1)}, bf16[8,768]{1,0:T(8,128)(2,1)S(1)}, u32[]{:S(2)}, u32[]{:S(2)}) %collective-permute-start.1) | collective-permute-done | bytes 12320 | tf_op jit(solution)/shard_map/ppermute | solution.py:363
  87.6 0.2 fusion.1
  88.0 0.7 reshape.89
  88.8 7.1 %all-to-all-start.3 = ((bf16[32,2,192]{2,1,0:T(2,128)(2,1)}), bf16[32,2,192]{2,1,0:T(2,128)(2,1)S(1)}, u32[]{:S(2)}, u32[]{:S(2)}) async-start(bf16[32,2,192]{2,1,0:T(2,128)(2,1)} %reshape.89), calls=%async_computation.3 | async-start | bytes 65536 | tf_op jit(solution)/shard_map/all_to_all | solution.py:272
  96.1 12.7 %all-to-all-done.3 = bf16[32,2,192]{2,1,0:T(2,128)(2,1)S(1)} async-done(((bf16[32,2,192]{2,1,0:T(2,128)(2,1)}), bf16[32,2,192]{2,1,0:T(2,128)(2,1)S(1)}, u32[]{:S(2)}, u32[]{:S(2)}) %all-to-all-start.3) | async-done | bytes 24608 | tf_op jit(solution)/shard_map/all_to_all | solution.py:272
  109.0 0.3 fusion
  109.6 0.7 copy.39
  110.3 4.8 %all-to-all-start.4 = ((bf16[64,8,96]{2,1,0:T(8,128)(2,1)}), bf16[64,8,96]{2,1,0:T(8,128)(2,1)S(1)}, u32[]{:S(2)}, u32[]{:S(2)}) async-start(bf16[64,8,96]{2,1,0:T(8,128)(2,1)} %copy.39), calls=%async_computation.4 | async-start | bytes 262144 | tf_op jit(solution)/shard_map/all_to_all | solution.py:272
  115.6 13.9 %all-to-all-done.4 = bf16[64,8,96]{2,1,0:T(8,128)(2,1)S(1)} async-done(((bf16[64,8,96]{2,1,0:T(8,128)(2,1)}), bf16[64,8,96]{2,1,0:T(8,128)(2,1)S(1)}, u32[]{:S(2)}, u32[]{:S(2)}) %all-to-all-start.4) | async-done | bytes 98336 | tf_op jit(solution)/shard_map/all_to_all | solution.py:272
  129.5 0.8 reshape.91
  130.3 6.1 %all-to-all-start.5 = ((bf16[64,2,192]{2,1,0:T(2,128)(2,1)}), bf16[64,2,192]{2,1,0:T(2,128)(2,1)S(1)}, u32[]{:S(2)}, u32[]{:S(2)}) async-start(bf16[64,2,192]{2,1,0:T(2,128)(2,1)} %reshape.91), calls=%async_computation.5 | async-start | bytes 131072 | tf_op jit(solution)/shard_map/all_to_all | solution.py:272
  136.4 0.2 add_convert_fusion
  136.9 13.0 %all-to-all-done.5 = bf16[64,2,192]{2,1,0:T(2,128)(2,1)S(1)} async-done(((bf16[64,2,192]{2,1,0:T(2,128)(2,1)}), bf16[64,2,192]{2,1,0:T(2,128)(2,1)S(1)}, u32[]{:S(2)}, u32[]{:S(2)}) %all-to-all-start.5) | async-done | bytes 49184 | tf_op jit(solution)/shard_map/all_to_all | solution.py:272
  150.2 0.3 fusion.32
  150.5 0.8 reshape.93
  151.3 4.9 %all-to-all-start.6 = ((bf16[64,2,192]{2,1,0:T(2,128)(2,1)}), bf16[64,2,192]{2,1,0:T(2,128)(2,1)S(1)}, u32[]{:S(2)}, u32[]{:S(2)}) async-start(bf16[64,2,192]{2,1,0:T(2,128)(2,1)} %reshape.93), calls=%async_computation.6 | async-start | bytes 131072 | tf_op jit(solution)/shard_map/all_to_all | solution.py:272
  156.2 0.2 convolution_add_fusion.5
  156.4 13.3 %all-to-all-done.6 = bf16[64,2,192]{2,1,0:T(2,128)(2,1)S(1)} async-done(((bf16[64,2,192]{2,1,0:T(2,128)(2,1)}), bf16[64,2,192]{2,1,0:T(2,128)(2,1)S(1)}, u32[]{:S(2)}, u32[]{:S(2)}) %all-to-all-start.6) | async-done | bytes 49184 | tf_op jit(solution)/shard_map/all_to_all | solution.py:272
  170.1 0.3 fusion.33
  170.5 0.7 broadcast_in_dim.19
  171.1 3.8 %all-to-all-start.7 = ((bf16[32,8,240]{2,1,0:T(8,128)(2,1)}), bf16[32,8,240]{2,1,0:T(8,128)(2,1)S(1)}, u32[]{:S(2)}, u32[]{:S(2)}) async-start(bf16[32,8,240]{2,1,0:T(8,128)(2,1)} %broadcast_in_dim.19), calls=%async_computation.7 | async-start | bytes 262144 | tf_op jit(solution)/shard_map/all_to_all | solution.py:272
  175.2 0.2 reshape.72
  175.4 0.3 convolution_add_fusion
  175.7 13.7 %all-to-all-done.7 = bf16[32,8,240]{2,1,0:T(8,128)(2,1)S(1)} async-done(((bf16[32,8,240]{2,1,0:T(8,128)(2,1)}), bf16[32,8,240]{2,1,0:T(8,128)(2,1)S(1)}, u32[]{:S(2)}, u32[]{:S(2)}) %all-to-all-start.7) | async-done | bytes 122912 | tf_op jit(solution)/shard_map/all_to_all | solution.py:272
  190.1 1.7 copy-done.3
  191.8 2.1 far_levels.1
  194.1 0.6 broadcast_in_dim.20
  194.7 17.0 %all-to-all-start.8 = ((bf16[8,8,96]{2,1,0:T(8,128)(2,1)}), bf16[8,8,96]{2,1,0:T(8,128)(2,1)S(1)}, u32[]{:S(2)}, u32[]{:S(2)}) async-start(bf16[8,8,96]{2,1,0:T(8,128)(2,1)} %broadcast_in_dim.20), calls=%async_computation.8 | async-start | bytes 32768 | tf_op jit(solution)/shard_map/all_to_all | solution.py:272
  211.8 0.7 concatenate.36
  212.5 3.8 %all-to-all-done.8 = bf16[8,8,96]{2,1,0:T(8,128)(2,1)S(1)} async-done(((bf16[8,8,96]{2,1,0:T(8,128)(2,1)}), bf16[8,8,96]{2,1,0:T(8,128)(2,1)S(1)}, u32[]{:S(2)}, u32[]{:S(2)}) %all-to-all-start.8) | async-done | bytes 12320 | tf_op jit(solution)/shard_map/all_to_all | solution.py:272
  216.3 0.8 convolution_subtract_fusion
  (77 shorter events, 4.1 us)
Async XLA Ops:
  7.2 168.2 %copy-start = (bf16[192,1536]{1,0:T(8,128)(2,1)S(1)}, bf16[192,1536]{1,0:T(8,128)(2,1)}, u32[]{:S(2)}) copy-start(bf16[192,1536]{1,0:T(8,128)(2,1)} %param.16) | copy-start | bytes 1769476
  7.2 34.3 %copy-start.11 = (f32[64,192]{1,0:T(8,128)S(1)}, f32[64,192]{1,0:T(8,128)}, u32[]{:S(2)}) copy-start(f32[64,192]{1,0:T(8,128)} %param.15) | copy-start | bytes 147460
  7.2 34.4 %copy-start.10 = (bf16[192,96]{1,0:T(8,128)(2,1)S(1)}, bf16[192,96]{1,0:T(8,128)(2,1)}, u32[]{:S(2)}) copy-start(bf16[192,96]{1,0:T(8,128)(2,1)} %param.17) | copy-start | bytes 110596
  7.2 68.9 %all-gather.5.cloned.1.call-start = ((), (), s32[]{:S(2)}) async-start(), calls=%async_computation.9 | async-start | bytes 1216512 | tf_op jit(solution)/shard_map/all_gather | solution.py:312
  8.9 161.6 %all-gather.7.cloned.1.call-start = ((), (), s32[]{:S(2)}) async-start(), calls=%async_computation.10 | async-start | bytes 2506752 | tf_op jit(solution)/shard_map/all_gather | solution.py:351
  9.8 7.1 %collective-permute-start = (f32[64,48]{1,0:T(8,128)S(1)}, f32[64,48]{1,0:T(8,128)S(1)}, u32[]{:S(2)}, u32[]{:S(2)}) collective-permute-start(f32[64,48]{1,0:T(8,128)S(1)} %copy.34), channel_id=1, source_target_pairs={{0,8},{8,0},{16,24},{24,16},{32,40},{40,32},{48,56},{56,48},{64,72... | collective-permute-start | bytes 36872 | tf_op jit(solution)/shard_map/ppermute | solution.py:300
  14.1 1.0 copy-start.4
  15.1 0.7 copy-start.7
  16.9 1.0 copy-start.5
  17.9 0.8 copy-start.6
  18.6 59.7 %copy-start.8 = (bf16[48,5952]{1,0:T(8,128)(2,1)S(1)}, bf16[48,5952]{1,0:T(8,128)(2,1)}, u32[]{:S(2)}) copy-start(bf16[48,5952]{1,0:T(8,128)(2,1)} %param.19) | copy-start | bytes 1714180
  41.5 54.5 %copy-start.9 = (bf16[48,6048]{1,0:T(8,128)(2,1)S(1)}, bf16[48,6048]{1,0:T(8,128)(2,1)}, u32[]{:S(2)}) copy-start(bf16[48,6048]{1,0:T(8,128)(2,1)} %param.18) | copy-start | bytes 1741828
  76.1 1.2 copy-start.1
  79.3 8.3 %collective-permute-start.1 = (bf16[8,768]{1,0:T(8,128)(2,1)S(1)}, bf16[8,768]{1,0:T(8,128)(2,1)S(1)}, u32[]{:S(2)}, u32[]{:S(2)}) collective-permute-start(bf16[8,768]{1,0:T(8,128)(2,1)S(1)} %get-tuple-element.17), channel_id=1, source_target_pairs={{0,96},{8,104},{16,112},{24,120},{32,64},{40,72},{48,80},{56,88},{... | collective-permute-start | bytes 36872 | tf_op jit(solution)/shard_map/ppermute | solution.py:363
  88.8 20.1 %all-to-all-start.3 = ((bf16[32,2,192]{2,1,0:T(2,128)(2,1)}), bf16[32,2,192]{2,1,0:T(2,128)(2,1)S(1)}, u32[]{:S(2)}, u32[]{:S(2)}) async-start(bf16[32,2,192]{2,1,0:T(2,128)(2,1)} %reshape.89), calls=%async_computation.3 | async-start | bytes 65536 | tf_op jit(solution)/shard_map/all_to_all | solution.py:272
  110.3 19.1 %all-to-all-start.4 = ((bf16[64,8,96]{2,1,0:T(8,128)(2,1)}), bf16[64,8,96]{2,1,0:T(8,128)(2,1)S(1)}, u32[]{:S(2)}, u32[]{:S(2)}) async-start(bf16[64,8,96]{2,1,0:T(8,128)(2,1)} %copy.39), calls=%async_computation.4 | async-start | bytes 262144 | tf_op jit(solution)/shard_map/all_to_all | solution.py:272
  130.3 19.5 %all-to-all-start.5 = ((bf16[64,2,192]{2,1,0:T(2,128)(2,1)}), bf16[64,2,192]{2,1,0:T(2,128)(2,1)S(1)}, u32[]{:S(2)}, u32[]{:S(2)}) async-start(bf16[64,2,192]{2,1,0:T(2,128)(2,1)} %reshape.91), calls=%async_computation.5 | async-start | bytes 131072 | tf_op jit(solution)/shard_map/all_to_all | solution.py:272
  151.3 18.4 %all-to-all-start.6 = ((bf16[64,2,192]{2,1,0:T(2,128)(2,1)}), bf16[64,2,192]{2,1,0:T(2,128)(2,1)S(1)}, u32[]{:S(2)}, u32[]{:S(2)}) async-start(bf16[64,2,192]{2,1,0:T(2,128)(2,1)} %reshape.93), calls=%async_computation.6 | async-start | bytes 131072 | tf_op jit(solution)/shard_map/all_to_all | solution.py:272
  156.4 33.6 %copy-start.2 = (bf16[384,1408]{1,0:T(8,128)(2,1)S(1)}, bf16[384,1408]{1,0:T(8,128)(2,1)}, u32[]{:S(2)}) copy-start(bf16[384,1408]{1,0:T(8,128)(2,1)} %all-gather.5.cloned.1.call-done.band_hbm.band_ref) | copy-start | bytes 3244036
  171.1 18.3 %all-to-all-start.7 = ((bf16[32,8,240]{2,1,0:T(8,128)(2,1)}), bf16[32,8,240]{2,1,0:T(8,128)(2,1)S(1)}, u32[]{:S(2)}, u32[]{:S(2)}) async-start(bf16[32,8,240]{2,1,0:T(8,128)(2,1)} %broadcast_in_dim.19), calls=%async_computation.7 | async-start | bytes 262144 | tf_op jit(solution)/shard_map/all_to_all | solution.py:272
  190.1 1.7 copy-start.3
  194.7 21.7 %all-to-all-start.8 = ((bf16[8,8,96]{2,1,0:T(8,128)(2,1)}), bf16[8,8,96]{2,1,0:T(8,128)(2,1)S(1)}, u32[]{:S(2)}, u32[]{:S(2)}) async-start(bf16[8,8,96]{2,1,0:T(8,128)(2,1)} %broadcast_in_dim.20), calls=%async_computation.8 | async-start | bytes 32768 | tf_op jit(solution)/shard_map/all_to_all | solution.py:272
Sparse Core Ops, SparseCore 0:
  10.1 66.0 all-gather.4
  79.3 68.4 all-gather.6

commit v4 on v3

--- a/solution.py
+++ b/solution.py
@@ -9,6 +9,7 @@
 F32 = jnp.float32
 ROW_CONTRACT = (((1,), (1,)), ((), ()))
 TILE = 1024
+ZIGZAG = (0, 2, 4, 6, 7, 5, 3, 1)
 
 
 def rows_dot(left, right):
@@ -61,7 +62,7 @@
     samples, inner = disp.shape
     return pl.pallas_call(
         prepare_kernel,
-        in_specs=[pl.BlockSpec(memory_space=pl.ANY), pl.BlockSpec(memory_space=pl.ANY)],
+        in_specs=[pl.BlockSpec(memory_space=pltpu.HBM), pl.BlockSpec(memory_space=pltpu.HBM)],
         out_shape=(
             jax.ShapeDtypeStruct((3 * samples, inner // 3), BF),
             jax.ShapeDtypeStruct((192, 192), BF),
@@ -161,7 +162,7 @@
     nodes = table.shape[1]
     all_nodes = nodes + width // 3
     whole = pl.BlockSpec(memory_space=pltpu.VMEM)
-    far = pl.BlockSpec(memory_space=pl.ANY)
+    far = pl.BlockSpec(memory_space=pltpu.HBM)
     return pl.pallas_call(
         element_kernel,
         in_specs=[whole, far, far, whole, whole],
@@ -185,24 +186,51 @@
     )(shared, modulus, connectivity, table, kron)
 
 
+def fetch_leaves(source, begin, target, semaphores):
+    height = target.shape[0] // len(ZIGZAG)
+    width = target.shape[1]
+    return [
+        fetch(source.at[at * height:(at + 1) * height, begin:begin + width],
+              target.at[leaf * height:(leaf + 1) * height], semaphores.at[at])
+        for at, leaf in enumerate(ZIGZAG)
+    ]
+
+
+def crop_kernel(source, target, semaphore):
+    fetch(source.at[:, :target.shape[1]], target, semaphore).wait()
+
+
+def crop(array, columns):
+    return pl.pallas_call(
+        crop_kernel,
+        in_specs=[pl.BlockSpec(memory_space=pltpu.HBM)],
+        out_specs=pl.BlockSpec(memory_space=pltpu.HBM),
+        out_shape=jax.ShapeDtypeStruct((array.shape[0], columns), array.dtype),
+        scratch_shapes=[pltpu.SemaphoreType.DMA],
+        name="crop",
+    )(array)
+
+
 def near_kernel(terms_ref, band_hbm, q_ref, part_ref, band_ref, last_ref, band_sem, last_sem):
     split = last_ref.shape[1]
     begin = band_hbm.shape[1] - split
-    band_copy = fetch(band_hbm.at[:, :band_ref.shape[1]], band_ref, band_sem)
-    last_copy = fetch(band_hbm.at[:, begin:], last_ref, last_sem)
     near, samples, width = terms_ref.shape
+    band_copies = fetch_leaves(band_hbm, 0, band_ref, band_sem)
+    last_copies = fetch_leaves(band_hbm, begin, last_ref, last_sem)
     half = near * width // 4
     terms = terms_ref[...].astype(F32)
     q1 = jnp.concatenate([terms[2 * k] + terms[2 * k + 1] for k in range(near // 2)], 1)
     q_ref[0] = q1
     low = q1.astype(BF)
-    band_copy.wait()
+    for copy in band_copies:
+        copy.wait()
     q2 = -jnp.concatenate(
         [plain_dot(low[:, :half], band_ref[:half, :half]), plain_dot(low[:, half:], band_ref[half:2 * half, :half])], 1)
     q_ref[1] = q2
     q3 = -plain_dot(q2.astype(BF), band_ref[:, half:3 * half])
     q_ref[2] = q3
-    last_copy.wait()
+    for copy in last_copies:
+        copy.wait()
     offset = 3 * half - begin
     part_ref[...] = (-plain_dot(q3.astype(BF), last_ref[:, offset:offset + 4 * half])).astype(BF)
 
@@ -214,12 +242,12 @@
     tail = bands.shape[1] - 3 * columns // 2 // 128 * 128
     return pl.pallas_call(
         near_kernel,
-        in_specs=[pl.BlockSpec(memory_space=pltpu.VMEM), pl.BlockSpec(memory_space=pl.ANY)],
+        in_specs=[pl.BlockSpec(memory_space=pltpu.VMEM), pl.BlockSpec(memory_space=pltpu.HBM)],
         scratch_shapes=[
             pltpu.VMEM((columns, lead), BF),
             pltpu.VMEM((columns, tail), BF),
-            pltpu.SemaphoreType.DMA,
-            pltpu.SemaphoreType.DMA,
+            pltpu.SemaphoreType.DMA((near,)),
+            pltpu.SemaphoreType.DMA((near,)),
         ],
         out_shape=(
             jax.ShapeDtypeStruct((3, samples, columns), F32),
@@ -230,16 +258,20 @@
     )(terms, bands)
 
 
-def far_kernel(front5_ref, z4_ref, z_ref, ring_hbm, band_ref, x4_ref, x_ref, ring_ref, upper_sem, lower_sem):
+def far_kernel(front5_ref, z4_ref, z_ref, ring_hbm, band_hbm, x4_ref, x_ref, ring_ref, band_ref,
+               upper_sem, lower_sem, band_sem):
     half = band_ref.shape[0] // 2
     middle = ring_ref.shape[0] // 2
     upper = fetch(ring_hbm.at[:middle], ring_ref.at[:middle], upper_sem)
     lower = fetch(ring_hbm.at[middle:], ring_ref.at[middle:], lower_sem)
+    band_copies = fetch_leaves(band_hbm, 0, band_ref, band_sem)
     upper.wait()
     first = rows_dot(front5_ref[...], ring_ref[:middle])
     lower.wait()
     x4 = z4_ref[...].astype(F32) - jnp.concatenate([first, rows_dot(front5_ref[...], ring_ref[middle:])], 1)
     x4_ref[...] = x4
+    for copy in band_copies:
+        copy.wait()
     x3 = z_ref[2].astype(F32) - rows_dot(x4.astype(BF), band_ref[:, 3 * half:7 * half])
     x_ref[2] = x3
     x2 = z_ref[1].astype(F32) - rows_dot(x3.astype(BF), band_ref[:, half:3 * half])
@@ -253,11 +285,13 @@
     whole = pl.BlockSpec(memory_space=pltpu.VMEM)
     return pl.pallas_call(
         far_kernel,
-        in_specs=[whole, whole, whole, pl.BlockSpec(memory_space=pl.ANY), whole],
+        in_specs=[whole, whole, whole] + [pl.BlockSpec(memory_space=pltpu.HBM)] * 2,
         scratch_shapes=[
             pltpu.VMEM(ring_band.shape, BF),
-            pltpu.SemaphoreType.DMA,
-            pltpu.SemaphoreType.DMA,
+            pltpu.VMEM(bands.shape, BF),
+            pltpu.SemaphoreType.DMA,
+            pltpu.SemaphoreType.DMA,
+            pltpu.SemaphoreType.DMA((len(ZIGZAG),)),
         ],
         out_shape=(
             jax.ShapeDtypeStruct(z4.shape, F32),
@@ -309,7 +343,8 @@
     near_groups = [[base + i for i in range(near)] for base in range(0, leaves, near)]
     ring_groups = group_lists(leaves, 4)
     spot = leaf_index % near
-    near_bands = lax.all_gather(coupling[:, :near_cols], "leaf", axis_index_groups=near_groups)
+    zigzag_groups = [[base + at for at in ZIGZAG] for base in range(0, leaves, near)]
+    near_bands = lax.all_gather(crop(coupling, near_cols), "leaf", axis_index_groups=zigzag_groups)
 
     def own_coupling(height):
         start = rows * (2**height - 4)

time: 225 us -> 222 us (0.987)
  Pallas kernels: 12 us -> 19.2 us
  waiting for transfers between devices: 82.3 us -> 75.6 us
    pallas_call x2 -> x3, Pallas kernels: 3.08 us -> 9.96 us  [the longest x1 5.21 us: crop(): pl.pallas_call(crop_kernel, in_specs=[pl.BlockSpec(memory_space=pltpu.HBM...]
    all_gather x1, waiting for transfers between devices: 5.52 us -> 0.01 us  [body(): lax.all_gather(crop(coupling, near_cols), 'leaf', axis_index_groups=zigza...]
    all_to_all x6, starting transfers between devices: 43.8 us -> 41 us  [exchange(): lax.all_to_all(value, axis, 0, 0, axis_index_groups=groups, tiled=True)]
  transfers between devices with their start and end apart: 10 -> 10, of which waited for: 8 -> 7; matrix products, arithmetic and copies ran while one was open for 4% -> 4% of each run, Pallas kernels for 4% -> 4%
where the time goes in v4:
time: 222 us; the launch traced here: 221 us
  waiting for transfers between devices  75.6 us (34%)
  starting transfers between devices  48.5 us (22%)
  blocking collectives  43 us (19%)
  Pallas kernels  19.2 us (9%)
  local copies, waits for them, and re-layouts  15.8 us (7%)
  between operations  14.6 us (7%)
  matrix products  3.27 us (1%)
    all_to_all x6, waiting for transfers between devices, exchange(): lax.all_to_all(value, axis, 0, 0, axis_index_groups=groups, tiled=True)  70.4 us
    all_to_all x3, blocking collectives, exchange(): lax.all_to_all(value, axis, 0, 0, axis_index_groups=groups, tiled=True)  43 us
    all_to_all x6, starting transfers between devices, exchange(): lax.all_to_all(value, axis, 0, 0, axis_index_groups=groups, tiled=True)  41 us
    unnamed x31, local copies, waits for them, and re-layouts  9.83 us
    pallas_call x1, Pallas kernels, assemble(): pl.pallas_call(element_kernel, in_specs=[whole, far, far, whole, whole],...  7.97 us
    ppermute x1, waiting for transfers between devices, body(): q4 = part4.astype(F32) + lax.ppermute(part4, 'leaf', across).astype(F32)  5.21 us
    pallas_call x1, Pallas kernels, crop(): pl.pallas_call(crop_kernel, in_specs=[pl.BlockSpec(memory_space=pltpu.HBM...  5.21 us
  transfers between devices with their start and end apart: 10, of which 7 were waited for; matrix products, arithmetic and copies ran while one was open for 4% of the time, Pallas kernels for 4%

profile of v4, /device:TPU:1, one launch (start us, length us, event | category | flops | bytes accessed | tf_op | source)
XLA Modules:
  0.0 220.7 jit_solution(331632723712920673)
XLA Ops:
  7.2 5.2 %crop.1 = bf16[48,1408]{1,0:T(8,128)(2,1)} custom-call(bf16[48,5952]{1,0:T(8,128)(2,1)} %source.1), custom_call_target="tpu_custom_call" | custom-call | tf_op jit(solution)/shard_map/crop/pallas_call | solution.py:204
  12.5 0.8 copy.34
  13.3 4.4 %collective-permute-start = (f32[64,48]{1,0:T(8,128)S(1)}, f32[64,48]{1,0:T(8,128)S(1)}, u32[]{:S(2)}, u32[]{:S(2)}) collective-permute-start(f32[64,48]{1,0:T(8,128)S(1)} %copy.34), channel_id=1, source_target_pairs={{0,8},{8,0},{16,24},{24,16},{32,40},{40,32},{48,56},{56,48},{64,72... | collective-permute-start | bytes 36872 | tf_op jit(solution)/shard_map/ppermute | solution.py:334
  17.7 1.0 copy-done.4
  18.7 0.7 copy-done.7
  19.4 1.0 prepare.1
  20.5 0.9 copy-done.5
  21.5 0.8 copy-done.6
  22.2 8.0 %elements.1 = (bf16[8,64,192]{2,1,0:T(8,128)(2,1)S(1)}, f32[64,96]{1,0:T(8,128)S(1)}) custom-call(f32[64,96]{1,0:T(8,128)S(1)} %maximum_select_fusion.shared_ref, f32[64,1024]{1,0:T(8,128)S(1)} %copy-done.5, s32[8,1024]{1,0:T(8,128)S(1)} %copy-done.6, bf16[192,512]{1,0:T(8,128)(2,1)S(1)} %get-tuple-element.13.inner_table_ref, ...), custom_call_target="tpu_custom_call" | custom-call | tf_op jit(solution)/shard_map/elements/pallas_call | solution.py:166
  30.2 14.5 %all_to_all.45 = bf16[8,64,192]{2,1,0:T(8,128)(2,1)S(1)} all-to-all(bf16[8,64,192]{2,1,0:T(8,128)(2,1)S(1)} %get-tuple-element.15), channel_id=1, replica_groups=mesh['leaf'=64,'front'=8] {'front'}, dimensions={0} | all-to-all | bytes 393216 | tf_op jit(solution)/shard_map/all_to_all | solution.py:306
  45.0 10.7 %all_to_all.46 = bf16[8,72,192]{2,1,0:T(8,128)(2,1)S(1)} all-to-all(bf16[8,72,192]{2,1,0:T(8,128)(2,1)S(1)} %maximum_maximum_fusion), channel_id=1, replica_groups=mesh['leaf'=64,'front'=8] {'front'}, dimensions={0} | all-to-all | bytes 442368 | tf_op jit(solution)/shard_map/all_to_all | solution.py:306
  55.8 17.9 %all_to_all.47.terms_ref = bf16[8,8,96]{2,1,0:T(8,128)(2,1)S(1)} all-to-all(bf16[8,8,96]{2,1,0:T(8,128)(2,1)S(1)} %broadcast_in_dim.15), channel_id=1, replica_groups={{0,8,16,24,32,40,48,56},{64,72,80,88,96,104,112,120},{128,136,144,152,1..., dimensions={0} | all-to-all | bytes 24576 | tf_op jit(solution)/shard_map/all_to_all | solution.py:306
  73.7 1.2 copy-done.1
  74.9 1.2 near_levels.1
  76.2 0.8 slice.90
  77.1 3.1 %collective-permute-start.1 = (bf16[8,768]{1,0:T(8,128)(2,1)S(1)}, bf16[8,768]{1,0:T(8,128)(2,1)S(1)}, u32[]{:S(2)}, u32[]{:S(2)}) collective-permute-start(bf16[8,768]{1,0:T(8,128)(2,1)S(1)} %get-tuple-element.17), channel_id=1, source_target_pairs={{0,96},{8,104},{16,112},{24,120},{32,64},{40,72},{48,80},{56,88},{... | collective-permute-start | bytes 36872 | tf_op jit(solution)/shard_map/ppermute | solution.py:398
  80.3 5.2 %collective-permute-done.1 = bf16[8,768]{1,0:T(8,128)(2,1)S(1)} collective-permute-done((bf16[8,768]{1,0:T(8,128)(2,1)S(1)}, bf16[8,768]{1,0:T(8,128)(2,1)S(1)}, u32[]{:S(2)}, u32[]{:S(2)}) %collective-permute-start.1) | collective-permute-done | bytes 12320 | tf_op jit(solution)/shard_map/ppermute | solution.py:398
  85.5 0.2 fusion.1
  85.9 0.7 reshape.89
  86.6 8.6 %all-to-all-start.3 = ((bf16[32,2,192]{2,1,0:T(2,128)(2,1)}), bf16[32,2,192]{2,1,0:T(2,128)(2,1)S(1)}, u32[]{:S(2)}, u32[]{:S(2)}) async-start(bf16[32,2,192]{2,1,0:T(2,128)(2,1)} %reshape.89), calls=%async_computation.3 | async-start | bytes 65536 | tf_op jit(solution)/shard_map/all_to_all | solution.py:306
  95.2 0.2 fusion.3
  95.4 12.5 %all-to-all-done.3 = bf16[32,2,192]{2,1,0:T(2,128)(2,1)S(1)} async-done(((bf16[32,2,192]{2,1,0:T(2,128)(2,1)}), bf16[32,2,192]{2,1,0:T(2,128)(2,1)S(1)}, u32[]{:S(2)}, u32[]{:S(2)}) %all-to-all-start.3) | async-done | bytes 24608 | tf_op jit(solution)/shard_map/all_to_all | solution.py:306
  108.1 0.3 fusion
  108.7 0.7 copy.39
  109.4 5.3 %all-to-all-start.4 = ((bf16[64,8,96]{2,1,0:T(8,128)(2,1)}), bf16[64,8,96]{2,1,0:T(8,128)(2,1)S(1)}, u32[]{:S(2)}, u32[]{:S(2)}) async-start(bf16[64,8,96]{2,1,0:T(8,128)(2,1)} %copy.39), calls=%async_computation.4 | async-start | bytes 262144 | tf_op jit(solution)/shard_map/all_to_all | solution.py:306
  115.2 14.1 %all-to-all-done.4 = bf16[64,8,96]{2,1,0:T(8,128)(2,1)S(1)} async-done(((bf16[64,8,96]{2,1,0:T(8,128)(2,1)}), bf16[64,8,96]{2,1,0:T(8,128)(2,1)S(1)}, u32[]{:S(2)}, u32[]{:S(2)}) %all-to-all-start.4) | async-done | bytes 98336 | tf_op jit(solution)/shard_map/all_to_all | solution.py:306
  129.3 0.8 reshape.91
  130.1 5.9 %all-to-all-start.5 = ((bf16[64,2,192]{2,1,0:T(2,128)(2,1)}), bf16[64,2,192]{2,1,0:T(2,128)(2,1)S(1)}, u32[]{:S(2)}, u32[]{:S(2)}) async-start(bf16[64,2,192]{2,1,0:T(2,128)(2,1)} %reshape.91), calls=%async_computation.5 | async-start | bytes 131072 | tf_op jit(solution)/shard_map/all_to_all | solution.py:306
  136.0 0.2 add_convert_fusion
  136.5 13.0 %all-to-all-done.5 = bf16[64,2,192]{2,1,0:T(2,128)(2,1)S(1)} async-done(((bf16[64,2,192]{2,1,0:T(2,128)(2,1)}), bf16[64,2,192]{2,1,0:T(2,128)(2,1)S(1)}, u32[]{:S(2)}, u32[]{:S(2)}) %all-to-all-start.5) | async-done | bytes 49184 | tf_op jit(solution)/shard_map/all_to_all | solution.py:306
  149.9 0.3 fusion.32
  150.2 0.8 reshape.93
  151.0 4.8 %all-to-all-start.6 = ((bf16[64,2,192]{2,1,0:T(2,128)(2,1)}), bf16[64,2,192]{2,1,0:T(2,128)(2,1)S(1)}, u32[]{:S(2)}, u32[]{:S(2)}) async-start(bf16[64,2,192]{2,1,0:T(2,128)(2,1)} %reshape.93), calls=%async_computation.6 | async-start | bytes 131072 | tf_op jit(solution)/shard_map/all_to_all | solution.py:306
  155.8 0.2 convolution_add_fusion.5
  156.0 13.3 %all-to-all-done.6 = bf16[64,2,192]{2,1,0:T(2,128)(2,1)S(1)} async-done(((bf16[64,2,192]{2,1,0:T(2,128)(2,1)}), bf16[64,2,192]{2,1,0:T(2,128)(2,1)S(1)}, u32[]{:S(2)}, u32[]{:S(2)}) %all-to-all-start.6) | async-done | bytes 49184 | tf_op jit(solution)/shard_map/all_to_all | solution.py:306
  169.6 0.3 fusion.33
  170.0 0.7 broadcast_in_dim.19
  170.7 3.8 %all-to-all-start.7 = ((bf16[32,8,240]{2,1,0:T(8,128)(2,1)}), bf16[32,8,240]{2,1,0:T(8,128)(2,1)S(1)}, u32[]{:S(2)}, u32[]{:S(2)}) async-start(bf16[32,8,240]{2,1,0:T(8,128)(2,1)} %broadcast_in_dim.19), calls=%async_computation.7 | async-start | bytes 262144 | tf_op jit(solution)/shard_map/all_to_all | solution.py:306
  174.7 0.2 reshape.72
  175.0 0.3 convolution_add_fusion
  175.3 13.7 %all-to-all-done.7 = bf16[32,8,240]{2,1,0:T(8,128)(2,1)S(1)} async-done(((bf16[32,8,240]{2,1,0:T(8,128)(2,1)}), bf16[32,8,240]{2,1,0:T(8,128)(2,1)S(1)}, u32[]{:S(2)}, u32[]{:S(2)}) %all-to-all-start.7) | async-done | bytes 122912 | tf_op jit(solution)/shard_map/all_to_all | solution.py:306
  189.7 1.7 copy-done.3
  191.3 3.8 %far_levels.1 = (f32[8,768]{1,0:T(8,128)S(1)}, f32[3,8,384]{2,1,0:T(8,128)S(1)}) custom-call(bf16[8,1536]{1,0:T(8,128)(2,1)S(1)} %reshape.80.front5_ref, bf16[8,768]{1,0:T(8,128)(2,1)S(1)} %reshape.81.z4_ref, bf16[3,8,384]{2,1,0:T(8,128)(2,1)S(1)} %reshape.83.z_ref, bf16[768,1536]{1,0:T(8,128)(2,1)S(1)} %copy-done.3, bf16[384,1408]{1,0:T(8,128)(2,1)S(1)} %copy-done.2), custom_call_target="tpu_custom_call" | custom-call | tf_op jit(solution)/shard_map/far_levels/pallas_call | solution.py:286
  195.3 0.6 broadcast_in_dim.20
  195.9 12.5 %all-to-all-start.8 = ((bf16[8,8,96]{2,1,0:T(8,128)(2,1)}), bf16[8,8,96]{2,1,0:T(8,128)(2,1)S(1)}, u32[]{:S(2)}, u32[]{:S(2)}) async-start(bf16[8,8,96]{2,1,0:T(8,128)(2,1)} %broadcast_in_dim.20), calls=%async_computation.8 | async-start | bytes 32768 | tf_op jit(solution)/shard_map/all_to_all | solution.py:306
  208.5 0.7 concatenate.36
  209.2 3.8 %all-to-all-done.8 = bf16[8,8,96]{2,1,0:T(8,128)(2,1)S(1)} async-done(((bf16[8,8,96]{2,1,0:T(8,128)(2,1)}), bf16[8,8,96]{2,1,0:T(8,128)(2,1)S(1)}, u32[]{:S(2)}, u32[]{:S(2)}) %all-to-all-start.8) | async-done | bytes 12320 | tf_op jit(solution)/shard_map/all_to_all | solution.py:306
  213.1 0.8 convolution_subtract_fusion
  (77 shorter events, 3.9 us)
Async XLA Ops:
  7.2 167.8 %copy-start = (bf16[192,1536]{1,0:T(8,128)(2,1)S(1)}, bf16[192,1536]{1,0:T(8,128)(2,1)}, u32[]{:S(2)}) copy-start(bf16[192,1536]{1,0:T(8,128)(2,1)} %param.16) | copy-start | bytes 1769476
  7.2 37.5 %copy-start.11 = (f32[64,192]{1,0:T(8,128)S(1)}, f32[64,192]{1,0:T(8,128)}, u32[]{:S(2)}) copy-start(f32[64,192]{1,0:T(8,128)} %param.15) | copy-start | bytes 147460
  7.2 37.5 %copy-start.10 = (bf16[192,96]{1,0:T(8,128)(2,1)S(1)}, bf16[192,96]{1,0:T(8,128)(2,1)}, u32[]{:S(2)}) copy-start(bf16[192,96]{1,0:T(8,128)(2,1)} %param.17) | copy-start | bytes 110596
  7.2 66.5 %all-gather.5.cloned.1.call-start = ((), (), s32[]{:S(2)}) async-start(), calls=%async_computation.9 | async-start | bytes 1216512 | tf_op jit(solution)/shard_map/all_gather | solution.py:347
  12.5 157.5 %all-gather.7.cloned.1.call-start = ((), (), s32[]{:S(2)}) async-start(), calls=%async_computation.10 | async-start | bytes 2506752 | tf_op jit(solution)/shard_map/all_gather | solution.py:386
  13.3 7.1 %collective-permute-start = (f32[64,48]{1,0:T(8,128)S(1)}, f32[64,48]{1,0:T(8,128)S(1)}, u32[]{:S(2)}, u32[]{:S(2)}) collective-permute-start(f32[64,48]{1,0:T(8,128)S(1)} %copy.34), channel_id=1, source_target_pairs={{0,8},{8,0},{16,24},{24,16},{32,40},{40,32},{48,56},{56,48},{64,72... | collective-permute-start | bytes 36872 | tf_op jit(solution)/shard_map/ppermute | solution.py:334
  17.7 1.0 copy-start.4
  18.7 0.7 copy-start.7
  20.5 1.0 copy-start.5
  21.5 0.8 copy-start.6
  22.2 54.0 %copy-start.8 = (bf16[48,5952]{1,0:T(8,128)(2,1)S(1)}, bf16[48,5952]{1,0:T(8,128)(2,1)}, u32[]{:S(2)}) copy-start(bf16[48,5952]{1,0:T(8,128)(2,1)} %source.1) | copy-start | bytes 1714180
  44.6 50.6 %copy-start.9 = (bf16[48,6048]{1,0:T(8,128)(2,1)S(1)}, bf16[48,6048]{1,0:T(8,128)(2,1)}, u32[]{:S(2)}) copy-start(bf16[48,6048]{1,0:T(8,128)(2,1)} %param.18) | copy-start | bytes 1741828
  73.7 1.2 copy-start.1
  77.1 8.3 %collective-permute-start.1 = (bf16[8,768]{1,0:T(8,128)(2,1)S(1)}, bf16[8,768]{1,0:T(8,128)(2,1)S(1)}, u32[]{:S(2)}, u32[]{:S(2)}) collective-permute-start(bf16[8,768]{1,0:T(8,128)(2,1)S(1)} %get-tuple-element.17), channel_id=1, source_target_pairs={{0,96},{8,104},{16,112},{24,120},{32,64},{40,72},{48,80},{56,88},{... | collective-permute-start | bytes 36872 | tf_op jit(solution)/shard_map/ppermute | solution.py:398
  86.6 21.3 %all-to-all-start.3 = ((bf16[32,2,192]{2,1,0:T(2,128)(2,1)}), bf16[32,2,192]{2,1,0:T(2,128)(2,1)S(1)}, u32[]{:S(2)}, u32[]{:S(2)}) async-start(bf16[32,2,192]{2,1,0:T(2,128)(2,1)} %reshape.89), calls=%async_computation.3 | async-start | bytes 65536 | tf_op jit(solution)/shard_map/all_to_all | solution.py:306
  109.4 19.8 %all-to-all-start.4 = ((bf16[64,8,96]{2,1,0:T(8,128)(2,1)}), bf16[64,8,96]{2,1,0:T(8,128)(2,1)S(1)}, u32[]{:S(2)}, u32[]{:S(2)}) async-start(bf16[64,8,96]{2,1,0:T(8,128)(2,1)} %copy.39), calls=%async_computation.4 | async-start | bytes 262144 | tf_op jit(solution)/shard_map/all_to_all | solution.py:306
  130.1 19.4 %all-to-all-start.5 = ((bf16[64,2,192]{2,1,0:T(2,128)(2,1)}), bf16[64,2,192]{2,1,0:T(2,128)(2,1)S(1)}, u32[]{:S(2)}, u32[]{:S(2)}) async-start(bf16[64,2,192]{2,1,0:T(2,128)(2,1)} %reshape.91), calls=%async_computation.5 | async-start | bytes 131072 | tf_op jit(solution)/shard_map/all_to_all | solution.py:306
  151.0 18.3 %all-to-all-start.6 = ((bf16[64,2,192]{2,1,0:T(2,128)(2,1)}), bf16[64,2,192]{2,1,0:T(2,128)(2,1)S(1)}, u32[]{:S(2)}, u32[]{:S(2)}) async-start(bf16[64,2,192]{2,1,0:T(2,128)(2,1)} %reshape.93), calls=%async_computation.6 | async-start | bytes 131072 | tf_op jit(solution)/shard_map/all_to_all | solution.py:306
  156.0 33.6 %copy-start.2 = (bf16[384,1408]{1,0:T(8,128)(2,1)S(1)}, bf16[384,1408]{1,0:T(8,128)(2,1)}, u32[]{:S(2)}) copy-start(bf16[384,1408]{1,0:T(8,128)(2,1)} %all-gather.5.cloned.1.call-done.band_hbm) | copy-start | bytes 3244036
  170.7 18.3 %all-to-all-start.7 = ((bf16[32,8,240]{2,1,0:T(8,128)(2,1)}), bf16[32,8,240]{2,1,0:T(8,128)(2,1)S(1)}, u32[]{:S(2)}, u32[]{:S(2)}) async-start(bf16[32,8,240]{2,1,0:T(8,128)(2,1)} %broadcast_in_dim.19), calls=%async_computation.7 | async-start | bytes 262144 | tf_op jit(solution)/shard_map/all_to_all | solution.py:306
  189.6 1.7 copy-start.3
  195.9 17.2 %all-to-all-start.8 = ((bf16[8,8,96]{2,1,0:T(8,128)(2,1)}), bf16[8,8,96]{2,1,0:T(8,128)(2,1)S(1)}, u32[]{:S(2)}, u32[]{:S(2)}) async-start(bf16[8,8,96]{2,1,0:T(8,128)(2,1)} %broadcast_in_dim.20), calls=%async_computation.8 | async-start | bytes 32768 | tf_op jit(solution)/shard_map/all_to_all | solution.py:306
Sparse Core Ops, SparseCore 0:
  12.6 50.7 all-gather.4
  77.1 63.9 all-gather.6

commit v5 on v4

--- a/solution.py
+++ b/solution.py
@@ -75,7 +75,7 @@
         ],
         compiler_params=pltpu.CompilerParams(vmem_limit_bytes=16 << 20),
         name="prepare",
-    )(disp, stiffness)
+    )(resident(disp), resident(stiffness))
 
 
 def element_kernel(shared_ref, modulus_hbm, conn_hbm, inner_table_ref, kron_ref, pieces_ref, sep_ref,
@@ -183,7 +183,7 @@
         ],
         compiler_params=pltpu.CompilerParams(vmem_limit_bytes=48 << 20),
         name="elements",
-    )(shared, modulus, connectivity, table, kron)
+    )(shared, resident(modulus), resident(connectivity), table, kron)
 
 
 def fetch_leaves(source, begin, target, semaphores):
@@ -196,19 +196,8 @@
     ]
 
 
-def crop_kernel(source, target, semaphore):
-    fetch(source.at[:, :target.shape[1]], target, semaphore).wait()
-
-
-def crop(array, columns):
-    return pl.pallas_call(
-        crop_kernel,
-        in_specs=[pl.BlockSpec(memory_space=pltpu.HBM)],
-        out_specs=pl.BlockSpec(memory_space=pltpu.HBM),
-        out_shape=jax.ShapeDtypeStruct((array.shape[0], columns), array.dtype),
-        scratch_shapes=[pltpu.SemaphoreType.DMA],
-        name="crop",
-    )(array)
+def resident(array):
+    return pltpu.with_memory_space_constraint(array, pltpu.HBM)
 
 
 def near_kernel(terms_ref, band_hbm, q_ref, part_ref, band_ref, last_ref, band_sem, last_sem):
@@ -255,43 +244,44 @@
         ),
         compiler_params=pltpu.CompilerParams(vmem_limit_bytes=16 << 20),
         name="near_levels",
-    )(terms, bands)
-
-
-def far_kernel(front5_ref, z4_ref, z_ref, ring_hbm, band_hbm, x4_ref, x_ref, ring_ref, band_ref,
-               upper_sem, lower_sem, band_sem):
-    half = band_ref.shape[0] // 2
+    )(terms, resident(bands))
+
+
+def far_kernel(front5_ref, z4_ref, z_ref, ring_hbm, near_ref, x4_ref, x_ref, ring_ref,
+               upper_sem, lower_sem):
+    half = near_ref.shape[0] // 2
+    height = near_ref.shape[0] // len(ZIGZAG)
     middle = ring_ref.shape[0] // 2
     upper = fetch(ring_hbm.at[:middle], ring_ref.at[:middle], upper_sem)
     lower = fetch(ring_hbm.at[middle:], ring_ref.at[middle:], lower_sem)
-    band_copies = fetch_leaves(band_hbm, 0, band_ref, band_sem)
     upper.wait()
     first = rows_dot(front5_ref[...], ring_ref[:middle])
     lower.wait()
     x4 = z4_ref[...].astype(F32) - jnp.concatenate([first, rows_dot(front5_ref[...], ring_ref[middle:])], 1)
     x4_ref[...] = x4
-    for copy in band_copies:
-        copy.wait()
-    x3 = z_ref[2].astype(F32) - rows_dot(x4.astype(BF), band_ref[:, 3 * half:7 * half])
+    places = [ZIGZAG.index(leaf) * height for leaf in range(len(ZIGZAG))]
+
+    def near_rows(first, last, begin, end):
+        return jnp.concatenate([near_ref[at:at + height, begin:end] for at in places[first:last]], 0)
+
+    x3 = z_ref[2].astype(F32) - rows_dot(x4.astype(BF), near_rows(0, 8, 3 * half, 7 * half))
     x_ref[2] = x3
-    x2 = z_ref[1].astype(F32) - rows_dot(x3.astype(BF), band_ref[:, half:3 * half])
+    x2 = z_ref[1].astype(F32) - rows_dot(x3.astype(BF), near_rows(0, 8, half, 3 * half))
     x_ref[1] = x2
     low = x2.astype(BF)
     x_ref[0] = z_ref[0].astype(F32) - jnp.concatenate(
-        [rows_dot(low[:, :half], band_ref[:half, :half]), rows_dot(low[:, half:], band_ref[half:, :half])], 1)
+        [rows_dot(low[:, :half], near_rows(0, 4, 0, half)), rows_dot(low[:, half:], near_rows(4, 8, 0, half))], 1)
 
 
 def far_levels(front5, z4, z_near, ring_band, bands):
     whole = pl.BlockSpec(memory_space=pltpu.VMEM)
     return pl.pallas_call(
         far_kernel,
-        in_specs=[whole, whole, whole] + [pl.BlockSpec(memory_space=pltpu.HBM)] * 2,
+        in_specs=[whole, whole, whole, pl.BlockSpec(memory_space=pltpu.HBM), whole],
         scratch_shapes=[
             pltpu.VMEM(ring_band.shape, BF),
-            pltpu.VMEM(bands.shape, BF),
-            pltpu.SemaphoreType.DMA,
-            pltpu.SemaphoreType.DMA,
-            pltpu.SemaphoreType.DMA((len(ZIGZAG),)),
+            pltpu.SemaphoreType.DMA,
+            pltpu.SemaphoreType.DMA,
         ],
         out_shape=(
             jax.ShapeDtypeStruct(z4.shape, F32),
@@ -299,7 +289,7 @@
         ),
         compiler_params=pltpu.CompilerParams(vmem_limit_bytes=24 << 20),
         name="far_levels",
-    )(front5, z4, z_near, ring_band, bands)
+    )(front5, z4, z_near, resident(ring_band), bands)
 
 
 def exchange(value, axis, groups=None):
@@ -344,7 +334,7 @@
     ring_groups = group_lists(leaves, 4)
     spot = leaf_index % near
     zigzag_groups = [[base + at for at in ZIGZAG] for base in range(0, leaves, near)]
-    near_bands = lax.all_gather(crop(coupling, near_cols), "leaf", axis_index_groups=zigzag_groups)
+    near_bands = lax.all_gather(coupling[:, :near_cols], "leaf", axis_index_groups=zigzag_groups)
 
     def own_coupling(height):
         start = rows * (2**height - 4)

time: 222 us -> 214 us (0.964)
  local copies, waits for them, and re-layouts: 15.8 us -> 11.2 us
  Pallas kernels: 19.2 us -> 15.3 us
    unnamed x31 -> x19, local copies, waits for them, and re-layouts: 9.83 us -> 3.53 us
    pallas_call x2 -> x1, Pallas kernels: 9.01 us -> 2.92 us  [far_levels(): pl.pallas_call(far_kernel, in_specs=[whole, whole, whole, pl.BlockSpec(me...]
  transfers between devices with their start and end apart: 10 -> 10, of which waited for: 7 -> 7; matrix products, arithmetic and copies ran while one was open for 4% -> 5% of each run, Pallas kernels for 4% -> 5%
where the time goes in v5:
time: 214 us; the launch traced here: 213 us
  waiting for transfers between devices  75.4 us (35%)
  starting transfers between devices  48.6 us (23%)
  blocking collectives  44.1 us (21%)
  Pallas kernels  15.3 us (7%)
  between operations  14.6 us (7%)
  local copies, waits for them, and re-layouts  11.2 us (5%)
  matrix products  3.26 us (2%)
    all_to_all x6, waiting for transfers between devices, exchange(): lax.all_to_all(value, axis, 0, 0, axis_index_groups=groups, tiled=True)  70.2 us
    all_to_all x3, blocking collectives, exchange(): lax.all_to_all(value, axis, 0, 0, axis_index_groups=groups, tiled=True)  44.1 us
    all_to_all x6, starting transfers between devices, exchange(): lax.all_to_all(value, axis, 0, 0, axis_index_groups=groups, tiled=True)  41.1 us
    pallas_call x1, Pallas kernels, assemble(): pl.pallas_call(element_kernel, in_specs=[whole, far, far, whole, whole],...  8.74 us
    ppermute x1, waiting for transfers between devices, body(): q4 = part4.astype(F32) + lax.ppermute(part4, 'leaf', across).astype(F32)  5.21 us
    ppermute x1, starting transfers between devices, body(): partner = lax.ppermute(separator_disp, 'leaf', pairs)  4.36 us
  transfers between devices with their start and end apart: 10, of which 7 were waited for; matrix products, arithmetic and copies ran while one was open for 5% of the time, Pallas kernels for 5%

profile of v5, /device:TPU:1, one launch (start us, length us, event | category | flops | bytes accessed | tf_op | source)
XLA Modules:
  0.0 213.1 jit_solution(4362472410150470404)
XLA Ops:
  7.2 1.6 slice.80
  8.9 0.8 copy.34
  9.8 4.4 %collective-permute-start = (f32[64,48]{1,0:T(8,128)S(1)}, f32[64,48]{1,0:T(8,128)S(1)}, u32[]{:S(2)}, u32[]{:S(2)}) collective-permute-start(f32[64,48]{1,0:T(8,128)S(1)} %copy.34), channel_id=1, source_target_pairs={{0,8},{8,0},{16,24},{24,16},{32,40},{40,32},{48,56},{56,48},{64,72... | collective-permute-start | bytes 36872 | tf_op jit(solution)/shard_map/ppermute | solution.py:324
  14.1 1.5 prepare.1
  15.8 8.7 %elements.1 = (bf16[8,64,192]{2,1,0:T(8,128)(2,1)S(1)}, f32[64,96]{1,0:T(8,128)S(1)}) custom-call(f32[64,96]{1,0:T(8,128)S(1)} %maximum_select_fusion.shared_ref, f32[64,1024]{1,0:T(8,128)} %modulus_hbm.1, s32[8,1024]{1,0:T(8,128)} %conn_hbm.1, bf16[192,512]{1,0:T(8,128)(2,1)S(1)} %get-tuple-element.13.inner_table_ref, ...), custom_call_target="tpu_custom_call" | custom-call | tf_op jit(solution)/shard_map/elements/pallas_call | solution.py:166
  24.5 15.5 %all_to_all.45 = bf16[8,64,192]{2,1,0:T(8,128)(2,1)S(1)} all-to-all(bf16[8,64,192]{2,1,0:T(8,128)(2,1)S(1)} %get-tuple-element.15), channel_id=1, replica_groups=mesh['leaf'=64,'front'=8] {'front'}, dimensions={0} | all-to-all | bytes 393216 | tf_op jit(solution)/shard_map/all_to_all | solution.py:296
  40.4 10.7 %all_to_all.46 = bf16[8,72,192]{2,1,0:T(8,128)(2,1)S(1)} all-to-all(bf16[8,72,192]{2,1,0:T(8,128)(2,1)S(1)} %maximum_maximum_fusion), channel_id=1, replica_groups=mesh['leaf'=64,'front'=8] {'front'}, dimensions={0} | all-to-all | bytes 442368 | tf_op jit(solution)/shard_map/all_to_all | solution.py:296
  51.2 17.9 %all_to_all.47.terms_ref = bf16[8,8,96]{2,1,0:T(8,128)(2,1)S(1)} all-to-all(bf16[8,8,96]{2,1,0:T(8,128)(2,1)S(1)} %broadcast_in_dim.15), channel_id=1, replica_groups={{0,8,16,24,32,40,48,56},{64,72,80,88,96,104,112,120},{128,136,144,152,1..., dimensions={0} | all-to-all | bytes 24576 | tf_op jit(solution)/shard_map/all_to_all | solution.py:296
  69.1 2.2 %near_levels.1 = (f32[3,8,384]{2,1,0:T(8,128)S(1)}, bf16[8,768]{1,0:T(8,128)(2,1)S(1)}) custom-call(bf16[8,8,96]{2,1,0:T(8,128)(2,1)S(1)} %all_to_all.47.terms_ref, bf16[384,1408]{1,0:T(8,128)(2,1)} %all-gather.5.cloned.1.call-done.band_hbm.near_ref), custom_call_target="tpu_custom_call" | custom-call | tf_op jit(solution)/shard_map/near_levels/pallas_call | solution.py:232
  71.3 0.8 slice.94
  72.2 3.1 %collective-permute-start.1 = (bf16[8,768]{1,0:T(8,128)(2,1)S(1)}, bf16[8,768]{1,0:T(8,128)(2,1)S(1)}, u32[]{:S(2)}, u32[]{:S(2)}) collective-permute-start(bf16[8,768]{1,0:T(8,128)(2,1)S(1)} %get-tuple-element.17), channel_id=1, source_target_pairs={{0,96},{8,104},{16,112},{24,120},{32,64},{40,72},{48,80},{56,88},{... | collective-permute-start | bytes 36872 | tf_op jit(solution)/shard_map/ppermute | solution.py:388
  75.4 5.2 %collective-permute-done.1 = bf16[8,768]{1,0:T(8,128)(2,1)S(1)} collective-permute-done((bf16[8,768]{1,0:T(8,128)(2,1)S(1)}, bf16[8,768]{1,0:T(8,128)(2,1)S(1)}, u32[]{:S(2)}, u32[]{:S(2)}) %collective-permute-start.1) | collective-permute-done | bytes 12320 | tf_op jit(solution)/shard_map/ppermute | solution.py:388
  80.6 0.2 fusion.1
  81.0 0.7 reshape.89
  81.7 8.6 %all-to-all-start.3 = ((bf16[32,2,192]{2,1,0:T(2,128)(2,1)}), bf16[32,2,192]{2,1,0:T(2,128)(2,1)S(1)}, u32[]{:S(2)}, u32[]{:S(2)}) async-start(bf16[32,2,192]{2,1,0:T(2,128)(2,1)} %reshape.89), calls=%async_computation.3 | async-start | bytes 65536 | tf_op jit(solution)/shard_map/all_to_all | solution.py:296
  90.4 0.2 fusion.3
  90.6 12.5 %all-to-all-done.3 = bf16[32,2,192]{2,1,0:T(2,128)(2,1)S(1)} async-done(((bf16[32,2,192]{2,1,0:T(2,128)(2,1)}), bf16[32,2,192]{2,1,0:T(2,128)(2,1)S(1)}, u32[]{:S(2)}, u32[]{:S(2)}) %all-to-all-start.3) | async-done | bytes 24608 | tf_op jit(solution)/shard_map/all_to_all | solution.py:296
  103.2 0.3 fusion
  103.4 0.2 reshape.75
  103.7 0.7 copy.39
  104.5 5.4 %all-to-all-start.4 = ((bf16[64,8,96]{2,1,0:T(8,128)(2,1)}), bf16[64,8,96]{2,1,0:T(8,128)(2,1)S(1)}, u32[]{:S(2)}, u32[]{:S(2)}) async-start(bf16[64,8,96]{2,1,0:T(8,128)(2,1)} %copy.39), calls=%async_computation.4 | async-start | bytes 262144 | tf_op jit(solution)/shard_map/all_to_all | solution.py:296
  109.9 0.2 fusion.2
  110.1 0.2 fusion.4
  110.3 13.9 %all-to-all-done.4 = bf16[64,8,96]{2,1,0:T(8,128)(2,1)S(1)} async-done(((bf16[64,8,96]{2,1,0:T(8,128)(2,1)}), bf16[64,8,96]{2,1,0:T(8,128)(2,1)S(1)}, u32[]{:S(2)}, u32[]{:S(2)}) %all-to-all-start.4) | async-done | bytes 98336 | tf_op jit(solution)/shard_map/all_to_all | solution.py:296
  124.3 0.8 reshape.91
  125.1 6.1 %all-to-all-start.5 = ((bf16[64,2,192]{2,1,0:T(2,128)(2,1)}), bf16[64,2,192]{2,1,0:T(2,128)(2,1)S(1)}, u32[]{:S(2)}, u32[]{:S(2)}) async-start(bf16[64,2,192]{2,1,0:T(2,128)(2,1)} %reshape.91), calls=%async_computation.5 | async-start | bytes 131072 | tf_op jit(solution)/shard_map/all_to_all | solution.py:296
  131.1 0.2 add_convert_fusion
  131.6 13.0 %all-to-all-done.5 = bf16[64,2,192]{2,1,0:T(2,128)(2,1)S(1)} async-done(((bf16[64,2,192]{2,1,0:T(2,128)(2,1)}), bf16[64,2,192]{2,1,0:T(2,128)(2,1)S(1)}, u32[]{:S(2)}, u32[]{:S(2)}) %all-to-all-start.5) | async-done | bytes 49184 | tf_op jit(solution)/shard_map/all_to_all | solution.py:296
  144.8 0.2 reshape.77
  145.0 0.3 fusion.32
  145.3 0.8 reshape.93
  146.1 4.9 %all-to-all-start.6 = ((bf16[64,2,192]{2,1,0:T(2,128)(2,1)}), bf16[64,2,192]{2,1,0:T(2,128)(2,1)S(1)}, u32[]{:S(2)}, u32[]{:S(2)}) async-start(bf16[64,2,192]{2,1,0:T(2,128)(2,1)} %reshape.93), calls=%async_computation.6 | async-start | bytes 131072 | tf_op jit(solution)/shard_map/all_to_all | solution.py:296
  151.0 0.2 convolution_add_fusion.5
  151.2 13.3 %all-to-all-done.6 = bf16[64,2,192]{2,1,0:T(2,128)(2,1)S(1)} async-done(((bf16[64,2,192]{2,1,0:T(2,128)(2,1)}), bf16[64,2,192]{2,1,0:T(2,128)(2,1)S(1)}, u32[]{:S(2)}, u32[]{:S(2)}) %all-to-all-start.6) | async-done | bytes 49184 | tf_op jit(solution)/shard_map/all_to_all | solution.py:296
  164.7 0.2 reshape.78
  164.9 0.3 fusion.33
  165.2 0.7 broadcast_in_dim.19
  165.9 3.8 %all-to-all-start.7 = ((bf16[32,8,240]{2,1,0:T(8,128)(2,1)}), bf16[32,8,240]{2,1,0:T(8,128)(2,1)S(1)}, u32[]{:S(2)}, u32[]{:S(2)}) async-start(bf16[32,8,240]{2,1,0:T(8,128)(2,1)} %broadcast_in_dim.19), calls=%async_computation.7 | async-start | bytes 262144 | tf_op jit(solution)/shard_map/all_to_all | solution.py:296
  169.8 0.2 copy.37
  169.9 0.2 reshape.72
  170.2 0.3 convolution_add_fusion
  170.5 13.7 %all-to-all-done.7 = bf16[32,8,240]{2,1,0:T(8,128)(2,1)S(1)} async-done(((bf16[32,8,240]{2,1,0:T(8,128)(2,1)}), bf16[32,8,240]{2,1,0:T(8,128)(2,1)S(1)}, u32[]{:S(2)}, u32[]{:S(2)}) %all-to-all-start.7) | async-done | bytes 122912 | tf_op jit(solution)/shard_map/all_to_all | solution.py:296
  184.8 2.9 %far_levels.1 = (f32[8,768]{1,0:T(8,128)S(1)}, f32[3,8,384]{2,1,0:T(8,128)S(1)}) custom-call(bf16[8,1536]{1,0:T(8,128)(2,1)S(1)} %reshape.80.front5_ref, bf16[8,768]{1,0:T(8,128)(2,1)S(1)} %reshape.81.z4_ref, bf16[3,8,384]{2,1,0:T(8,128)(2,1)S(1)} %reshape.83.z_ref, bf16[768,1536]{1,0:T(8,128)(2,1)} %all-gather.7.cloned.1.call-done.ring_hbm, ...), custom_call_target="tpu_custom_call" | custom-call | tf_op jit(solution)/shard_map/far_levels/pallas_call | solution.py:278
  187.9 0.6 broadcast_in_dim.20
  188.5 12.2 %all-to-all-start.8 = ((bf16[8,8,96]{2,1,0:T(8,128)(2,1)}), bf16[8,8,96]{2,1,0:T(8,128)(2,1)S(1)}, u32[]{:S(2)}, u32[]{:S(2)}) async-start(bf16[8,8,96]{2,1,0:T(8,128)(2,1)} %broadcast_in_dim.20), calls=%async_computation.8 | async-start | bytes 32768 | tf_op jit(solution)/shard_map/all_to_all | solution.py:296
  200.9 0.7 concatenate.36
  201.6 3.8 %all-to-all-done.8 = bf16[8,8,96]{2,1,0:T(8,128)(2,1)S(1)} async-done(((bf16[8,8,96]{2,1,0:T(8,128)(2,1)}), bf16[8,8,96]{2,1,0:T(8,128)(2,1)S(1)}, u32[]{:S(2)}, u32[]{:S(2)}) %all-to-all-start.8) | async-done | bytes 12320 | tf_op jit(solution)/shard_map/all_to_all | solution.py:296
  205.4 0.8 convolution_subtract_fusion
  (65 shorter events, 2.8 us)
Async XLA Ops:
  7.2 163.0 %copy-start = (bf16[192,1536]{1,0:T(8,128)(2,1)S(1)}, bf16[192,1536]{1,0:T(8,128)(2,1)}, u32[]{:S(2)}) copy-start(bf16[192,1536]{1,0:T(8,128)(2,1)} %param.16) | copy-start | bytes 1769476
  7.2 32.9 %copy-start.5 = (f32[64,192]{1,0:T(8,128)S(1)}, f32[64,192]{1,0:T(8,128)}, u32[]{:S(2)}) copy-start(f32[64,192]{1,0:T(8,128)} %param.15) | copy-start | bytes 147460
  7.2 33.0 %copy-start.4 = (bf16[192,96]{1,0:T(8,128)(2,1)S(1)}, bf16[192,96]{1,0:T(8,128)(2,1)}, u32[]{:S(2)}) copy-start(bf16[192,96]{1,0:T(8,128)(2,1)} %param.17) | copy-start | bytes 110596
  7.2 61.9 %all-gather.5.cloned.1.call-start = ((), (), s32[]{:S(2)}) async-start(), calls=%async_computation.9 | async-start | bytes 1216512 | tf_op jit(solution)/shard_map/all_gather | solution.py:337
  8.9 156.3 %all-gather.7.cloned.1.call-start = ((), (), s32[]{:S(2)}) async-start(), calls=%async_computation.10 | async-start | bytes 2506752 | tf_op jit(solution)/shard_map/all_gather | solution.py:376
  9.8 5.9 %collective-permute-start = (f32[64,48]{1,0:T(8,128)S(1)}, f32[64,48]{1,0:T(8,128)S(1)}, u32[]{:S(2)}, u32[]{:S(2)}) collective-permute-start(f32[64,48]{1,0:T(8,128)S(1)} %copy.34), channel_id=1, source_target_pairs={{0,8},{8,0},{16,24},{24,16},{32,40},{40,32},{48,56},{56,48},{64,72... | collective-permute-start | bytes 36872 | tf_op jit(solution)/shard_map/ppermute | solution.py:324
  15.7 55.6 %copy-start.2 = (bf16[48,5952]{1,0:T(8,128)(2,1)S(1)}, bf16[48,5952]{1,0:T(8,128)(2,1)}, u32[]{:S(2)}) copy-start(bf16[48,5952]{1,0:T(8,128)(2,1)} %param.19) | copy-start | bytes 1714180
  40.1 50.3 %copy-start.3 = (bf16[48,6048]{1,0:T(8,128)(2,1)S(1)}, bf16[48,6048]{1,0:T(8,128)(2,1)}, u32[]{:S(2)}) copy-start(bf16[48,6048]{1,0:T(8,128)(2,1)} %param.18) | copy-start | bytes 1741828
  72.2 8.3 %collective-permute-start.1 = (bf16[8,768]{1,0:T(8,128)(2,1)S(1)}, bf16[8,768]{1,0:T(8,128)(2,1)S(1)}, u32[]{:S(2)}, u32[]{:S(2)}) collective-permute-start(bf16[8,768]{1,0:T(8,128)(2,1)S(1)} %get-tuple-element.17), channel_id=1, source_target_pairs={{0,96},{8,104},{16,112},{24,120},{32,64},{40,72},{48,80},{56,88},{... | collective-permute-start | bytes 36872 | tf_op jit(solution)/shard_map/ppermute | solution.py:388
  81.7 21.3 %all-to-all-start.3 = ((bf16[32,2,192]{2,1,0:T(2,128)(2,1)}), bf16[32,2,192]{2,1,0:T(2,128)(2,1)S(1)}, u32[]{:S(2)}, u32[]{:S(2)}) async-start(bf16[32,2,192]{2,1,0:T(2,128)(2,1)} %reshape.89), calls=%async_computation.3 | async-start | bytes 65536 | tf_op jit(solution)/shard_map/all_to_all | solution.py:296
  104.5 19.7 %all-to-all-start.4 = ((bf16[64,8,96]{2,1,0:T(8,128)(2,1)}), bf16[64,8,96]{2,1,0:T(8,128)(2,1)S(1)}, u32[]{:S(2)}, u32[]{:S(2)}) async-start(bf16[64,8,96]{2,1,0:T(8,128)(2,1)} %copy.39), calls=%async_computation.4 | async-start | bytes 262144 | tf_op jit(solution)/shard_map/all_to_all | solution.py:296
  125.1 19.5 %all-to-all-start.5 = ((bf16[64,2,192]{2,1,0:T(2,128)(2,1)}), bf16[64,2,192]{2,1,0:T(2,128)(2,1)S(1)}, u32[]{:S(2)}, u32[]{:S(2)}) async-start(bf16[64,2,192]{2,1,0:T(2,128)(2,1)} %reshape.91), calls=%async_computation.5 | async-start | bytes 131072 | tf_op jit(solution)/shard_map/all_to_all | solution.py:296
  146.1 18.5 %all-to-all-start.6 = ((bf16[64,2,192]{2,1,0:T(2,128)(2,1)}), bf16[64,2,192]{2,1,0:T(2,128)(2,1)S(1)}, u32[]{:S(2)}, u32[]{:S(2)}) async-start(bf16[64,2,192]{2,1,0:T(2,128)(2,1)} %reshape.93), calls=%async_computation.6 | async-start | bytes 131072 | tf_op jit(solution)/shard_map/all_to_all | solution.py:296
  151.2 33.6 %copy-start.1 = (bf16[384,1408]{1,0:T(8,128)(2,1)S(1)}, bf16[384,1408]{1,0:T(8,128)(2,1)}, u32[]{:S(2)}) copy-start(bf16[384,1408]{1,0:T(8,128)(2,1)} %all-gather.5.cloned.1.call-done.band_hbm.near_ref) | copy-start | bytes 3244036
  165.9 18.3 %all-to-all-start.7 = ((bf16[32,8,240]{2,1,0:T(8,128)(2,1)}), bf16[32,8,240]{2,1,0:T(8,128)(2,1)S(1)}, u32[]{:S(2)}, u32[]{:S(2)}) async-start(bf16[32,8,240]{2,1,0:T(8,128)(2,1)} %broadcast_in_dim.19), calls=%async_computation.7 | async-start | bytes 262144 | tf_op jit(solution)/shard_map/all_to_all | solution.py:296
  188.5 16.9 %all-to-all-start.8 = ((bf16[8,8,96]{2,1,0:T(8,128)(2,1)}), bf16[8,8,96]{2,1,0:T(8,128)(2,1)S(1)}, u32[]{:S(2)}, u32[]{:S(2)}) async-start(bf16[8,8,96]{2,1,0:T(8,128)(2,1)} %broadcast_in_dim.20), calls=%async_computation.8 | async-start | bytes 32768 | tf_op jit(solution)/shard_map/all_to_all | solution.py:296
Sparse Core Ops, SparseCore 0:
  10.1 51.3 all-gather.4
  72.2 64.0 all-gather.6

commit v6 on v5

--- a/solution.py
+++ b/solution.py
@@ -322,6 +322,8 @@
     own_samples = samples // fronts
     pairs = [(source, source ^ 1) for source in range(leaves)]
     partner = lax.ppermute(separator_disp, "leaf", pairs)
+    start5 = rows * (2**5 - 4)
+    partner, own_band5 = lax.optimization_barrier((partner, coupling[:, start5:2 * start5 + 4 * rows]))
     upper_leaf = leaf_index % 2 == 1
     shared = jnp.where(
         upper_leaf,
@@ -372,9 +374,8 @@
     near_terms = exchange(jnp.broadcast_to(term.astype(BF)[None], (near,) + term.shape), "leaf", near_groups)
     bands = near_bands.reshape(near * rows, near_cols)
     near_q, part4 = near_levels(near_terms, bands)
-    start5 = rows * (2**5 - 4)
     ring_band = lax.all_gather(
-        lax.optimization_barrier((coupling, part4))[0][:, start5:2 * start5 + 4 * rows], "leaf",
+        lax.optimization_barrier((own_band5, part4))[0], "leaf",
         axis_index_groups=ring_groups,
     ).reshape(16 * rows, 32 * rows)
     q1, q2, q3 = near_q[0], near_q[1], near_q[2]

time: 214 us -> 214 us (level)
  no operation moved by 1% of the time
where the time goes in v6:
time: 214 us; the launch traced here: 213 us
  waiting for transfers between devices  75.3 us (35%)
  starting transfers between devices  49.3 us (23%)
  blocking collectives  42.7 us (20%)
  Pallas kernels  15.3 us (7%)
  between operations  14.6 us (7%)
  local copies, waits for them, and re-layouts  12.1 us (6%)
  matrix products  3.27 us (2%)
    all_to_all x6, waiting for transfers between devices, exchange(): lax.all_to_all(value, axis, 0, 0, axis_index_groups=groups, tiled=True)  70.4 us
    all_to_all x3, blocking collectives, exchange(): lax.all_to_all(value, axis, 0, 0, axis_index_groups=groups, tiled=True)  42.7 us
    all_to_all x6, starting transfers between devices, exchange(): lax.all_to_all(value, axis, 0, 0, axis_index_groups=groups, tiled=True)  41.5 us
    pallas_call x1, Pallas kernels, assemble(): pl.pallas_call(element_kernel, in_specs=[whole, far, far, whole, whole],...  8.68 us
    ppermute x1, waiting for transfers between devices, body(): q4 = part4.astype(F32) + lax.ppermute(part4, 'leaf', across).astype(F32)  4.89 us
    ppermute x1, starting transfers between devices, body(): partner = lax.ppermute(separator_disp, 'leaf', pairs)  4.36 us
  transfers between devices with their start and end apart: 10, of which 7 were waited for; matrix products, arithmetic and copies ran while one was open for 5% of the time, Pallas kernels for 5%

profile of v6, /device:TPU:1, one launch (start us, length us, event | category | flops | bytes accessed | tf_op | source)
XLA Modules:
  0.0 213.1 jit_solution(11968019230118835909)
XLA Ops:
  7.2 1.6 slice.79
  8.9 0.8 copy.34
  9.8 4.4 %collective-permute-start = (f32[64,48]{1,0:T(8,128)S(1)}, f32[64,48]{1,0:T(8,128)S(1)}, u32[]{:S(2)}, u32[]{:S(2)}) collective-permute-start(f32[64,48]{1,0:T(8,128)S(1)} %copy.34), channel_id=1, source_target_pairs={{0,8},{8,0},{16,24},{24,16},{32,40},{40,32},{48,56},{56,48},{64,72... | collective-permute-start | bytes 36872 | tf_op jit(solution)/shard_map/ppermute | solution.py:324
  14.1 1.7 slice.74
  15.8 1.5 prepare.1
  17.4 8.7 %elements.1 = (bf16[8,64,192]{2,1,0:T(8,128)(2,1)S(1)}, f32[64,96]{1,0:T(8,128)S(1)}) custom-call(f32[64,96]{1,0:T(8,128)S(1)} %maximum_select_fusion.shared_ref, f32[64,1024]{1,0:T(8,128)} %modulus_hbm.1, s32[8,1024]{1,0:T(8,128)} %conn_hbm.1, bf16[192,512]{1,0:T(8,128)(2,1)S(1)} %get-tuple-element.16.inner_table_ref, ...), custom_call_target="tpu_custom_call" | custom-call | tf_op jit(solution)/shard_map/elements/pallas_call | solution.py:166
  26.1 14.1 %all_to_all.45 = bf16[8,64,192]{2,1,0:T(8,128)(2,1)S(1)} all-to-all(bf16[8,64,192]{2,1,0:T(8,128)(2,1)S(1)} %get-tuple-element.18), channel_id=1, replica_groups=mesh['leaf'=64,'front'=8] {'front'}, dimensions={0} | all-to-all | bytes 393216 | tf_op jit(solution)/shard_map/all_to_all | solution.py:296
  40.6 10.7 %all_to_all.46 = bf16[8,72,192]{2,1,0:T(8,128)(2,1)S(1)} all-to-all(bf16[8,72,192]{2,1,0:T(8,128)(2,1)S(1)} %maximum_maximum_fusion), channel_id=1, replica_groups=mesh['leaf'=64,'front'=8] {'front'}, dimensions={0} | all-to-all | bytes 442368 | tf_op jit(solution)/shard_map/all_to_all | solution.py:296
  51.4 17.9 %all_to_all.47.terms_ref = bf16[8,8,96]{2,1,0:T(8,128)(2,1)S(1)} all-to-all(bf16[8,8,96]{2,1,0:T(8,128)(2,1)S(1)} %broadcast_in_dim.15), channel_id=1, replica_groups={{0,8,16,24,32,40,48,56},{64,72,80,88,96,104,112,120},{128,136,144,152,1..., dimensions={0} | all-to-all | bytes 24576 | tf_op jit(solution)/shard_map/all_to_all | solution.py:296
  69.2 2.2 %near_levels.1 = (f32[3,8,384]{2,1,0:T(8,128)S(1)}, bf16[8,768]{1,0:T(8,128)(2,1)S(1)}) custom-call(bf16[8,8,96]{2,1,0:T(8,128)(2,1)S(1)} %all_to_all.47.terms_ref, bf16[384,1408]{1,0:T(8,128)(2,1)} %all-gather.5.cloned.1.call-done.band_hbm.near_ref), custom_call_target="tpu_custom_call" | custom-call | tf_op jit(solution)/shard_map/near_levels/pallas_call | solution.py:232
  71.6 3.4 %collective-permute-start.1 = (bf16[8,768]{1,0:T(8,128)(2,1)S(1)}, bf16[8,768]{1,0:T(8,128)(2,1)S(1)}, u32[]{:S(2)}, u32[]{:S(2)}) collective-permute-start(bf16[8,768]{1,0:T(8,128)(2,1)S(1)} %get-tuple-element.20), channel_id=1, source_target_pairs={{0,96},{8,104},{16,112},{24,120},{32,64},{40,72},{48,80},{56,88},{... | collective-permute-start | bytes 36872 | tf_op jit(solution)/shard_map/ppermute | solution.py:389
  75.0 4.9 %collective-permute-done.1 = bf16[8,768]{1,0:T(8,128)(2,1)S(1)} collective-permute-done((bf16[8,768]{1,0:T(8,128)(2,1)S(1)}, bf16[8,768]{1,0:T(8,128)(2,1)S(1)}, u32[]{:S(2)}, u32[]{:S(2)}) %collective-permute-start.1) | collective-permute-done | bytes 12320 | tf_op jit(solution)/shard_map/ppermute | solution.py:389
  80.0 0.2 fusion.1
  80.3 0.7 reshape.89
  81.1 8.9 %all-to-all-start.3 = ((bf16[32,2,192]{2,1,0:T(2,128)(2,1)}), bf16[32,2,192]{2,1,0:T(2,128)(2,1)S(1)}, u32[]{:S(2)}, u32[]{:S(2)}) async-start(bf16[32,2,192]{2,1,0:T(2,128)(2,1)} %reshape.89), calls=%async_computation.3 | async-start | bytes 65536 | tf_op jit(solution)/shard_map/all_to_all | solution.py:296
  90.1 0.2 fusion.3
  90.3 12.5 %all-to-all-done.3 = bf16[32,2,192]{2,1,0:T(2,128)(2,1)S(1)} async-done(((bf16[32,2,192]{2,1,0:T(2,128)(2,1)}), bf16[32,2,192]{2,1,0:T(2,128)(2,1)S(1)}, u32[]{:S(2)}, u32[]{:S(2)}) %all-to-all-start.3) | async-done | bytes 24608 | tf_op jit(solution)/shard_map/all_to_all | solution.py:296
  102.9 0.3 fusion
  103.2 0.2 reshape.75
  103.5 0.7 copy.39
  104.3 5.3 %all-to-all-start.4 = ((bf16[64,8,96]{2,1,0:T(8,128)(2,1)}), bf16[64,8,96]{2,1,0:T(8,128)(2,1)S(1)}, u32[]{:S(2)}, u32[]{:S(2)}) async-start(bf16[64,8,96]{2,1,0:T(8,128)(2,1)} %copy.39), calls=%async_computation.4 | async-start | bytes 262144 | tf_op jit(solution)/shard_map/all_to_all | solution.py:296
  109.6 0.2 fusion.2
  109.8 0.2 fusion.4
  110.0 13.8 %all-to-all-done.4 = bf16[64,8,96]{2,1,0:T(8,128)(2,1)S(1)} async-done(((bf16[64,8,96]{2,1,0:T(8,128)(2,1)}), bf16[64,8,96]{2,1,0:T(8,128)(2,1)S(1)}, u32[]{:S(2)}, u32[]{:S(2)}) %all-to-all-start.4) | async-done | bytes 98336 | tf_op jit(solution)/shard_map/all_to_all | solution.py:296
  123.9 0.8 reshape.91
  124.7 6.2 %all-to-all-start.5 = ((bf16[64,2,192]{2,1,0:T(2,128)(2,1)}), bf16[64,2,192]{2,1,0:T(2,128)(2,1)S(1)}, u32[]{:S(2)}, u32[]{:S(2)}) async-start(bf16[64,2,192]{2,1,0:T(2,128)(2,1)} %reshape.91), calls=%async_computation.5 | async-start | bytes 131072 | tf_op jit(solution)/shard_map/all_to_all | solution.py:296
  130.8 0.2 add_convert_fusion
  131.3 13.2 %all-to-all-done.5 = bf16[64,2,192]{2,1,0:T(2,128)(2,1)S(1)} async-done(((bf16[64,2,192]{2,1,0:T(2,128)(2,1)}), bf16[64,2,192]{2,1,0:T(2,128)(2,1)S(1)}, u32[]{:S(2)}, u32[]{:S(2)}) %all-to-all-start.5) | async-done | bytes 49184 | tf_op jit(solution)/shard_map/all_to_all | solution.py:296
  144.6 0.2 reshape.77
  144.8 0.3 fusion.32
  145.1 0.8 reshape.93
  145.9 4.7 %all-to-all-start.6 = ((bf16[64,2,192]{2,1,0:T(2,128)(2,1)}), bf16[64,2,192]{2,1,0:T(2,128)(2,1)S(1)}, u32[]{:S(2)}, u32[]{:S(2)}) async-start(bf16[64,2,192]{2,1,0:T(2,128)(2,1)} %reshape.93), calls=%async_computation.6 | async-start | bytes 131072 | tf_op jit(solution)/shard_map/all_to_all | solution.py:296
  150.7 0.2 convolution_add_fusion.5
  150.9 13.3 %all-to-all-done.6 = bf16[64,2,192]{2,1,0:T(2,128)(2,1)S(1)} async-done(((bf16[64,2,192]{2,1,0:T(2,128)(2,1)}), bf16[64,2,192]{2,1,0:T(2,128)(2,1)S(1)}, u32[]{:S(2)}, u32[]{:S(2)}) %all-to-all-start.6) | async-done | bytes 49184 | tf_op jit(solution)/shard_map/all_to_all | solution.py:296
  164.4 0.2 reshape.78
  164.6 0.3 fusion.33
  164.9 0.7 broadcast_in_dim.19
  165.6 3.8 %all-to-all-start.7 = ((bf16[32,8,240]{2,1,0:T(8,128)(2,1)}), bf16[32,8,240]{2,1,0:T(8,128)(2,1)S(1)}, u32[]{:S(2)}, u32[]{:S(2)}) async-start(bf16[32,8,240]{2,1,0:T(8,128)(2,1)} %broadcast_in_dim.19), calls=%async_computation.7 | async-start | bytes 262144 | tf_op jit(solution)/shard_map/all_to_all | solution.py:296
  169.5 0.2 copy.37
  169.6 0.2 reshape.72
  169.9 0.3 convolution_add_fusion
  170.2 13.8 %all-to-all-done.7 = bf16[32,8,240]{2,1,0:T(8,128)(2,1)S(1)} async-done(((bf16[32,8,240]{2,1,0:T(8,128)(2,1)}), bf16[32,8,240]{2,1,0:T(8,128)(2,1)S(1)}, u32[]{:S(2)}, u32[]{:S(2)}) %all-to-all-start.7) | async-done | bytes 122912 | tf_op jit(solution)/shard_map/all_to_all | solution.py:296
  184.6 2.9 %far_levels.1 = (f32[8,768]{1,0:T(8,128)S(1)}, f32[3,8,384]{2,1,0:T(8,128)S(1)}) custom-call(bf16[8,1536]{1,0:T(8,128)(2,1)S(1)} %reshape.80.front5_ref, bf16[8,768]{1,0:T(8,128)(2,1)S(1)} %reshape.81.z4_ref, bf16[3,8,384]{2,1,0:T(8,128)(2,1)S(1)} %reshape.83.z_ref, bf16[768,1536]{1,0:T(8,128)(2,1)} %all-gather.7.cloned.1.call-done.ring_hbm, ...), custom_call_target="tpu_custom_call" | custom-call | tf_op jit(solution)/shard_map/far_levels/pallas_call | solution.py:278
  187.7 0.6 broadcast_in_dim.20
  188.3 12.4 %all-to-all-start.8 = ((bf16[8,8,96]{2,1,0:T(8,128)(2,1)}), bf16[8,8,96]{2,1,0:T(8,128)(2,1)S(1)}, u32[]{:S(2)}, u32[]{:S(2)}) async-start(bf16[8,8,96]{2,1,0:T(8,128)(2,1)} %broadcast_in_dim.20), calls=%async_computation.8 | async-start | bytes 32768 | tf_op jit(solution)/shard_map/all_to_all | solution.py:296
  200.9 0.7 concatenate.36
  201.6 3.8 %all-to-all-done.8 = bf16[8,8,96]{2,1,0:T(8,128)(2,1)S(1)} async-done(((bf16[8,8,96]{2,1,0:T(8,128)(2,1)}), bf16[8,8,96]{2,1,0:T(8,128)(2,1)S(1)}, u32[]{:S(2)}, u32[]{:S(2)}) %all-to-all-start.8) | async-done | bytes 12320 | tf_op jit(solution)/shard_map/all_to_all | solution.py:296
  205.4 0.8 convolution_subtract_fusion
  (65 shorter events, 2.8 us)
Async XLA Ops:
  7.2 162.7 %copy-start = (bf16[192,1536]{1,0:T(8,128)(2,1)S(1)}, bf16[192,1536]{1,0:T(8,128)(2,1)}, u32[]{:S(2)}) copy-start(bf16[192,1536]{1,0:T(8,128)(2,1)} %param.16) | copy-start | bytes 1769476
  7.2 33.1 %copy-start.5 = (f32[64,192]{1,0:T(8,128)S(1)}, f32[64,192]{1,0:T(8,128)}, u32[]{:S(2)}) copy-start(f32[64,192]{1,0:T(8,128)} %param.15) | copy-start | bytes 147460
  7.2 33.1 %copy-start.4 = (bf16[192,96]{1,0:T(8,128)(2,1)S(1)}, bf16[192,96]{1,0:T(8,128)(2,1)}, u32[]{:S(2)}) copy-start(bf16[192,96]{1,0:T(8,128)(2,1)} %param.17) | copy-start | bytes 110596
  7.2 62.0 %all-gather.5.cloned.1.call-start = ((), (), s32[]{:S(2)}) async-start(), calls=%async_computation.9 | async-start | bytes 1216512 | tf_op jit(solution)/shard_map/all_gather | solution.py:339
  8.9 156.0 %all-gather.7.cloned.1.call-start = ((), (), s32[]{:S(2)}) async-start(), calls=%async_computation.10 | async-start | bytes 2506752 | tf_op jit(solution)/shard_map/all_gather | solution.py:377
  9.8 7.6 %collective-permute-start = (f32[64,48]{1,0:T(8,128)S(1)}, f32[64,48]{1,0:T(8,128)S(1)}, u32[]{:S(2)}, u32[]{:S(2)}) collective-permute-start(f32[64,48]{1,0:T(8,128)S(1)} %copy.34), channel_id=1, source_target_pairs={{0,8},{8,0},{16,24},{24,16},{32,40},{40,32},{48,56},{56,48},{64,72... | collective-permute-start | bytes 36872 | tf_op jit(solution)/shard_map/ppermute | solution.py:324
  26.1 53.8 %copy-start.2 = (bf16[48,5952]{1,0:T(8,128)(2,1)S(1)}, bf16[48,5952]{1,0:T(8,128)(2,1)}, u32[]{:S(2)}) copy-start(bf16[48,5952]{1,0:T(8,128)(2,1)} %param.19) | copy-start | bytes 1714180
  40.2 49.8 %copy-start.3 = (bf16[48,6048]{1,0:T(8,128)(2,1)S(1)}, bf16[48,6048]{1,0:T(8,128)(2,1)}, u32[]{:S(2)}) copy-start(bf16[48,6048]{1,0:T(8,128)(2,1)} %param.18) | copy-start | bytes 1741828
  71.6 8.3 %collective-permute-start.1 = (bf16[8,768]{1,0:T(8,128)(2,1)S(1)}, bf16[8,768]{1,0:T(8,128)(2,1)S(1)}, u32[]{:S(2)}, u32[]{:S(2)}) collective-permute-start(bf16[8,768]{1,0:T(8,128)(2,1)S(1)} %get-tuple-element.20), channel_id=1, source_target_pairs={{0,96},{8,104},{16,112},{24,120},{32,64},{40,72},{48,80},{56,88},{... | collective-permute-start | bytes 36872 | tf_op jit(solution)/shard_map/ppermute | solution.py:389
  81.1 21.7 %all-to-all-start.3 = ((bf16[32,2,192]{2,1,0:T(2,128)(2,1)}), bf16[32,2,192]{2,1,0:T(2,128)(2,1)S(1)}, u32[]{:S(2)}, u32[]{:S(2)}) async-start(bf16[32,2,192]{2,1,0:T(2,128)(2,1)} %reshape.89), calls=%async_computation.3 | async-start | bytes 65536 | tf_op jit(solution)/shard_map/all_to_all | solution.py:296
  104.3 19.5 %all-to-all-start.4 = ((bf16[64,8,96]{2,1,0:T(8,128)(2,1)}), bf16[64,8,96]{2,1,0:T(8,128)(2,1)S(1)}, u32[]{:S(2)}, u32[]{:S(2)}) async-start(bf16[64,8,96]{2,1,0:T(8,128)(2,1)} %copy.39), calls=%async_computation.4 | async-start | bytes 262144 | tf_op jit(solution)/shard_map/all_to_all | solution.py:296
  124.7 19.8 %all-to-all-start.5 = ((bf16[64,2,192]{2,1,0:T(2,128)(2,1)}), bf16[64,2,192]{2,1,0:T(2,128)(2,1)S(1)}, u32[]{:S(2)}, u32[]{:S(2)}) async-start(bf16[64,2,192]{2,1,0:T(2,128)(2,1)} %reshape.91), calls=%async_computation.5 | async-start | bytes 131072 | tf_op jit(solution)/shard_map/all_to_all | solution.py:296
  145.9 18.3 %all-to-all-start.6 = ((bf16[64,2,192]{2,1,0:T(2,128)(2,1)}), bf16[64,2,192]{2,1,0:T(2,128)(2,1)S(1)}, u32[]{:S(2)}, u32[]{:S(2)}) async-start(bf16[64,2,192]{2,1,0:T(2,128)(2,1)} %reshape.93), calls=%async_computation.6 | async-start | bytes 131072 | tf_op jit(solution)/shard_map/all_to_all | solution.py:296
  150.9 33.7 %copy-start.1 = (bf16[384,1408]{1,0:T(8,128)(2,1)S(1)}, bf16[384,1408]{1,0:T(8,128)(2,1)}, u32[]{:S(2)}) copy-start(bf16[384,1408]{1,0:T(8,128)(2,1)} %all-gather.5.cloned.1.call-done.band_hbm.near_ref) | copy-start | bytes 3244036
  165.6 18.4 %all-to-all-start.7 = ((bf16[32,8,240]{2,1,0:T(8,128)(2,1)}), bf16[32,8,240]{2,1,0:T(8,128)(2,1)S(1)}, u32[]{:S(2)}, u32[]{:S(2)}) async-start(bf16[32,8,240]{2,1,0:T(8,128)(2,1)} %broadcast_in_dim.19), calls=%async_computation.7 | async-start | bytes 262144 | tf_op jit(solution)/shard_map/all_to_all | solution.py:296
  188.3 17.1 %all-to-all-start.8 = ((bf16[8,8,96]{2,1,0:T(8,128)(2,1)}), bf16[8,8,96]{2,1,0:T(8,128)(2,1)S(1)}, u32[]{:S(2)}, u32[]{:S(2)}) async-start(bf16[8,8,96]{2,1,0:T(8,128)(2,1)} %broadcast_in_dim.20), calls=%async_computation.8 | async-start | bytes 32768 | tf_op jit(solution)/shard_map/all_to_all | solution.py:296
Sparse Core Ops, SparseCore 0:
  10.1 50.7 all-gather.4
  71.6 64.3 all-gather.6
